TPU v7x, 32 devices: a whole 2x2x4 slice. The times are simulated.
32 devices in a mesh: dp: 8 (over z, core), mp: 4 (over y, x).
Axes of the slice: x: 2, y: 2, z: 4, core: 2. Of those that a mesh axis runs over, the one named last changes fastest.
Arguments:
- tokens: bfloat16 [12288, 2048], P(('dp', 'mp')), may hold values from -6 to 6
- segment_ids: int32 [16, 768], P('dp'), may hold values from 0 to 5, never falling along the last dimension, each value on 1 to 256 neighbouring positions
- query_weight: bfloat16 [2048, 2048], P(None, 'mp'), may hold values from -0.125 to 0.125
- key_weight: bfloat16 [2048, 2048], P(None, 'mp'), may hold values from -0.125 to 0.125
- value_weight: bfloat16 [2048, 2048], P(None, 'mp'), may hold values from -0.125 to 0.125
- out_weight: bfloat16 [2048, 2048], P('mp'), may hold values from -0.75 to 0.75
- up_weight: bfloat16 [2048, 8192], P(None, 'mp'), may hold values from -0.125 to 0.125
- down_weight: bfloat16 [8192, 2048], P('mp'), may hold values from -0.0625 to 0.0625
- attn_gain: float32 [2048], replicated, may hold values from 0.5 to 1.5
- mlp_gain: float32 [2048], replicated, may hold values from 0.5 to 1.5
- out_cotangent: bfloat16 [12288, 2048], P(('dp', 'mp')), may hold values from -18 to 18
Outputs:
- layer_output: bfloat16 [12288, 2048], P(('dp', 'mp'))
- tokens_grad: float32 [12288, 2048], P(('dp', 'mp'))
- query_weight_grad: float32 [2048, 2048], P('dp', 'mp')
- key_weight_grad: float32 [2048, 2048], P('dp', 'mp')
- value_weight_grad: float32 [2048, 2048], P('dp', 'mp')
- out_weight_grad: float32 [2048, 2048], P('mp', 'dp')
- up_weight_grad: float32 [2048, 8192], P('dp', 'mp')
- down_weight_grad: float32 [8192, 2048], P('mp', 'dp')
- attn_gain_grad: float32 [2048], replicated
- mlp_gain_grad: float32 [2048], replicated
Inputs may be any that keep to these rules, and one draw needn't show every extreme that they name: `segment_ids`: within each packed sequence the clip numbers never fall; each clip covers 1 to 256 tokens, and some clip covers exactly 256.
All inputs are finite; a program needn't handle non-finite values.
Results may differ from a plain program's by a relative error of at most 0.02.
Values may be sent and summed in bfloat16 or wider, within the bound.
A program may use at most 192 MiB of HBM per device.

v0:
```python
import math

import jax
import jax.numpy as jnp
from jax import lax
from jax.sharding import PartitionSpec as P

HEAD_DIM = 128


epsilon = 1e-05
masked_score = -1e30


def norm_rows(values, gain):
    centre = jnp.mean(values, axis=-1, keepdims=True)
    centred = values - centre
    spread = jnp.mean(centred * centred, axis=-1, keepdims=True)
    return centred * lax.rsqrt(spread + epsilon) * gain


def gelu_tanh(values):
    return jax.nn.gelu(values, approximate=True)


def block_allowed(segment):
    position = jnp.arange(segment.shape[0])
    return (position[None, :] <= position[:, None]) & (segment[:, None] == segment[None, :])


def rows_times(left_rows, right_matrix):
    return jnp.dot(left_rows, right_matrix, preferred_element_type=jnp.float32)


def rows_times_back(left_rows, right_matrix):
    return lax.dot_general(
        left_rows, right_matrix, (((1,), (1,)), ((), ())), preferred_element_type=jnp.float32
    )


def attn_input_back(
    queries_grad, keys_grad, values_grad, query_weight, key_weight, value_weight, score_scale
):
    total_grad = rows_times_back(queries_grad, query_weight) * score_scale
    total_grad = total_grad + rows_times_back(keys_grad, key_weight)
    return total_grad + rows_times_back(values_grad, value_weight)


def attend_forward(packed):
    queries, keys_in, values_in, segment = packed
    scores = jnp.einsum("qhd,khd->hqk", queries, keys_in, preferred_element_type=jnp.float32)
    scores = jnp.where(block_allowed(segment)[None], scores, masked_score)
    row_max = jnp.max(scores, axis=-1, keepdims=True)
    expanded = jnp.exp(scores - row_max)
    row_total = jnp.sum(expanded, axis=-1, keepdims=True)
    probs_low = (expanded / row_total).astype(jnp.bfloat16)
    context = jnp.einsum("hqk,khd->qhd", probs_low, values_in, preferred_element_type=jnp.float32)
    return (context.astype(jnp.bfloat16), (row_max + jnp.log(row_total))[:, :, 0])


def attend_backward(packed):
    queries, keys_in, values_in, segment, context_grad, log_total = packed
    scores = jnp.einsum("qhd,khd->hqk", queries, keys_in, preferred_element_type=jnp.float32)
    scores = jnp.where(block_allowed(segment)[None], scores, masked_score)
    attn_probs = jnp.exp(scores - log_total[:, :, None])
    probs_grad = jnp.einsum(
        "qhd,khd->hqk", context_grad, values_in, preferred_element_type=jnp.float32
    )
    values_grad = jnp.einsum(
        "hqk,qhd->khd",
        attn_probs.astype(jnp.bfloat16),
        context_grad,
        preferred_element_type=jnp.float32,
    )
    inner_sum = jnp.sum(attn_probs * probs_grad, axis=-1, keepdims=True)
    scores_grad = (attn_probs * (probs_grad - inner_sum)).astype(jnp.bfloat16)
    queries_grad = jnp.einsum(
        "hqk,khd->qhd", scores_grad, keys_in, preferred_element_type=jnp.float32
    )
    keys_grad = jnp.einsum("hqk,qhd->khd", scores_grad, queries, preferred_element_type=jnp.float32)
    return (
        queries_grad.astype(jnp.bfloat16),
        keys_grad.astype(jnp.bfloat16),
        values_grad.astype(jnp.bfloat16),
    )


def local(
    tokens,
    segment_ids,
    query_weight,
    key_weight,
    value_weight,
    out_weight,
    up_weight,
    down_weight,
    attn_gain,
    mlp_gain,
    out_cotangent,
):
    seq_count, seq_length = segment_ids.shape
    group_rows = seq_count * seq_length
    head_count = query_weight.shape[1] // HEAD_DIM
    score_scale = 1.0 / math.sqrt(HEAD_DIM)
    shaped = (seq_count, seq_length, head_count, HEAD_DIM)
    flat_shape = (group_rows, head_count * HEAD_DIM)
    residual_in = tokens.astype(jnp.float32)
    normed_attn, attn_norm_back = jax.vjp(norm_rows, residual_in, attn_gain)
    gathered_attn = lax.all_gather(normed_attn.astype(jnp.bfloat16), "mp", axis=0, tiled=True)
    queries = (
        jnp.dot(gathered_attn, query_weight, preferred_element_type=jnp.float32) * score_scale
    ).astype(jnp.bfloat16)
    keys_all = jnp.dot(gathered_attn, key_weight, preferred_element_type=jnp.float32).astype(
        jnp.bfloat16
    )
    values_all = jnp.dot(gathered_attn, value_weight, preferred_element_type=jnp.float32).astype(
        jnp.bfloat16
    )
    queries_seq = queries.reshape(shaped)
    keys_seq = keys_all.reshape(shaped)
    values_seq = values_all.reshape(shaped)
    context, log_total = lax.map(attend_forward, (queries_seq, keys_seq, values_seq, segment_ids))
    context_flat = context.reshape(flat_shape)
    attn_rows = lax.psum_scatter(
        rows_times(context_flat, out_weight).astype(jnp.bfloat16),
        "mp",
        scatter_dimension=0,
        tiled=True,
    ).astype(jnp.float32)
    residual_mid = residual_in + attn_rows
    normed_mlp, mlp_norm_back = jax.vjp(norm_rows, residual_mid, mlp_gain)
    gathered_mlp = lax.all_gather(normed_mlp.astype(jnp.bfloat16), "mp", axis=0, tiled=True)
    pre_act = jnp.dot(gathered_mlp, up_weight, preferred_element_type=jnp.float32)
    activated, gelu_back = jax.vjp(gelu_tanh, pre_act)
    hidden = activated.astype(jnp.bfloat16)
    mlp_rows = lax.psum_scatter(
        rows_times(hidden, down_weight).astype(jnp.bfloat16), "mp", scatter_dimension=0, tiled=True
    ).astype(jnp.float32)
    layer_output = (residual_mid + mlp_rows).astype(jnp.bfloat16)
    cotangent_all = lax.all_gather(out_cotangent, "mp", axis=0, tiled=True)
    down_weight_grad = jnp.einsum(
        "rf,rd->fd", hidden, cotangent_all, preferred_element_type=jnp.float32
    )
    hidden_grad = lax.dot_general(
        cotangent_all, down_weight, (((1,), (1,)), ((), ())), preferred_element_type=jnp.float32
    )
    pre_grad = gelu_back(hidden_grad)[0].astype(jnp.bfloat16)
    up_weight_grad = jnp.einsum(
        "rd,rf->df", gathered_mlp, pre_grad, preferred_element_type=jnp.float32
    )
    normed_mlp_grad = lax.psum_scatter(
        rows_times_back(pre_grad, up_weight).astype(jnp.bfloat16),
        "mp",
        scatter_dimension=0,
        tiled=True,
    ).astype(jnp.float32)
    middle_back, mlp_gain_grad = mlp_norm_back(normed_mlp_grad)
    middle_grad = out_cotangent.astype(jnp.float32) + middle_back
    middle_all_grad = lax.all_gather(middle_grad.astype(jnp.bfloat16), "mp", axis=0, tiled=True)
    out_weight_grad = jnp.einsum(
        "rc,rd->cd", context_flat, middle_all_grad, preferred_element_type=jnp.float32
    )
    context_grad = lax.dot_general(
        middle_all_grad, out_weight, (((1,), (1,)), ((), ())), preferred_element_type=jnp.float32
    ).astype(jnp.bfloat16)
    queries_grad, keys_grad, values_grad = lax.map(
        attend_backward,
        (queries_seq, keys_seq, values_seq, segment_ids, context_grad.reshape(shaped), log_total),
    )
    queries_grad = queries_grad.reshape(flat_shape)
    keys_grad = keys_grad.reshape(flat_shape)
    values_grad = values_grad.reshape(flat_shape)
    query_weight_grad = (
        jnp.einsum("rd,rc->dc", gathered_attn, queries_grad, preferred_element_type=jnp.float32)
        * score_scale
    )
    key_weight_grad = jnp.einsum(
        "rd,rc->dc", gathered_attn, keys_grad, preferred_element_type=jnp.float32
    )
    value_weight_grad = jnp.einsum(
        "rd,rc->dc", gathered_attn, values_grad, preferred_element_type=jnp.float32
    )
    normed_attn_grad = lax.psum_scatter(
        attn_input_back(
            queries_grad,
            keys_grad,
            values_grad,
            query_weight,
            key_weight,
            value_weight,
            score_scale,
        ).astype(jnp.bfloat16),
        "mp",
        scatter_dimension=0,
        tiled=True,
    ).astype(jnp.float32)
    token_back, attn_gain_grad = attn_norm_back(normed_attn_grad)
    tokens_grad = middle_grad + token_back
    attn_gain_grad, mlp_gain_grad = lax.psum((attn_gain_grad, mlp_gain_grad), ("dp", "mp"))
    (
        query_weight_grad,
        key_weight_grad,
        value_weight_grad,
        out_weight_grad,
        up_weight_grad,
        down_weight_grad,
    ) = (
        lax.psum_scatter(
            query_weight_grad.astype(jnp.bfloat16), "dp", scatter_dimension=0, tiled=True
        ).astype(jnp.float32),
        lax.psum_scatter(
            key_weight_grad.astype(jnp.bfloat16), "dp", scatter_dimension=0, tiled=True
        ).astype(jnp.float32),
        lax.psum_scatter(
            value_weight_grad.astype(jnp.bfloat16), "dp", scatter_dimension=0, tiled=True
        ).astype(jnp.float32),
        lax.psum_scatter(
            out_weight_grad.astype(jnp.bfloat16), "dp", scatter_dimension=1, tiled=True
        ).astype(jnp.float32),
        lax.psum_scatter(
            up_weight_grad.astype(jnp.bfloat16), "dp", scatter_dimension=0, tiled=True
        ).astype(jnp.float32),
        lax.psum_scatter(
            down_weight_grad.astype(jnp.bfloat16), "dp", scatter_dimension=1, tiled=True
        ).astype(jnp.float32),
    )
    return (
        layer_output,
        tokens_grad,
        query_weight_grad,
        key_weight_grad,
        value_weight_grad,
        out_weight_grad,
        up_weight_grad,
        down_weight_grad,
        attn_gain_grad,
        mlp_gain_grad,
    )


def solution(mesh):
    return jax.shard_map(
        local,
        mesh=mesh,
        in_specs=(
            P(("dp", "mp"), None),
            P("dp", None),
            P(None, "mp"),
            P(None, "mp"),
            P(None, "mp"),
            P("mp", None),
            P(None, "mp"),
            P("mp", None),
            P(),
            P(),
            P(("dp", "mp"), None),
        ),
        out_specs=(
            P(("dp", "mp"), None),
            P(("dp", "mp"), None),
            P("dp", "mp"),
            P("dp", "mp"),
            P("dp", "mp"),
            P("mp", "dp"),
            P("dp", "mp"),
            P("mp", "dp"),
            P(),
            P(),
        ),
        check_vma=False,
    )
```

profile of v0, /device:TPU:0, one launch (start us, length us, event | category | flops | bytes accessed | tf_op | source)
XLA Modules:
  0.0 1105.6 jit_solution(7210589673843302547)
XLA Ops:
  14.0 73.0 %all-gather.5.cloned.1.call-done = bf16[1536,2048]{1,0:T(8,128)(2,1)} async-done(((bf16[384,2048]{1,0:T(8,128)(2,1)}), bf16[1536,2048]{1,0:T(8,128)(2,1)}) %all-gather.5.cloned.1.call-update) | async-done | bytes 6291472 | tf_op jit(solution)/shard_map/all_gather | solution.py:109
  87.0 8.0 convolution_convert_fusion.11
  94.9 3.7 reshape.216
  101.6 7.3 fusion.63
  115.3 7.3 convolution_convert_fusion.12
  127.6 28.2 %while.26 = (s32[]{:T(128)}, bf16[2,768,4,128]{3,2,1,0:T(4,128)(2,1)}, f32[2,4,768]{2,1,0:T(4,128)S(1)}, bf16[2,768,4,128]{3,2,1,0:T(4,128)(2,1)}, s32[2,768]{1,...) while((s32[]{:T(128)}, ...), condition=%wide.region_5.6_spmd, body=%wide.region_2.5_spmd.sunk | while | flops 1231352832 | bytes 43362440 | solution.py:122
  135.4 3.6 fusion.137
  149.5 3.6 fusion.137
  155.8 7.2 convolution_convert_fusion.6
  163.8 69.6 %reduce-scatter.11.cloned.1.call-done = bf16[384,2048]{1,0:T(8,128)(2,1)} async-done(((bf16[1536,2048]{1,0:T(8,128)(2,1)}), bf16[384,2048]{1,0:T(8,128)(2,1)}) %reduce-scatter.11.cloned.1.call-update) | async-done | bytes 1572880 | tf_op jit(solution)/shard_map/reduce_scatter | solution.py:124
  238.9 66.6 %all-gather.9.cloned.1.call-done = bf16[1536,2048]{1,0:T(8,128)(2,1)} async-done(((bf16[384,2048]{1,0:T(8,128)(2,1)}), bf16[1536,2048]{1,0:T(8,128)(2,1)}) %all-gather.9.cloned.1.call-update) | async-done | bytes 6291472 | tf_op jit(solution)/shard_map/all_gather | solution.py:140
  305.5 19.1 %fusion.89 = f32[1536,2048]{1,0:T(8,128)} fusion(bf16[1536,2048]{1,0:T(8,128)(2,1)} %all-gather.9.cloned.1.call-done, bf16[2048,2048]{1,0:T(8,128)(2,1)} %param.22), kind=kOutput, calls=%fused_computation.146 | convolution fusion | flops 12884901888 | bytes 27262976 | tf_op jit(solution)/shard_map/dot_general | solution.py:144
  324.5 53.4 %all-gather.7.cloned.1.call-done = bf16[1536,2048]{1,0:T(8,128)(2,1)} async-done(((bf16[384,2048]{1,0:T(8,128)(2,1)}), bf16[1536,2048]{1,0:T(8,128)(2,1)}) %all-gather.7.cloned.1.call-update) | async-done | bytes 6291472 | tf_op jit(solution)/shard_map/all_gather | solution.py:132
  377.9 29.6 %fusion.48 = (bf16[1536,2048]{1,0:T(8,128)(2,1)}, f32[1536,2048]{1,0:T(8,128)}) fusion(f32[1536,2048]{1,0:T(8,128)} %fusion.89, bf16[1536,2048]{1,0:T(8,128)(2,1)} %all-gather.7.cloned.1.call-done, bf16[2048,2048]{1,0:T(8,128)(2,1)} %param.21), kind=kOutput, calls=%fused_computation.68 | convolution fusion | flops 12947816448 | bytes 46137344 | tf_op jit(solution)/shard_map/dot_general | solution.py:133
  407.5 19.1 %convolution_convert_fusion.4 = bf16[1536,2048]{1,0:T(8,128)(2,1)} fusion(bf16[1536,2048]{1,0:T(8,128)(2,1)} %get-tuple-element.190, bf16[2048,2048]{1,0:T(8,128)(2,1)} %param.21), kind=kOutput, calls=%fused_computation.73 | convolution fusion | flops 12888047616 | bytes 20971520 | tf_op jit(solution)/shard_map/dot_general | solution.py:36
  426.7 20.5 %convolution_convert_fusion.5 = bf16[1536,2048]{1,0:T(8,128)(2,1)} fusion(bf16[2048,2048]{1,0:T(8,128)(2,1)} %param.22, f32[1536,2048]{1,0:T(8,128)} %get-tuple-element.191), kind=kOutput, calls=%fused_computation.74 | convolution fusion | flops 12916359168 | bytes 27262976 | tf_op jit(solution)/shard_map/dot_general | solution.py:32
  447.3 49.7 %reduce-scatter.15.cloned.1.call-done = bf16[384,2048]{1,0:T(8,128)(2,1)} async-done(((bf16[1536,2048]{1,0:T(8,128)(2,1)}), bf16[384,2048]{1,0:T(8,128)(2,1)}) %reduce-scatter.15.cloned.1.call-update) | async-done | bytes 1572880 | tf_op jit(solution)/shard_map/reduce_scatter | solution.py:151
  497.0 4.4 fusion.59
  501.4 68.7 %reduce-scatter.13.cloned.1.call-done = bf16[384,2048]{1,0:T(8,128)(2,1)} async-done(((bf16[1536,2048]{1,0:T(8,128)(2,1)}), bf16[384,2048]{1,0:T(8,128)(2,1)}) %reduce-scatter.13.cloned.1.call-update) | async-done | bytes 1572880 | tf_op jit(solution)/shard_map/reduce_scatter | solution.py:136
  570.1 5.5 fusion.88
  578.9 19.6 %convolution_convert_fusion.3 = bf16[2048,2048]{1,0:T(8,128)(2,1)} fusion(bf16[1536,2048]{1,0:T(8,128)(2,1)} %all-gather.7.cloned.1.call-done, bf16[1536,2048]{1,0:T(8,128)(2,1)} %get-tuple-element.190), kind=kOutput, calls=%fused_computation.72 | convolution fusion | flops 12889096192 | bytes 20971520 | tf_op jit(solution)/shard_map/rd,rf->df/dot_general | solution.py:148
  598.5 22.5 %convolution_convert_fusion.2 = bf16[2048,2048]{1,0:T(8,128)(2,1)} fusion(bf16[1536,2048]{1,0:T(8,128)(2,1)} %all-gather.9.cloned.1.call-done, f32[1536,2048]{1,0:T(8,128)} %get-tuple-element.191), kind=kOutput, calls=%fused_computation.71 | convolution fusion | flops 12917407744 | bytes 27262976 | tf_op jit(solution)/shard_map/rf,rd->fd/dot_general | solution.py:141
  621.1 28.0 %all-gather.11.cloned.1.call-done = bf16[1536,2048]{1,0:T(8,128)(2,1)} async-done(((bf16[384,2048]{1,0:T(8,128)(2,1)}), bf16[1536,2048]{1,0:T(8,128)(2,1)}) %all-gather.11.cloned.1.call-update) | async-done | bytes 6291472 | tf_op jit(solution)/shard_map/all_gather | solution.py:159
  649.1 7.8 convolution_convert_fusion.10
  657.0 3.7 reshape.218
  660.6 8.1 convolution_convert_fusion.7
  673.6 99.9 %while.27 = (s32[]{:T(128)}, bf16[2,768,4,128]{3,2,1,0:T(4,128)(2,1)}, bf16[2,768,4,128]{3,2,1,0:T(4,128)(2,1)}, bf16[2,768,4,128]{3,2,1,0:T(4,128)(2,1)}, bf16[...) while((s32[]{:T(128)}, ...), condition=%wide.region_15.16_spmd, body=%wide.region_13.15_spmd.sunk | while | flops 3051156480 | bytes 169179440 | solution.py:166
  679.6 3.6 copy-done.1
  689.0 8.2 multiply_reduce_fusion.3
  697.2 10.9 multiply_convert_fusion.7
  708.1 4.5 fusion.149
  729.1 3.6 copy-done.1
  738.5 8.1 multiply_reduce_fusion.3
  746.6 11.5 %multiply_convert_fusion.7 = bf16[4,768,768]{1,2,0:T(8,128)(2,1)} fusion(f32[4,768,768]{1,2,0:T(8,128)} %get-tuple-element.304, f32[4,768,768]{1,2,0:T(8,128)} %copy-done.1, f32[4,768]{1,0:T(4,128)S(1)} %get-tuple-element.305, f32[4,768]{1,0:T(4,128)S(1)} %dynamic-slice_bitcast_fusion.2, pred[768,768]{0,1:T(8,128)(4,1)S(1)} %fusion.146), kind=kLoop, calls=%fused_computation.21.clone.1 | loop fusion | flops 11796480 | bytes 24207360 | tf_op jit(solution)/shard_map/while/body/eval_jaxpr/convert_element_type | solution.py:76
  758.1 4.4 fusion.149
  773.5 8.1 multiply_convert_fusion.2
  781.7 8.1 convolution_convert_fusion.8
  789.8 8.1 convolution_convert_fusion.9
  798.3 10.2 fusion.72
  808.5 6.5 fusion.69
  815.0 15.8 %add_convert_fusion = bf16[1536,2048]{1,0:T(8,128)(2,1)} fusion(f32[1536,2048]{1,0:T(8,128)} %fusion.69, f32[1536,2048]{1,0:T(8,128)} %fusion.72, bf16[2048,512]{1,0:T(8,128)(2,1)} %param.17, bf16[192,8,4,128]{3,2,1,0:T(4,128)(2,1)} %bitcast.147), kind=kOutput, calls=%fused_computation.69 | convolution fusion | flops 3233808384 | bytes 35127296 | tf_op jit(solution)/shard_map/dot_general | solution.py:36
  836.4 31.3 %reduce-scatter.25.cloned.1.call-done = bf16[512,256]{1,0:T(8,128)(2,1)} async-done(((bf16[512,2048]{1,0:T(8,128)(2,1)}), bf16[512,256]{1,0:T(8,128)(2,1)}) %reduce-scatter.25.cloned.1.call-update) | async-done | bytes 262160 | tf_op jit(solution)/shard_map/reduce_scatter | solution.py:217
  869.4 34.9 %reduce-scatter.19.cloned.1.call-done = bf16[256,512]{1,0:T(8,128)(2,1)} async-done(((bf16[2048,512]{1,0:T(8,128)(2,1)}), bf16[256,512]{1,0:T(8,128)(2,1)}) %reduce-scatter.19.cloned.1.call-update) | async-done | bytes 262160 | tf_op jit(solution)/shard_map/reduce_scatter | solution.py:208
  906.1 34.9 %reduce-scatter.23.cloned.1.call-done = bf16[256,512]{1,0:T(8,128)(2,1)} async-done(((bf16[2048,512]{1,0:T(8,128)(2,1)}), bf16[256,512]{1,0:T(8,128)(2,1)}) %reduce-scatter.23.cloned.1.call-update) | async-done | bytes 262160 | tf_op jit(solution)/shard_map/reduce_scatter | solution.py:214
  942.9 34.9 %reduce-scatter.21.cloned.1.call-done = bf16[256,512]{1,0:T(8,128)(2,1)} async-done(((bf16[2048,512]{1,0:T(8,128)(2,1)}), bf16[256,512]{1,0:T(8,128)(2,1)}) %reduce-scatter.21.cloned.1.call-update) | async-done | bytes 262160 | tf_op jit(solution)/shard_map/reduce_scatter | solution.py:211
  979.6 70.0 %reduce-scatter.17.cloned.1.call-done = bf16[384,2048]{1,0:T(8,128)(2,1)} async-done(((bf16[1536,2048]{1,0:T(8,128)(2,1)}), bf16[384,2048]{1,0:T(8,128)(2,1)}) %reduce-scatter.17.cloned.1.call-update) | async-done | bytes 1572880 | tf_op jit(solution)/shard_map/reduce_scatter | solution.py:183
  1054.0 39.5 %all-reduce = (f32[2048]{0:T(1024)}, f32[2048]{0:T(1024)}) all-reduce(f32[2048]{0:T(1024)S(1)} %get-tuple-element.143, f32[2048]{0:T(1024)S(1)} %copy-done.27), channel_id=1, replica_groups=mesh['dp'=8,'mp'=4] {'dp','mp'}, use_global_device_ids=true, to_apply=%region_26.27 | all-reduce | flops 4096 | bytes 32768 | tf_op jit(solution)/shard_map/psum | solution.py:199
  1093.5 5.1 add_add_fusion.2
  (184 shorter events, 118.7 us)
Async XLA Ops:
  7.2 148.6 %copy-start = (bf16[512,2048]{1,0:T(8,128)(2,1)S(1)}, bf16[512,2048]{1,0:T(8,128)(2,1)}, u32[]{:S(2)}) copy-start(bf16[512,2048]{1,0:T(8,128)(2,1)} %param.20) | copy-start | bytes 6291460
  7.2 5.0 copy-start.20
  7.2 79.8 %all-gather.5.cloned.1.call-start = ((), (), s32[]{:S(2)}) async-start(), calls=%async_computation.10 | async-start | bytes 7864320 | tf_op jit(solution)/shard_map/all_gather | solution.py:109
  7.2 5.0 copy-start.3
  9.1 2.5 copy-start.22
  13.9 219.5 %reduce-scatter.11.cloned.1.call-start = ((), (), s32[]{:S(2)}) async-start(), calls=%async_computation.11 | async-start | bytes 7864320 | tf_op jit(solution)/shard_map/reduce_scatter | solution.py:124
  98.6 2.9 copy-start.14
  112.4 2.9 copy-start.32
  122.6 5.1 copy-start.18
  155.8 7.2 copy-start.16
  163.1 142.4 %all-gather.9.cloned.1.call-start = ((), (), s32[]{:S(2)}) async-start(), calls=%async_computation.14 | async-start | bytes 7864320 | tf_op jit(solution)/shard_map/all_gather | solution.py:140
  163.1 73.9 %copy-start.24 = (f32[2048]{0:T(1024)S(1)}, f32[2048]{0:T(1024)}, u32[]{:S(2)}) copy-start(f32[2048]{0:T(1024)} %param.24) | copy-start | bytes 24580
  163.8 214.1 %all-gather.7.cloned.1.call-start = ((), (), s32[]{:S(2)}) async-start(), calls=%async_computation.12 | async-start | bytes 7864320 | tf_op jit(solution)/shard_map/all_gather | solution.py:132
  233.4 2.5 copy-start.4
  233.4 2.8 copy-start.9
  238.8 258.2 %reduce-scatter.15.cloned.1.call-start = ((), (), s32[]{:S(2)}) async-start(), calls=%async_computation.15 | async-start | bytes 7864320 | tf_op jit(solution)/shard_map/reduce_scatter | solution.py:151
  426.7 143.4 %reduce-scatter.13.cloned.1.call-start = ((), (), s32[]{:S(2)}) async-start(), calls=%async_computation.13 | async-start | bytes 7864320 | tf_op jit(solution)/shard_map/reduce_scatter | solution.py:136
  447.2 201.9 %all-gather.11.cloned.1.call-start = ((), (), s32[]{:S(2)}) async-start(), calls=%async_computation.16 | async-start | bytes 7864320 | tf_op jit(solution)/shard_map/all_gather | solution.py:159
  570.1 7.2 copy-start.13
  578.8 252.0 %reduce-scatter.27.cloned.1.call-start = ((), (), s32[]{:S(2)}) async-start(), calls=%async_computation.22 | async-start | bytes 9437184 | tf_op jit(solution)/shard_map/reduce_scatter | solution.py:220
  598.5 235.2 %reduce-scatter.29.cloned.1.call-start = ((), (), s32[]{:S(2)}) async-start(), calls=%async_computation.23 | async-start | bytes 9437184 | tf_op jit(solution)/shard_map/reduce_scatter | solution.py:223
  621.0 246.6 %reduce-scatter.25.cloned.1.call-start = ((), (), s32[]{:S(2)}) async-start(), calls=%async_computation.21 | async-start | bytes 2359296 | tf_op jit(solution)/shard_map/reduce_scatter | solution.py:217
  668.8 4.8 copy-start.17
  668.8 4.8 copy-start.19
  668.8 235.5 %reduce-scatter.19.cloned.1.call-start = ((), (), s32[]{:S(2)}) async-start(), calls=%async_computation.18 | async-start | bytes 2359296 | tf_op jit(solution)/shard_map/reduce_scatter | solution.py:208
  673.8 4.4 copy-start.6
  673.8 4.4 copy-start.8
  679.6 3.6 copy-start.1
  708.1 4.5 copy-start.2
  708.1 4.6 copy-start.7
  723.3 4.5 copy-start.6
  723.3 4.5 copy-start.8
  729.1 3.6 copy-start.1
  758.1 4.4 copy-start.2
  758.1 4.6 copy-start.7
  781.6 159.5 %reduce-scatter.23.cloned.1.call-start = ((), (), s32[]{:S(2)}) async-start(), calls=%async_computation.20 | async-start | bytes 2359296 | tf_op jit(solution)/shard_map/reduce_scatter | solution.py:214
  789.8 188.0 %reduce-scatter.21.cloned.1.call-start = ((), (), s32[]{:S(2)}) async-start(), calls=%async_computation.19 | async-start | bytes 2359296 | tf_op jit(solution)/shard_map/reduce_scatter | solution.py:211
  798.0 251.6 %reduce-scatter.17.cloned.1.call-start = ((), (), s32[]{:S(2)}) async-start(), calls=%async_computation.17 | async-start | bytes 7864320 | tf_op jit(solution)/shard_map/reduce_scatter | solution.py:183
  798.3 10.2 copy-start.15
  798.3 10.2 copy-start.33
  833.6 215.9 %copy-start.21 = (f32[2048]{0:T(1024)S(1)}, f32[2048]{0:T(1024)}, u32[]{:S(2)}) copy-start(f32[2048]{0:T(1024)} %param.23) | copy-start | bytes 24580
  833.6 215.9 %copy-start.23 = (f32[384]{0:T(512)S(1)}, f32[384]{0:T(512)}, u32[]{:S(2)}) copy-start(f32[384]{0:T(512)} %copy-done.22) | copy-start | bytes 4612
  836.4 216.0 %copy-start.31 = (f32[384]{0:T(512)S(1)}, f32[384]{0:T(512)}, u32[]{:S(2)}) copy-start(f32[384]{0:T(512)} %copy-done.30) | copy-start | bytes 4612
  836.4 216.0 %copy-start.26 = (f32[384]{0:T(512)S(1)}, f32[384]{0:T(512)}, u32[]{:S(2)}) copy-start(f32[384]{0:T(512)} %copy-done.25) | copy-start | bytes 4612
  979.6 74.4 %copy-start.27 = (f32[2048]{0:T(1024)S(1)}, f32[2048]{0:T(1024)}, u32[]{:S(2)}) copy-start(f32[2048]{0:T(1024)} %get-tuple-element.141) | copy-start | bytes 24580
  979.6 113.9 %copy-start.29 = (f32[384]{0:T(512)S(1)}, f32[384]{0:T(512)}, u32[]{:S(2)}) copy-start(f32[384]{0:T(512)} %copy-done.28) | copy-start | bytes 4612
  1049.6 2.8 copy-start.5
  1049.6 2.8 copy-start.12
  (6 other events, 8.0 us)
Sparse Core Ops, SparseCore 0:
  14.1 72.8 all-gather.4
  163.2 70.2 reduce-scatter.10
  235.3 70.1 all-gather.8
  307.7 70.1 all-gather.6
  426.8 70.1 reduce-scatter.14
  499.8 70.1 reduce-scatter.12
  579.0 70.1 all-gather.10
  651.4 89.5 reduce-scatter.26
  743.4 87.9 reduce-scatter.28
  833.5 34.0 reduce-scatter.24
  870.0 34.3 reduce-scatter.18
  906.5 34.5 reduce-scatter.22
  943.4 34.3 reduce-scatter.20
  980.6 68.8 reduce-scatter.16
where the time goes:
time: 1110 us
  waiting for transfers between devices  616 us (55%)
  matrix products  285 us (26%)
  local copies, waits for them, and re-layouts  78.1 us (7%)
  other arithmetic  71.6 us (6%)
  blocking collectives  39.5 us (4%)
  between operations  14.6 us (1%)
    all_gather x1, waiting for transfers between devices, local(): lax.all_gather(normed_attn.astype(jnp.bfloat16), 'mp', axis=0, tiled=True)  73 us
    reduce_scatter x1, waiting for transfers between devices, local(): lax.psum_scatter(attn_input_back(queries_grad, keys_grad, values_grad, qu...  70 us
    reduce_scatter x1, waiting for transfers between devices, local(): lax.psum_scatter(rows_times(context_flat, out_weight).astype(jnp.bfloat16...  69.6 us
    reduce_scatter x1, waiting for transfers between devices, local(): lax.psum_scatter(rows_times(hidden, down_weight).astype(jnp.bfloat16), 'm...  68.7 us
    all_gather x1, waiting for transfers between devices, local(): cotangent_all = lax.all_gather(out_cotangent, 'mp', axis=0, tiled=True)  66.6 us
    all_gather x1, waiting for transfers between devices, local(): lax.all_gather(normed_mlp.astype(jnp.bfloat16), 'mp', axis=0, tiled=True)  53.4 us
    dot_general x4, matrix products, rows_times_back(): lax.dot_general(left_rows, right_matrix, (((1,), (1,)), ((), ())), prefer...  51.6 us
    reduce_scatter x1, waiting for transfers between devices, local(): lax.psum_scatter(rows_times_back(pre_grad, up_weight).astype(jnp.bfloat16...  49.7 us
  transfers between devices with their start and end apart: 14, of which 12 were waited for; matrix products, arithmetic and copies ran while one was open for 25% of the time, Pallas kernels for 0%

commit v1 on v0

v1 whole, which is shorter than its diff:
```python
import functools
import math

import jax
import jax.numpy as jnp
from jax import lax
from jax.experimental import pallas as pl
from jax.experimental.pallas import tpu as pltpu
from jax.sharding import PartitionSpec as P

HEAD_DIM = 128
CLIP_MOST = 256
epsilon = 1e-05
masked_score = -1e30
bf16, f32 = jnp.bfloat16, jnp.float32
VMEM_LIMIT = 60 * 1024 * 1024


def dot(a, b, ca, cb):
    return lax.dot_general(a, b, (((ca,), (cb,)), ((), ())), preferred_element_type=f32)


class Group:
    def __init__(self, count):
        self.count = count

    def swap(self, value, r):
        return lax.ppermute(value, "mp", [(m, m ^ r) for m in range(self.count)])

    def gather(self, low, high):
        if self.count == 4:
            low_x, high_y = self.swap(low, 1), self.swap(high, 2)
            high_x, low_y = self.swap(high, 1), self.swap(low, 2)
            low_d, high_d = self.swap(low_x, 2), self.swap(high_y, 1)
            return [(low, high), (low_x, high_x), (low_y, high_y), (low_d, high_d)]
        me = lax.axis_index("mp")
        blocks = lax.all_gather(jnp.concatenate([low, high]), "mp")
        half = low.shape[0]
        out = []
        for r in range(self.count):
            block = lax.dynamic_index_in_dim(blocks, me ^ r, 0, keepdims=False)
            out.append((block[:half], block[half:]))
        return out

    def reduce(self, parts):
        if self.count == 4:
            early_x, early_y = self.swap(parts[1][0], 1), self.swap(parts[2][1], 2)
            got_x, got_y = self.swap(parts[3][0], 1), self.swap(parts[3][1], 2)
            late_x = self.swap(add(parts[1][1], got_y), 1)
            late_y = self.swap(add(parts[2][0], got_x), 2)
            return (
                (parts[0][0], early_x, late_y),
                (parts[0][1], late_x, early_y),
            )
        me = lax.axis_index("mp")
        blocks = jnp.stack([jnp.concatenate(p) for p in parts])
        blocks = jnp.take(blocks, jnp.arange(self.count) ^ me, axis=0)
        own = lax.psum_scatter(blocks, "mp", scatter_dimension=0, tiled=False)
        half = own.shape[0] // 2
        return ((own[:half],), (own[half:],))


def add(a, b):
    return (a.astype(f32) + b.astype(f32)).astype(bf16)


def total(values):
    out = values[0].astype(f32)
    for v in values[1:]:
        out = out + v.astype(f32)
    return out


def norm_parts(values):
    centre = jnp.mean(values, axis=-1, keepdims=True)
    centred = values - centre
    spread = jnp.mean(centred * centred, axis=-1, keepdims=True)
    scale = lax.rsqrt(spread + epsilon)
    return centred * scale, scale


def norm_rows(values, gain):
    return norm_parts(values)[0] * gain


def norm_back(values, gain, grad):
    unit, scale = norm_parts(values)
    q = grad * gain
    back = scale * (
        q - jnp.mean(q, axis=-1, keepdims=True) - unit * jnp.mean(q * unit, axis=-1, keepdims=True)
    )
    return back, jnp.sum(grad * unit, axis=0)


def mm_kernel(trans, sizes, scaled, *refs):
    n = len(sizes)
    xs, w = refs[:n], refs[n]
    scale = refs[n + 1] if scaled else None
    outs = refs[n + 1 + scaled :]
    x = jnp.concatenate([r[...] for r in xs], axis=0) if n > 1 else xs[0][...]
    acc = dot(x, w[...], 1, 1 if trans else 0)
    if scaled:
        acc = acc * scale[...]
    at = 0
    for o in outs:
        o[...] = acc[at : at + o.shape[0]].astype(o.dtype)
        at += o.shape[0]


def mm(xs, w, *, trans=False, tile=512, scale=None, outs=None, name="mm"):
    depth = xs[0].shape[1]
    width = w.shape[0] if trans else w.shape[1]
    tile = min(tile, width)
    sizes = [x.shape[0] for x in xs]
    outs = outs or sizes
    scaled = scale is not None
    in_specs = [pl.BlockSpec((s, depth), lambda j: (0, 0)) for s in sizes]
    in_specs.append(
        pl.BlockSpec((tile, depth), lambda j: (j, 0))
        if trans
        else pl.BlockSpec((depth, tile), lambda j: (0, j))
    )
    args = [*xs, w]
    if scaled:
        in_specs.append(pl.BlockSpec((1, tile), lambda j: (0, j)))
        args.append(scale)
    rows = sum(sizes)
    return pl.pallas_call(
        functools.partial(mm_kernel, trans, sizes, scaled),
        grid=(width // tile,),
        in_specs=in_specs,
        out_specs=[pl.BlockSpec((s, tile), lambda j: (0, j)) for s in outs],
        out_shape=[jax.ShapeDtypeStruct((s, width), bf16) for s in outs],
        compiler_params=pltpu.CompilerParams(vmem_limit_bytes=VMEM_LIMIT),
        cost_estimate=pl.CostEstimate(
            flops=2 * rows * depth * width,
            bytes_accessed=2 * (rows * depth + depth * width + rows * width),
            transcendentals=0,
        ),
        name=name,
    )(*args)


def gelu_both(u):
    c = math.sqrt(2.0 / math.pi)
    square = u * u
    t = jnp.tanh(c * (u + 0.044715 * (u * square)))
    half = 0.5 * (1.0 + t)
    value = u * half
    slope = half + (0.5 * c) * u * (1.0 - t * t) * (1.0 + (3 * 0.044715) * square)
    return value, slope


def feed_kernel(tiles, x0, x1, c0, c1, up, down, hid, pre, y0, y1, g0, g1, acc_y, acc_g):
    j = pl.program_id(0)
    x = jnp.concatenate([x0[...], x1[...]], axis=0)
    c = jnp.concatenate([c0[...], c1[...]], axis=0)
    value, slope = gelu_both(dot(x, up[...], 1, 0))
    value = value.astype(bf16)
    hid[...] = value
    grad = (dot(c, down[...], 1, 1) * slope).astype(bf16)
    pre[...] = grad
    y = dot(value, down[...], 1, 0)
    g = dot(grad, up[...], 1, 1)

    @pl.when(j == 0)
    def _():
        acc_y[...] = y
        acc_g[...] = g

    @pl.when((j > 0) & (j < tiles - 1))
    def _():
        acc_y[...] += y
        acc_g[...] += g

    @pl.when(j == tiles - 1)
    def _():
        half = x0.shape[0]
        last_y, last_g = acc_y[...] + y, acc_g[...] + g
        y0[...] = last_y[:half].astype(bf16)
        y1[...] = last_y[half:].astype(bf16)
        g0[...] = last_g[:half].astype(bf16)
        g1[...] = last_g[half:].astype(bf16)


def feed_block(x, c, up, down, tile=512):
    half, width = x[0].shape
    units = up.shape[1]
    rows = 2 * half
    tiles = units // tile
    whole = pl.BlockSpec((half, width), lambda j: (0, 0))
    part = pl.BlockSpec((rows, tile), lambda j: (0, j))
    small = jax.ShapeDtypeStruct((half, width), bf16)
    big = jax.ShapeDtypeStruct((rows, units), bf16)
    hid, pre, y0, y1, g0, g1 = pl.pallas_call(
        functools.partial(feed_kernel, tiles),
        grid=(tiles,),
        in_specs=[
            whole,
            whole,
            whole,
            whole,
            pl.BlockSpec((width, tile), lambda j: (0, j)),
            pl.BlockSpec((tile, width), lambda j: (j, 0)),
        ],
        out_specs=[part, part, whole, whole, whole, whole],
        out_shape=[big, big, small, small, small, small],
        scratch_shapes=[pltpu.VMEM((rows, width), f32), pltpu.VMEM((rows, width), f32)],
        compiler_params=pltpu.CompilerParams(vmem_limit_bytes=VMEM_LIMIT),
        cost_estimate=pl.CostEstimate(
            flops=8 * rows * width * units,
            bytes_accessed=4 * (2 * rows * width + width * units + rows * units),
            transcendentals=rows * units,
        ),
        name="feed_block",
    )(*x, *c, up, down)
    return hid, pre, (y0, y1), (g0, g1)


def load_blocks(order, blocks, target):
    rows = blocks[0][0].shape[0] * 2
    for r, (low, high) in enumerate(blocks):
        at = pl.multiple_of((order[0] ^ r) * rows, rows)
        target[pl.ds(at, rows // 2), :] = low[...]
        target[pl.ds(at + rows // 2, rows // 2), :] = high[...]


def store_blocks(order, source, blocks, cast=None):
    rows = blocks[0][0].shape[0] * 2
    for r, (low, high) in enumerate(blocks):
        at = pl.multiple_of((order[0] ^ r) * rows, rows)
        low[...] = source[pl.ds(at, rows // 2), :].astype(low.dtype)
        high[...] = source[pl.ds(at + rows // 2, rows // 2), :].astype(high.dtype)


def pairs(refs):
    return [(refs[i], refs[i + 1]) for i in range(0, len(refs), 2)]


def allowed_of(seg_col, seg_row, q0, k0, k1, rows):
    same = seg_col[q0 : q0 + rows, :] == seg_row[:, k0:k1]
    shape = (rows, k1 - k0)
    i = lax.broadcasted_iota(jnp.int32, shape, 0) + q0
    j = lax.broadcasted_iota(jnp.int32, shape, 1) + k0
    return same & (j <= i)


def attend_kernel(nb, order, seg_col, seg_row, *refs):
    q_in, k_in, v_in = pairs(refs[: 2 * nb]), pairs(refs[2 * nb : 4 * nb]), pairs(refs[4 * nb : 6 * nb])
    out = pairs(refs[6 * nb : 8 * nb])
    q, k, v, o = refs[8 * nb :]
    load_blocks(order, q_in, q)
    load_blocks(order, k_in, k)
    load_blocks(order, v_in, v)
    step = CLIP_MOST
    for q0 in range(0, q.shape[0], step):
        k0, k1 = max(0, q0 - step), q0 + step
        s = dot(q[q0:k1, :], k[k0:k1, :], 1, 1)
        s = jnp.where(allowed_of(seg_col, seg_row, q0, k0, k1, step), s, masked_score)
        e = jnp.exp(s - jnp.max(s, axis=-1, keepdims=True))
        p = (e * (1.0 / jnp.sum(e, axis=-1, keepdims=True))).astype(bf16)
        o[q0:k1, :] = dot(p, v[k0:k1, :], 1, 0)
    store_blocks(order, o, out)


def attend_specs(blocks, heads):
    half = blocks[0][0].shape[0]
    specs, args = [], []
    for which in range(3):
        for low, high in blocks:
            for value in (low, high):
                specs.append(pl.BlockSpec((half, HEAD_DIM), lambda h, o, w=which: (0, w * heads + h)))
                args.append(value)
    return specs, args


def attend(order, seg, blocks):
    nb = len(blocks)
    half = blocks[0][0].shape[0]
    heads = blocks[0][0].shape[1] // (3 * HEAD_DIM)
    length = seg.shape[0]
    specs, args = attend_specs(blocks, heads)
    outs = pl.pallas_call(
        functools.partial(attend_kernel, nb),
        grid_spec=pltpu.PrefetchScalarGridSpec(
            num_scalar_prefetch=1,
            grid=(heads,),
            in_specs=[
                pl.BlockSpec((length, 1), lambda h, o: (0, 0)),
                pl.BlockSpec((1, length), lambda h, o: (0, 0)),
                *specs,
            ],
            out_specs=[pl.BlockSpec((half, HEAD_DIM), lambda h, o: (0, h))] * (2 * nb),
            scratch_shapes=[pltpu.VMEM((length, HEAD_DIM), bf16)] * 3
            + [pltpu.VMEM((length, HEAD_DIM), f32)],
        ),
        out_shape=[jax.ShapeDtypeStruct((half, heads * HEAD_DIM), bf16)] * (2 * nb),
        compiler_params=pltpu.CompilerParams(vmem_limit_bytes=VMEM_LIMIT),
        cost_estimate=pl.CostEstimate(
            flops=4 * heads * length * 512 * HEAD_DIM,
            bytes_accessed=8 * heads * length * HEAD_DIM,
            transcendentals=heads * length * 512,
        ),
        name="attend",
    )(order, seg.reshape(length, 1), seg.reshape(1, length), *args)
    return pairs(outs)


def attend_back_kernel(nb, scale, order, seg_col, seg_row, *refs):
    q_in, k_in, v_in, c_in = (pairs(refs[i * 2 * nb : (i + 1) * 2 * nb]) for i in range(4))
    dq_out, dk_out, dv_out = (pairs(refs[i * 2 * nb : (i + 1) * 2 * nb]) for i in range(4, 7))
    q, k, v, c, dq, dk, dv = refs[14 * nb :]
    load_blocks(order, q_in, q)
    load_blocks(order, k_in, k)
    load_blocks(order, v_in, v)
    load_blocks(order, c_in, c)
    step = CLIP_MOST
    length = q.shape[0]
    for q0 in range(0, length, step):
        k0, k1 = max(0, q0 - step), q0 + step
        qb, cb, kb, vb = q[q0:k1, :], c[q0:k1, :], k[k0:k1, :], v[k0:k1, :]
        s = dot(qb, kb, 1, 1)
        s = jnp.where(allowed_of(seg_col, seg_row, q0, k0, k1, step), s, masked_score)
        e = jnp.exp(s - jnp.max(s, axis=-1, keepdims=True))
        p = e * (1.0 / jnp.sum(e, axis=-1, keepdims=True))
        dp = dot(cb, vb, 1, 1)
        inner = jnp.sum(p * dp, axis=-1, keepdims=True)
        ds = (p * (dp - inner)).astype(bf16)
        dq[q0:k1, :] = dot(ds, kb, 1, 0) * scale
        dkb = dot(ds, qb, 0, 0)
        dvb = dot(p.astype(bf16), cb, 0, 0)
        if q0 > 0:
            dk[k0:q0, :] += dkb[:step]
            dv[k0:q0, :] += dvb[:step]
            dkb, dvb = dkb[step:], dvb[step:]
        dk[q0:k1, :] = dkb
        dv[q0:k1, :] = dvb
    store_blocks(order, dq, dq_out)
    store_blocks(order, dk, dk_out)
    store_blocks(order, dv, dv_out)


def attend_back(order, seg, blocks, grads, scale):
    nb = len(blocks)
    half = blocks[0][0].shape[0]
    heads = blocks[0][0].shape[1] // (3 * HEAD_DIM)
    length = seg.shape[0]
    specs, args = attend_specs(blocks, heads)
    for low, high in grads:
        specs += [pl.BlockSpec((half, HEAD_DIM), lambda h, o: (0, h))] * 2
        args += [low, high]
    outs = pl.pallas_call(
        functools.partial(attend_back_kernel, nb, scale),
        grid_spec=pltpu.PrefetchScalarGridSpec(
            num_scalar_prefetch=1,
            grid=(heads,),
            in_specs=[
                pl.BlockSpec((length, 1), lambda h, o: (0, 0)),
                pl.BlockSpec((1, length), lambda h, o: (0, 0)),
                *specs,
            ],
            out_specs=[pl.BlockSpec((half, HEAD_DIM), lambda h, o: (0, h))] * (6 * nb),
            scratch_shapes=[pltpu.VMEM((length, HEAD_DIM), bf16)] * 4
            + [pltpu.VMEM((length, HEAD_DIM), f32)] * 3,
        ),
        out_shape=[jax.ShapeDtypeStruct((half, heads * HEAD_DIM), bf16)] * (6 * nb),
        compiler_params=pltpu.CompilerParams(vmem_limit_bytes=VMEM_LIMIT),
        cost_estimate=pl.CostEstimate(
            flops=10 * heads * length * 512 * HEAD_DIM,
            bytes_accessed=14 * heads * length * HEAD_DIM,
            transcendentals=heads * length * 512,
        ),
        name="attend_back",
    )(order, seg.reshape(length, 1), seg.reshape(1, length), *args)
    outs = [pairs(outs[i * 2 * nb : (i + 1) * 2 * nb]) for i in range(3)]
    return [
        tuple(jnp.concatenate([outs[w][b][i] for w in range(3)], axis=1) for i in range(2))
        for b in range(nb)
    ]


def rows_of(blocks):
    return jnp.concatenate([half for block in blocks for half in block], axis=0)


def weight_grad(left, right):
    return lax.dot_general(left, right, (((0,), (0,)), ((), ())), preferred_element_type=f32).astype(bf16)


def scatter_sum(value, dim):
    return lax.psum_scatter(value, "dp", scatter_dimension=dim, tiled=True).astype(f32)


def local(
    group_count,
    tokens,
    segment_ids,
    query_weight,
    key_weight,
    value_weight,
    out_weight,
    up_weight,
    down_weight,
    attn_gain,
    mlp_gain,
    out_cotangent,
):
    group = Group(group_count)
    seq_count, length = segment_ids.shape
    per_seq = group_count // seq_count
    score_scale = 1.0 / math.sqrt(HEAD_DIM)
    me = lax.axis_index("mp")
    order = (me % per_seq).astype(jnp.int32).reshape(1)
    half = tokens.shape[0] // 2
    columns = query_weight.shape[1]

    def halves(value):
        return value[:half], value[half:]

    segs = [
        lax.dynamic_index_in_dim(segment_ids, (me // per_seq) ^ s, 0, keepdims=False)
        for s in range(seq_count)
    ]
    residual_in = [part.astype(f32) for part in halves(tokens)]
    normed = [norm_rows(part, attn_gain).astype(bf16) for part in residual_in]
    attn_in = group.gather(*normed)
    cot = group.gather(*halves(out_cotangent))

    qkv_weight = jnp.concatenate([query_weight, key_weight, value_weight], axis=1)
    qkv_scale = jnp.concatenate(
        [jnp.full((1, columns), score_scale, f32), jnp.ones((1, 2 * columns), f32)], axis=1
    )
    qkv = [mm(block, qkv_weight, scale=qkv_scale, name="qkv") for block in attn_in]
    context = []
    for s in range(seq_count):
        context += attend(order, segs[s], qkv[s * per_seq : (s + 1) * per_seq])
    attn_parts = [mm(block, out_weight, name="out_proj") for block in context]
    attn_rows = group.reduce(attn_parts)
    residual_mid = [residual_in[i] + total(attn_rows[i]) for i in range(2)]
    normed_mid = [norm_rows(part, mlp_gain).astype(bf16) for part in residual_mid]
    mlp_in = group.gather(*normed_mid)

    fed = [feed_block(mlp_in[r], cot[r], up_weight, down_weight) for r in range(group_count)]
    mlp_rows = group.reduce([f[2] for f in fed])
    mid_rows = group.reduce([f[3] for f in fed])
    hidden = jnp.concatenate([f[0] for f in fed], axis=0)
    pre_grad = jnp.concatenate([f[1] for f in fed], axis=0)
    layer_output = jnp.concatenate(
        [(residual_mid[i] + total(mlp_rows[i])).astype(bf16) for i in range(2)], axis=0
    )
    down_grad = scatter_sum(weight_grad(hidden, rows_of(cot)), 1)
    up_grad = scatter_sum(weight_grad(rows_of(mlp_in), pre_grad), 0)

    middle, mlp_gain_grad = [], 0.0
    for i in range(2):
        back, gain_grad = norm_back(residual_mid[i], mlp_gain, total(mid_rows[i]))
        middle.append(halves(out_cotangent)[i].astype(f32) + back)
        mlp_gain_grad = mlp_gain_grad + gain_grad
    middle_all = group.gather(*[part.astype(bf16) for part in middle])
    context_grad = [mm(block, out_weight, trans=True, name="context_grad") for block in middle_all]
    out_grad = scatter_sum(weight_grad(rows_of(context), rows_of(middle_all)), 1)

    qkv_grad = []
    for s in range(seq_count):
        at = slice(s * per_seq, (s + 1) * per_seq)
        qkv_grad += attend_back(order, segs[s], qkv[at], context_grad[at], score_scale)
    parts = [mm(block, qkv_weight, trans=True, name="qkv_back") for block in qkv_grad]
    attn_back_rows = group.reduce(parts)
    qkv_weight_grad = scatter_sum(weight_grad(rows_of(attn_in), rows_of(qkv_grad)), 0)

    tokens_grad, attn_gain_grad = [], 0.0
    for i in range(2):
        back, gain_grad = norm_back(residual_in[i], attn_gain, total(attn_back_rows[i]))
        tokens_grad.append(middle[i] + back)
        attn_gain_grad = attn_gain_grad + gain_grad
    attn_gain_grad, mlp_gain_grad = lax.psum((attn_gain_grad, mlp_gain_grad), ("dp", "mp"))
    return (
        layer_output,
        jnp.concatenate(tokens_grad, axis=0),
        qkv_weight_grad[:, :columns],
        qkv_weight_grad[:, columns : 2 * columns],
        qkv_weight_grad[:, 2 * columns :],
        out_grad,
        up_grad,
        down_grad,
        attn_gain_grad,
        mlp_gain_grad,
    )


def solution(mesh):
    return jax.shard_map(
        functools.partial(local, mesh.shape["mp"]),
        mesh=mesh,
        in_specs=(
            P(("dp", "mp"), None),
            P("dp", None),
            P(None, "mp"),
            P(None, "mp"),
            P(None, "mp"),
            P("mp", None),
            P(None, "mp"),
            P("mp", None),
            P(),
            P(),
            P(("dp", "mp"), None),
        ),
        out_specs=(
            P(("dp", "mp"), None),
            P(("dp", "mp"), None),
            P("dp", "mp"),
            P("dp", "mp"),
            P("dp", "mp"),
            P("mp", "dp"),
            P("dp", "mp"),
            P("mp", "dp"),
            P(),
            P(),
        ),
        check_vma=False,
    )
```

time: 1110 us -> 779 us (0.70)
  waiting for transfers between devices: 616 us -> 241 us
  matrix products: 285 us -> 57.1 us
  Pallas kernels: 0 us -> 211 us
  starting transfers between devices: 0.83 us -> 53 us
    reduce_scatter x10 -> x4, waiting for transfers between devices: 394 us -> 85.8 us  [scatter_sum(): lax.psum_scatter(value, 'dp', scatter_dimension=dim, tiled=True).astype(f32)]
    dot_general x32 -> x4, matrix products: 285 us -> 57.1 us  [weight_grad(): lax.dot_general(left, right, (((0,), (0,)), ((), ())), preferred_element_...]
    all_gather x4 -> x0, waiting for transfers between devices: 221 us -> none  [the longest x1 73 us: local(): lax.all_gather(normed_attn.astype(jnp.bfloat16), 'mp', axis=0, tiled=True)]
    pallas_call x0 -> x24, Pallas kernels: none -> 211 us  [the longest x4 85.9 us: feed_block(): pl.pallas_call(functools.partial(feed_kernel, tiles), grid=(tiles,), in_s...]
    ppermute x0 -> x48, waiting for transfers between devices: none -> 155 us  [swap(): return lax.ppermute(value, 'mp', [(m, m ^ r) for m in range(self.count)])]
    unnamed x56 -> x285, local copies, waits for them, and re-layouts: 3.2 us -> 74.2 us
    ppermute x0 -> x48, starting transfers between devices: none -> 52.8 us  [swap(): return lax.ppermute(value, 'mp', [(m, m ^ r) for m in range(self.count)])]
    dynamic_update_slice x14 -> x0, local copies, waits for them, and re-layouts: 27.5 us -> none  [local(): lax.map(attend_forward, (queries_seq, keys_seq, values_seq, segment_ids))]
  transfers between devices with their start and end apart: 14 -> 52, of which waited for: 12 -> 18; matrix products, arithmetic and copies ran while one was open for 25% -> 22% of each run, Pallas kernels for 0% -> 27%
where the time goes in v1:
time: 779 us; the launch traced here: 774 us
  waiting for transfers between devices  241 us (31%)
  Pallas kernels  211 us (27%)
  local copies, waits for them, and re-layouts  88 us (11%)
  other arithmetic  68.1 us (9%)
  matrix products  57.1 us (7%)
  starting transfers between devices  53 us (7%)
  blocking collectives  41.6 us (5%)
  between operations  14.9 us (2%)
    ppermute x48, waiting for transfers between devices, swap(): return lax.ppermute(value, 'mp', [(m, m ^ r) for m in range(self.count)])  155 us
    pallas_call x4, Pallas kernels, feed_block(): pl.pallas_call(functools.partial(feed_kernel, tiles), grid=(tiles,), in_s...  85.9 us
    reduce_scatter x4, waiting for transfers between devices, scatter_sum(): lax.psum_scatter(value, 'dp', scatter_dimension=dim, tiled=True).astype(f32)  85.8 us
    pallas_call x16, Pallas kernels, mm(): pl.pallas_call(functools.partial(mm_kernel, trans, sizes, scaled), grid=(...  85.2 us
    unnamed x285, local copies, waits for them, and re-layouts  74.2 us
    dot_general x4, matrix products, weight_grad(): lax.dot_general(left, right, (((0,), (0,)), ((), ())), preferred_element_...  57.1 us
    ppermute x48, starting transfers between devices, swap(): return lax.ppermute(value, 'mp', [(m, m ^ r) for m in range(self.count)])  52.8 us
    psum x1, blocking collectives, local(): lax.psum((attn_gain_grad, mlp_gain_grad), ('dp', 'mp'))  41.6 us
  transfers between devices with their start and end apart: 52, of which 18 were waited for; matrix products, arithmetic and copies ran while one was open for 22% of the time, Pallas kernels for 27%

profile of v1, /device:TPU:0, one launch (start us, length us, event | category | flops | bytes accessed | tf_op | source)
XLA Modules:
  0.0 774.3 jit_solution(4359926540042401751)
XLA Ops:
  23.3 11.8 %collective-permute-done.4.refs_1_ = bf16[192,2048]{1,0:T(8,128)(2,1)} collective-permute-done((bf16[192,2048]{1,0:T(8,128)(2,1)}, bf16[192,2048]{1,0:T(8,128)(2,1)}, u32[]{:S(2)}, u32[]{:S(2)}) %collective-permute-start.4) | collective-permute-done | bytes 786464 | tf_op jit(solution)/shard_map/ppermute | solution.py:28
  37.1 16.9 %collective-permute-done.refs_0_ = bf16[192,2048]{1,0:T(8,128)(2,1)} collective-permute-done((bf16[192,2048]{1,0:T(8,128)(2,1)}, bf16[192,2048]{1,0:T(8,128)(2,1)}, u32[]{:S(2)}, u32[]{:S(2)}) %collective-permute-start) | collective-permute-done | bytes 786464 | tf_op jit(solution)/shard_map/ppermute | solution.py:28
  60.7 6.6 qkv.6
  69.3 15.4 %collective-permute-done.5.refs_0_ = bf16[192,2048]{1,0:T(8,128)(2,1)S(1)} collective-permute-done((bf16[192,2048]{1,0:T(8,128)(2,1)}, bf16[192,2048]{1,0:T(8,128)(2,1)S(1)}, u32[]{:S(2)}, u32[]{:S(2)}) %collective-permute-start.5) | collective-permute-done | bytes 786464 | tf_op jit(solution)/shard_map/ppermute | solution.py:28
  85.6 6.5 qkv.7
  92.1 8.2 %attend.3 = (bf16[192,512]{1,0:T(8,128)(2,1)}, bf16[192,512]{1,0:T(8,128)(2,1)}, bf16[192,512]{1,0:T(8,128)(2,1)}, bf16[192,512]{1,0:T(8,128)(2,1)}) custom-call(s32[1]{0:T(128)} %bitcast.order, s32[768,1]{1,0:T(8,128)} %copy.22.seg_col, s32[1,768]{1,0:T(1,128)} %copy-done.93, bf16[192,1536]{1,0:T(8,128)(2,1)} %get-tuple-element.108.refs_0_.refs_4_.refs_8_, ...), custom_call_target="tpu_custom_call" | custom-call | flops 805306368 | bytes 3145728 | tf_op jit(solution)/shard_map/attend/pallas_call | solution.py:283
  100.3 4.4 out_proj.7
  106.4 6.5 qkv.4
  112.8 6.5 qkv.5
  120.8 8.2 %attend.2 = (bf16[192,512]{1,0:T(8,128)(2,1)}, bf16[192,512]{1,0:T(8,128)(2,1)}, bf16[192,512]{1,0:T(8,128)(2,1)}, bf16[192,512]{1,0:T(8,128)(2,1)}) custom-call(s32[1]{0:T(128)} %bitcast.order, s32[768,1]{1,0:T(8,128)} %copy.21.seg_col, s32[1,768]{1,0:T(1,128)} %copy-done.94, bf16[192,1536]{1,0:T(8,128)(2,1)} %get-tuple-element.98.refs_0_.refs_4_.refs_8_, ...), custom_call_target="tpu_custom_call" | custom-call | flops 805306368 | bytes 3145728 | tf_op jit(solution)/shard_map/attend/pallas_call | solution.py:283
  129.1 4.5 out_proj.5
  134.8 4.3 out_proj.6
  147.5 4.5 out_proj.4
  160.1 16.7 %collective-permute-done.8 = bf16[192,2048]{1,0:T(8,128)(2,1)} collective-permute-done((bf16[192,2048]{1,0:T(8,128)(2,1)}, bf16[192,2048]{1,0:T(8,128)(2,1)}, u32[]{:S(2)}, u32[]{:S(2)}) %collective-permute-start.8) | collective-permute-done | bytes 786464 | tf_op jit(solution)/shard_map/ppermute | solution.py:28
  185.1 8.5 %collective-permute-done.20.c1 = bf16[192,2048]{1,0:T(8,128)(2,1)} collective-permute-done((bf16[192,2048]{1,0:T(8,128)(2,1)}, bf16[192,2048]{1,0:T(8,128)(2,1)}, u32[]{:S(2)}, u32[]{:S(2)}) %collective-permute-start.20) | collective-permute-done | bytes 786464 | tf_op jit(solution)/shard_map/ppermute | solution.py:28
  202.3 22.1 %collective-permute-done.18.x1 = bf16[192,2048]{1,0:T(8,128)(2,1)} collective-permute-done((bf16[192,2048]{1,0:T(8,128)(2,1)S(1)}, bf16[192,2048]{1,0:T(8,128)(2,1)}, u32[]{:S(2)}, u32[]{:S(2)}) %collective-permute-start.18) | collective-permute-done | bytes 786464 | tf_op jit(solution)/shard_map/ppermute | solution.py:28
  227.9 21.6 %feed_block.6 = (bf16[384,2048]{1,0:T(8,128)(2,1)}, bf16[384,2048]{1,0:T(8,128)(2,1)}, bf16[192,2048]{1,0:T(8,128)(2,1)}, bf16[192,2048]{1,0:T(8,128)(2,1)}, bf1...) custom-call(bf16[192,2048]{1,0:T(8,128)(2,1)} %copy-done.64, bf16[192,2048]{1,0:T(8,128)(2,1)} %collective-permute-done.18.x1, ...), custom_call_target="tpu_custom_call" | custom-call | flops 12884901888 | bytes 26214400 | tf_op jit(solution)/shard_map/feed_block/pallas_call | solution.py:195
  250.7 4.7 collective-permute-done.22.x1
  256.5 5.5 collective-permute-done.21.x0
  262.1 21.4 %feed_block.7 = (bf16[384,2048]{1,0:T(8,128)(2,1)}, bf16[384,2048]{1,0:T(8,128)(2,1)}, bf16[192,2048]{1,0:T(8,128)(2,1)}, bf16[192,2048]{1,0:T(8,128)(2,1)}, bf1...) custom-call(bf16[192,2048]{1,0:T(8,128)(2,1)} %collective-permute-done.21.x0, ...), custom_call_target="tpu_custom_call" | custom-call | flops 12884901888 | bytes 26214400 | tf_op jit(solution)/shard_map/feed_block/pallas_call | solution.py:195
  286.4 21.7 %feed_block.5 = (bf16[384,2048]{1,0:T(8,128)(2,1)}, bf16[384,2048]{1,0:T(8,128)(2,1)}, bf16[192,2048]{1,0:T(8,128)(2,1)}, bf16[192,2048]{1,0:T(8,128)(2,1)}, bf1...) custom-call(bf16[192,2048]{1,0:T(8,128)(2,1)} %copy-done.66, bf16[192,2048]{1,0:T(8,128)(2,1)} %copy-done.72, ...), custom_call_target="tpu_custom_call" | custom-call | flops 12884901888 | bytes 26214400 | tf_op jit(solution)/shard_map/feed_block/pallas_call | solution.py:195
  309.7 11.5 %collective-permute-done.31 = bf16[192,2048]{1,0:T(8,128)(2,1)} collective-permute-done((bf16[192,2048]{1,0:T(8,128)(2,1)}, bf16[192,2048]{1,0:T(8,128)(2,1)}, u32[]{:S(2)}, u32[]{:S(2)}) %collective-permute-start.31) | collective-permute-done | bytes 786464 | tf_op jit(solution)/shard_map/ppermute | solution.py:28
  327.8 11.7 %collective-permute-done.33 = bf16[192,2048]{1,0:T(8,128)(2,1)S(1)} collective-permute-done((bf16[192,2048]{1,0:T(8,128)(2,1)}, bf16[192,2048]{1,0:T(8,128)(2,1)S(1)}, u32[]{:S(2)}, u32[]{:S(2)}) %collective-permute-start.33) | collective-permute-done | bytes 786464 | tf_op jit(solution)/shard_map/ppermute | solution.py:28
  342.5 13.9 %collective-permute-done.27 = bf16[192,2048]{1,0:T(8,128)(2,1)S(1)} collective-permute-done((bf16[192,2048]{1,0:T(8,128)(2,1)S(1)}, bf16[192,2048]{1,0:T(8,128)(2,1)S(1)}, u32[]{:S(2)}, u32[]{:S(2)}) %collective-permute-start.27) | collective-permute-done | bytes 786464 | tf_op jit(solution)/shard_map/ppermute | solution.py:28
  361.6 21.3 %feed_block.4 = (bf16[384,2048]{1,0:T(8,128)(2,1)}, bf16[384,2048]{1,0:T(8,128)(2,1)}, bf16[192,2048]{1,0:T(8,128)(2,1)}, bf16[192,2048]{1,0:T(8,128)(2,1)}, bf1...) custom-call(bf16[192,2048]{1,0:T(8,128)(2,1)} %copy-done.74, bf16[192,2048]{1,0:T(8,128)(2,1)} %copy-done.75, ...), custom_call_target="tpu_custom_call" | custom-call | flops 12884901888 | bytes 26214400 | tf_op jit(solution)/shard_map/feed_block/pallas_call | solution.py:195
  383.0 6.6 multiply_reduce_fusion
  389.6 3.9 constant_dynamic-update-slice_fusion.36
  393.6 3.8 constant_dynamic-update-slice_fusion.35
  404.8 3.8 context_grad.4
  409.4 8.4 %collective-permute-done.36.refs_0_ = bf16[192,2048]{1,0:T(8,128)(2,1)S(1)} collective-permute-done((bf16[192,2048]{1,0:T(8,128)(2,1)}, bf16[192,2048]{1,0:T(8,128)(2,1)S(1)}, u32[]{:S(2)}, u32[]{:S(2)}) %collective-permute-start.36) | collective-permute-done | bytes 786464 | tf_op jit(solution)/shard_map/ppermute | solution.py:28
  418.7 3.8 context_grad.5
  422.5 11.4 %attend_back.2 = (bf16[192,512]{1,0:T(8,128)(2,1)}, bf16[192,512]{1,0:T(8,128)(2,1)}, bf16[192,512]{1,0:T(8,128)(2,1)}, bf16[192,512]{1,0:T(8,128)(2,1)}, bf16[1...) custom-call(s32[1]{0:T(128)} %bitcast.order, ...), custom_call_target="tpu_custom_call" | custom-call | flops 2013265920 | bytes 5505024 | tf_op jit(solution)/shard_map/attend_back/pallas_call | solution.py:352
  449.4 3.8 context_grad.6
  459.2 7.4 convolution_convert_fusion.3
  469.7 3.8 context_grad.7
  473.5 11.7 %attend_back.3 = (bf16[192,512]{1,0:T(8,128)(2,1)}, bf16[192,512]{1,0:T(8,128)(2,1)}, bf16[192,512]{1,0:T(8,128)(2,1)}, bf16[192,512]{1,0:T(8,128)(2,1)}, bf16[1...) custom-call(s32[1]{0:T(128)} %bitcast.order, ...), custom_call_target="tpu_custom_call" | custom-call | flops 2013265920 | bytes 5505024 | tf_op jit(solution)/shard_map/attend_back/pallas_call | solution.py:352
  497.8 15.3 %convolution_convert_fusion.2 = bf16[2048,1536]{1,0:T(8,128)(2,1)} fusion(bf16[1536,2048]{1,0:T(8,128)(2,1)} %constant_dynamic-update-slice_fusion.3, bf16[1536,1536]{1,0:T(8,128)(2,1)} %constant_dynamic-update-slice_fusion.52), kind=kOutput, calls=%fused_computation.2 | convolution fusion | flops 9666822144 | bytes 17301504 | tf_op jit(solution)/shard_map/dot_general | solution.py:387
  522.2 16.8 %convolution_convert_fusion = bf16[2048,2048]{1,0:T(8,128)(2,1)} fusion(bf16[1536,2048]{1,0:T(8,128)(2,1)S(1)} %constant_dynamic-update-slice_fusion.45, bf16[384,2048]{1,0:T(8,128)(2,1)S(1)} %copy-done.113, bf16[384,2048]{1,0:T(8,128)(2,1)S(1)} %copy-done.111, bf16[384,2048]{1,0:T(8,128)(2,1)S(1)} %copy-done.114, bf16[384,2048]{1,0:T(8,128)(2,1)} %get-tuple-element.182), kind=kOutput, calls=%fused_computation | convolution fusion | flops 12914262016 | bytes 20971520 | tf_op jit(solution)/shard_map/dot_general | solution.py:387
  549.7 17.6 %convolution_convert_fusion.1 = bf16[2048,2048]{1,0:T(8,128)(2,1)} fusion(bf16[1536,2048]{1,0:T(8,128)(2,1)} %constant_dynamic-update-slice_fusion.37, bf16[384,2048]{1,0:T(8,128)(2,1)S(1)} %copy-done.110, bf16[384,2048]{1,0:T(8,128)(2,1)S(1)} %copy-done.109, bf16[384,2048]{1,0:T(8,128)(2,1)S(1)} %copy-done.112, bf16[384,2048]{1,0:T(8,128)(2,1)S(1)} %copy-done.115), kind=kOutput, calls=%fused_computation.1 | convolution fusion | flops 12914262016 | bytes 20971520 | tf_op jit(solution)/shard_map/dot_general | solution.py:387
  571.9 6.6 qkv_back.7
  579.1 6.6 qkv_back.5
  590.5 6.5 qkv_back.6
  609.5 6.7 qkv_back.4
  616.3 3.4 collective-permute-done.44
  620.6 4.1 fusion.31
  624.7 41.6 %all-reduce = (f32[2048]{0:T(1024)}, f32[2048]{0:T(1024)}) all-reduce(f32[2048]{0:T(1024)S(1)} %add.201, f32[2048]{0:T(1024)S(1)} %copy-done.97), channel_id=1, replica_groups=mesh['dp'=8,'mp'=4] {'dp','mp'}, use_global_device_ids=true, to_apply=%region_22.23 | all-reduce | flops 4096 | bytes 32768 | tf_op jit(solution)/shard_map/psum | solution.py:476
  666.4 3.7 fusion.37
  679.0 85.8 %reduce-scatter.9.cloned.1.call-done = bf16[256,2048]{1,0:T(8,128)(2,1)} async-done(((bf16[2048,2048]{1,0:T(8,128)(2,1)}), bf16[256,2048]{1,0:T(8,128)(2,1)}) %reduce-scatter.9.cloned.1.call-update) | async-done | bytes 1048592 | tf_op jit(solution)/shard_map/reduce_scatter | solution.py:391
  (438 shorter events, 191.6 us)
Async XLA Ops:
  7.2 664.9 %reduce-scatter.7.cloned.1.call-start = ((), (), s32[]{:S(2)}) async-start(), calls=%async_computation.5 | async-start | bytes 2359296 | tf_op jit(solution)/shard_map/reduce_scatter | solution.py:391
  13.4 21.6 %collective-permute-start.4 = (bf16[192,2048]{1,0:T(8,128)(2,1)}, bf16[192,2048]{1,0:T(8,128)(2,1)}, u32[]{:S(2)}, u32[]{:S(2)}) collective-permute-start(bf16[192,2048]{1,0:T(8,128)(2,1)} %get-tuple-element.218.refs_1_), channel_id=1, source_target_pairs={{0,2},{1,3},{2,0},{3,1},{4,6},{5,7},{6,4},{7,5},{8,10},{9,11},{10,... | collective-permute-start | bytes 2359304 | tf_op jit(solution)/shard_map/ppermute | solution.py:28
  16.4 96.4 %collective-permute-start.1 = (bf16[192,2048]{1,0:T(8,128)(2,1)}, bf16[192,2048]{1,0:T(8,128)(2,1)}, u32[]{:S(2)}, u32[]{:S(2)}) collective-permute-start(bf16[192,2048]{1,0:T(8,128)(2,1)} %get-tuple-element.218.refs_1_), channel_id=1, source_target_pairs={{0,1},{1,0},{2,3},{3,2},{4,5},{5,4},{6,7},{7,6},{8,9},{9,8},{10,11... | collective-permute-start | bytes 2359304 | tf_op jit(solution)/shard_map/ppermute | solution.py:28
  17.9 42.8 %collective-permute-start.3 = (bf16[192,2048]{1,0:T(8,128)(2,1)}, bf16[192,2048]{1,0:T(8,128)(2,1)}, u32[]{:S(2)}, u32[]{:S(2)}) collective-permute-start(bf16[192,2048]{1,0:T(8,128)(2,1)} %get-tuple-element.220.refs_0_), channel_id=1, source_target_pairs={{0,2},{1,3},{2,0},{3,1},{4,6},{5,7},{6,4},{7,5},{8,10},{9,11},{10,... | collective-permute-start | bytes 2359304 | tf_op jit(solution)/shard_map/ppermute | solution.py:28
  18.4 35.6 %collective-permute-start = (bf16[192,2048]{1,0:T(8,128)(2,1)}, bf16[192,2048]{1,0:T(8,128)(2,1)}, u32[]{:S(2)}, u32[]{:S(2)}) collective-permute-start(bf16[192,2048]{1,0:T(8,128)(2,1)} %get-tuple-element.220.refs_0_), channel_id=1, source_target_pairs={{0,1},{1,0},{2,3},{3,2},{4,5},{5,4},{6,7},{7,6},{8,9},{9,8},{10,11... | collective-permute-start | bytes 2359304 | tf_op jit(solution)/shard_map/ppermute | solution.py:28
  19.8 180.5 %collective-permute-start.19 = (bf16[192,2048]{1,0:T(8,128)(2,1)}, bf16[192,2048]{1,0:T(8,128)(2,1)}, u32[]{:S(2)}, u32[]{:S(2)}) collective-permute-start(bf16[192,2048]{1,0:T(8,128)(2,1)} %get-tuple-element.230.c0), channel_id=1, source_target_pairs={{0,2},{1,3},{2,0},{3,1},{4,6},{5,7},{6,4},{7,5},{8,10},{9,11},{10,... | collective-permute-start | bytes 2359304 | tf_op jit(solution)/shard_map/ppermute | solution.py:28
  35.1 34.2 %collective-permute-start.6 = (bf16[192,2048]{1,0:T(8,128)(2,1)}, bf16[192,2048]{1,0:T(8,128)(2,1)S(1)}, u32[]{:S(2)}, u32[]{:S(2)}) collective-permute-start(bf16[192,2048]{1,0:T(8,128)(2,1)} %collective-permute-done.4.refs_1_), channel_id=1, source_target_pairs={{0,1},{1,0},{2,3},{3,2},{4,5},{5,4},{6,7},{7,6},{8,9},{9,8},{10,11... | collective-permute-start | bytes 2359304 | tf_op jit(solution)/shard_map/ppermute | solution.py:28
  54.0 30.7 %collective-permute-start.5 = (bf16[192,2048]{1,0:T(8,128)(2,1)}, bf16[192,2048]{1,0:T(8,128)(2,1)S(1)}, u32[]{:S(2)}, u32[]{:S(2)}) collective-permute-start(bf16[192,2048]{1,0:T(8,128)(2,1)} %collective-permute-done.refs_0_), channel_id=1, source_target_pairs={{0,2},{1,3},{2,0},{3,1},{4,6},{5,7},{6,4},{7,5},{8,10},{9,11},{10,... | collective-permute-start | bytes 2359304 | tf_op jit(solution)/shard_map/ppermute | solution.py:28
  104.6 34.7 %collective-permute-start.7 = (bf16[192,2048]{1,0:T(8,128)(2,1)}, bf16[192,2048]{1,0:T(8,128)(2,1)}, u32[]{:S(2)}, u32[]{:S(2)}) collective-permute-start(bf16[192,2048]{1,0:T(8,128)(2,1)} %get-tuple-element.117), channel_id=1, source_target_pairs={{0,1},{1,0},{2,3},{3,2},{4,5},{5,4},{6,7},{7,6},{8,9},{9,8},{10,11... | collective-permute-start | bytes 2359304 | tf_op jit(solution)/shard_map/ppermute | solution.py:28
  119.3 24.4 %collective-permute-start.9 = (bf16[192,2048]{1,0:T(8,128)(2,1)}, bf16[192,2048]{1,0:T(8,128)(2,1)}, u32[]{:S(2)}, u32[]{:S(2)}) collective-permute-start(bf16[192,2048]{1,0:T(8,128)(2,1)} %get-tuple-element.120), channel_id=1, source_target_pairs={{0,2},{1,3},{2,0},{3,1},{4,6},{5,7},{6,4},{7,5},{8,10},{9,11},{10,... | collective-permute-start | bytes 2359304 | tf_op jit(solution)/shard_map/ppermute | solution.py:28
  133.5 24.2 %collective-permute-start.2 = (bf16[192,2048]{1,0:T(8,128)(2,1)}, bf16[192,2048]{1,0:T(8,128)(2,1)S(1)}, u32[]{:S(2)}, u32[]{:S(2)}) collective-permute-start(bf16[192,2048]{1,0:T(8,128)(2,1)} %get-tuple-element.107), channel_id=1, source_target_pairs={{0,1},{1,0},{2,3},{3,2},{4,5},{5,4},{6,7},{7,6},{8,9},{9,8},{10,11... | collective-permute-start | bytes 2359304 | tf_op jit(solution)/shard_map/ppermute | solution.py:28
  139.1 20.7 %collective-permute-start.11 = (bf16[192,2048]{1,0:T(8,128)(2,1)}, bf16[192,2048]{1,0:T(8,128)(2,1)S(1)}, u32[]{:S(2)}, u32[]{:S(2)}) collective-permute-start(bf16[192,2048]{1,0:T(8,128)(2,1)} %get-tuple-element.121), channel_id=1, source_target_pairs={{0,2},{1,3},{2,0},{3,1},{4,6},{5,7},{6,4},{7,5},{8,10},{9,11},{10,... | collective-permute-start | bytes 2359304 | tf_op jit(solution)/shard_map/ppermute | solution.py:28
  141.9 34.8 %collective-permute-start.8 = (bf16[192,2048]{1,0:T(8,128)(2,1)}, bf16[192,2048]{1,0:T(8,128)(2,1)}, u32[]{:S(2)}, u32[]{:S(2)}) collective-permute-start(bf16[192,2048]{1,0:T(8,128)(2,1)} %add_convert_fusion.9), channel_id=1, source_target_pairs={{0,2},{1,3},{2,0},{3,1},{4,6},{5,7},{6,4},{7,5},{8,10},{9,11},{10,... | collective-permute-start | bytes 2359304 | tf_op jit(solution)/shard_map/ppermute | solution.py:28
  146.0 30.8 %collective-permute-start.10 = (bf16[192,2048]{1,0:T(8,128)(2,1)}, bf16[192,2048]{1,0:T(8,128)(2,1)}, u32[]{:S(2)}, u32[]{:S(2)}) collective-permute-start(bf16[192,2048]{1,0:T(8,128)(2,1)} %add_convert_fusion.8), channel_id=1, source_target_pairs={{0,1},{1,0},{2,3},{3,2},{4,5},{5,4},{6,7},{7,6},{8,9},{9,8},{10,11... | collective-permute-start | bytes 2359304 | tf_op jit(solution)/shard_map/ppermute | solution.py:28
  157.7 44.3 %collective-permute-start.14 = (bf16[192,2048]{1,0:T(8,128)(2,1)}, bf16[192,2048]{1,0:T(8,128)(2,1)}, u32[]{:S(2)}, u32[]{:S(2)}) collective-permute-start(bf16[192,2048]{1,0:T(8,128)(2,1)} %get-tuple-element.230.c0), channel_id=1, source_target_pairs={{0,1},{1,0},{2,3},{3,2},{4,5},{5,4},{6,7},{7,6},{8,9},{9,8},{10,11... | collective-permute-start | bytes 2359304 | tf_op jit(solution)/shard_map/ppermute | solution.py:28
  159.8 33.8 %collective-permute-start.20 = (bf16[192,2048]{1,0:T(8,128)(2,1)}, bf16[192,2048]{1,0:T(8,128)(2,1)}, u32[]{:S(2)}, u32[]{:S(2)}) collective-permute-start(bf16[192,2048]{1,0:T(8,128)(2,1)} %get-tuple-element.229.c1), channel_id=1, source_target_pairs={{0,2},{1,3},{2,0},{3,1},{4,6},{5,7},{6,4},{7,5},{8,10},{9,11},{10,... | collective-permute-start | bytes 2359304 | tf_op jit(solution)/shard_map/ppermute | solution.py:28
  181.5 43.5 %collective-permute-start.17 = (bf16[192,2048]{1,0:T(8,128)(2,1)S(1)}, bf16[192,2048]{1,0:T(8,128)(2,1)S(1)}, u32[]{:S(2)}, u32[]{:S(2)}) collective-permute-start(bf16[192,2048]{1,0:T(8,128)(2,1)S(1)} %get-tuple-element.210.x0), channel_id=1, source_target_pairs={{0,2},{1,3},{2,0},{3,1},{4,6},{5,7},{6,4},{7,5},{8,10},{9,11},{10,... | collective-permute-start | bytes 2359304 | tf_op jit(solution)/shard_map/ppermute | solution.py:28
  181.8 44.6 %collective-permute-start.12 = (bf16[192,2048]{1,0:T(8,128)(2,1)S(1)}, bf16[192,2048]{1,0:T(8,128)(2,1)S(1)}, u32[]{:S(2)}, u32[]{:S(2)}) collective-permute-start(bf16[192,2048]{1,0:T(8,128)(2,1)S(1)} %get-tuple-element.210.x0), channel_id=1, source_target_pairs={{0,1},{1,0},{2,3},{3,2},{4,5},{5,4},{6,7},{7,6},{8,9},{9,8},{10,11... | collective-permute-start | bytes 2359304 | tf_op jit(solution)/shard_map/ppermute | solution.py:28
  193.6 30.8 %collective-permute-start.18 = (bf16[192,2048]{1,0:T(8,128)(2,1)S(1)}, bf16[192,2048]{1,0:T(8,128)(2,1)}, u32[]{:S(2)}, u32[]{:S(2)}) collective-permute-start(bf16[192,2048]{1,0:T(8,128)(2,1)S(1)} %get-tuple-element.208.x1), channel_id=1, source_target_pairs={{0,2},{1,3},{2,0},{3,1},{4,6},{5,7},{6,4},{7,5},{8,10},{9,11},{10,... | collective-permute-start | bytes 2359304 | tf_op jit(solution)/shard_map/ppermute | solution.py:28
  200.3 84.7 %collective-permute-start.15 = (bf16[192,2048]{1,0:T(8,128)(2,1)}, bf16[192,2048]{1,0:T(8,128)(2,1)}, u32[]{:S(2)}, u32[]{:S(2)}) collective-permute-start(bf16[192,2048]{1,0:T(8,128)(2,1)} %get-tuple-element.229.c1), channel_id=1, source_target_pairs={{0,1},{1,0},{2,3},{3,2},{4,5},{5,4},{6,7},{7,6},{8,9},{9,8},{10,11... | collective-permute-start | bytes 2359304 | tf_op jit(solution)/shard_map/ppermute | solution.py:28
  202.0 47.5 %collective-permute-start.24 = (bf16[192,2048]{1,0:T(8,128)(2,1)}, bf16[192,2048]{1,0:T(8,128)(2,1)}, u32[]{:S(2)}, u32[]{:S(2)}) collective-permute-start(bf16[192,2048]{1,0:T(8,128)(2,1)} %collective-permute-done.20.c1), channel_id=1, source_target_pairs={{0,1},{1,0},{2,3},{3,2},{4,5},{5,4},{6,7},{7,6},{8,9},{9,8},{10,11... | collective-permute-start | bytes 2359304 | tf_op jit(solution)/shard_map/ppermute | solution.py:28
  224.4 25.7 %collective-permute-start.23 = (bf16[192,2048]{1,0:T(8,128)(2,1)}, bf16[192,2048]{1,0:T(8,128)(2,1)}, u32[]{:S(2)}, u32[]{:S(2)}) collective-permute-start(bf16[192,2048]{1,0:T(8,128)(2,1)} %collective-permute-done.14.c0), channel_id=1, source_target_pairs={{0,2},{1,3},{2,0},{3,1},{4,6},{5,7},{6,4},{7,5},{8,10},{9,11},{10,... | collective-permute-start | bytes 2359304 | tf_op jit(solution)/shard_map/ppermute | solution.py:28
  225.0 30.4 %collective-permute-start.22 = (bf16[192,2048]{1,0:T(8,128)(2,1)}, bf16[192,2048]{1,0:T(8,128)(2,1)}, u32[]{:S(2)}, u32[]{:S(2)}) collective-permute-start(bf16[192,2048]{1,0:T(8,128)(2,1)} %collective-permute-done.18.x1), channel_id=1, source_target_pairs={{0,1},{1,0},{2,3},{3,2},{4,5},{5,4},{6,7},{7,6},{8,9},{9,8},{10,11... | collective-permute-start | bytes 2359304 | tf_op jit(solution)/shard_map/ppermute | solution.py:28
  226.4 35.6 %collective-permute-start.21 = (bf16[192,2048]{1,0:T(8,128)(2,1)S(1)}, bf16[192,2048]{1,0:T(8,128)(2,1)}, u32[]{:S(2)}, u32[]{:S(2)}) collective-permute-start(bf16[192,2048]{1,0:T(8,128)(2,1)S(1)} %collective-permute-done.12.x0), channel_id=1, source_target_pairs={{0,2},{1,3},{2,0},{3,1},{4,6},{5,7},{6,4},{7,5},{8,10},{9,11},{10,... | collective-permute-start | bytes 2359304 | tf_op jit(solution)/shard_map/ppermute | solution.py:28
  249.5 36.0 %collective-permute-start.13 = (bf16[192,2048]{1,0:T(8,128)(2,1)}, bf16[192,2048]{1,0:T(8,128)(2,1)S(1)}, u32[]{:S(2)}, u32[]{:S(2)}) collective-permute-start(bf16[192,2048]{1,0:T(8,128)(2,1)} %copy-done.75), channel_id=1, source_target_pairs={{0,1},{1,0},{2,3},{3,2},{4,5},{5,4},{6,7},{7,6},{8,9},{9,8},{10,11... | collective-permute-start | bytes 2359304 | tf_op jit(solution)/shard_map/ppermute | solution.py:28
  250.1 107.4 %collective-permute-start.29 = (bf16[192,2048]{1,0:T(8,128)(2,1)}, bf16[192,2048]{1,0:T(8,128)(2,1)}, u32[]{:S(2)}, u32[]{:S(2)}) collective-permute-start(bf16[192,2048]{1,0:T(8,128)(2,1)} %get-tuple-element.129), channel_id=1, source_target_pairs={{0,2},{1,3},{2,0},{3,1},{4,6},{5,7},{6,4},{7,5},{8,10},{9,11},{10,... | collective-permute-start | bytes 2359304 | tf_op jit(solution)/shard_map/ppermute | solution.py:28
  255.4 104.2 %collective-permute-start.35 = (bf16[192,2048]{1,0:T(8,128)(2,1)}, bf16[192,2048]{1,0:T(8,128)(2,1)}, u32[]{:S(2)}, u32[]{:S(2)}) collective-permute-start(bf16[192,2048]{1,0:T(8,128)(2,1)} %get-tuple-element.137), channel_id=1, source_target_pairs={{0,2},{1,3},{2,0},{3,1},{4,6},{5,7},{6,4},{7,5},{8,10},{9,11},{10,... | collective-permute-start | bytes 2359304 | tf_op jit(solution)/shard_map/ppermute | solution.py:28
  283.4 40.6 %collective-permute-start.25 = (bf16[192,2048]{1,0:T(8,128)(2,1)}, bf16[192,2048]{1,0:T(8,128)(2,1)}, u32[]{:S(2)}, u32[]{:S(2)}) collective-permute-start(bf16[192,2048]{1,0:T(8,128)(2,1)} %get-tuple-element.125), channel_id=1, source_target_pairs={{0,1},{1,0},{2,3},{3,2},{4,5},{5,4},{6,7},{7,6},{8,9},{9,8},{10,11... | collective-permute-start | bytes 2359304 | tf_op jit(solution)/shard_map/ppermute | solution.py:28
  285.0 36.2 %collective-permute-start.31 = (bf16[192,2048]{1,0:T(8,128)(2,1)}, bf16[192,2048]{1,0:T(8,128)(2,1)}, u32[]{:S(2)}, u32[]{:S(2)}) collective-permute-start(bf16[192,2048]{1,0:T(8,128)(2,1)} %get-tuple-element.133), channel_id=1, source_target_pairs={{0,1},{1,0},{2,3},{3,2},{4,5},{5,4},{6,7},{7,6},{8,9},{9,8},{10,11... | collective-permute-start | bytes 2359304 | tf_op jit(solution)/shard_map/ppermute | solution.py:28
  308.1 53.2 %collective-permute-start.16 = (bf16[192,2048]{1,0:T(8,128)(2,1)}, bf16[192,2048]{1,0:T(8,128)(2,1)}, u32[]{:S(2)}, u32[]{:S(2)}) collective-permute-start(bf16[192,2048]{1,0:T(8,128)(2,1)} %get-tuple-element.123), channel_id=1, source_target_pairs={{0,1},{1,0},{2,3},{3,2},{4,5},{5,4},{6,7},{7,6},{8,9},{9,8},{10,11... | collective-permute-start | bytes 2359304 | tf_op jit(solution)/shard_map/ppermute | solution.py:28
  321.1 18.4 %collective-permute-start.33 = (bf16[192,2048]{1,0:T(8,128)(2,1)}, bf16[192,2048]{1,0:T(8,128)(2,1)S(1)}, u32[]{:S(2)}, u32[]{:S(2)}) collective-permute-start(bf16[192,2048]{1,0:T(8,128)(2,1)} %get-tuple-element.136), channel_id=1, source_target_pairs={{0,2},{1,3},{2,0},{3,1},{4,6},{5,7},{6,4},{7,5},{8,10},{9,11},{10,... | collective-permute-start | bytes 2359304 | tf_op jit(solution)/shard_map/ppermute | solution.py:28
  324.0 32.4 %collective-permute-start.27 = (bf16[192,2048]{1,0:T(8,128)(2,1)S(1)}, bf16[192,2048]{1,0:T(8,128)(2,1)S(1)}, u32[]{:S(2)}, u32[]{:S(2)}) collective-permute-start(bf16[192,2048]{1,0:T(8,128)(2,1)S(1)} %copy-done.108), channel_id=1, source_target_pairs={{0,2},{1,3},{2,0},{3,1},{4,6},{5,7},{6,4},{7,5},{8,10},{9,11},{10,... | collective-permute-start | bytes 2359304 | tf_op jit(solution)/shard_map/ppermute | solution.py:28
  339.5 43.4 %collective-permute-start.30 = (bf16[192,2048]{1,0:T(8,128)(2,1)}, bf16[192,2048]{1,0:T(8,128)(2,1)}, u32[]{:S(2)}, u32[]{:S(2)}) collective-permute-start(bf16[192,2048]{1,0:T(8,128)(2,1)} %get-tuple-element.131), channel_id=1, source_target_pairs={{0,1},{1,0},{2,3},{3,2},{4,5},{5,4},{6,7},{7,6},{8,9},{9,8},{10,11... | collective-permute-start | bytes 2359304 | tf_op jit(solution)/shard_map/ppermute | solution.py:28
  356.4 26.6 %collective-permute-start.26 = (bf16[192,2048]{1,0:T(8,128)(2,1)}, bf16[192,2048]{1,0:T(8,128)(2,1)}, u32[]{:S(2)}, u32[]{:S(2)}) collective-permute-start(bf16[192,2048]{1,0:T(8,128)(2,1)} %add_convert_fusion.7), channel_id=1, source_target_pairs={{0,2},{1,3},{2,0},{3,1},{4,6},{5,7},{6,4},{7,5},{8,10},{9,11},{10,... | collective-permute-start | bytes 2359304 | tf_op jit(solution)/shard_map/ppermute | solution.py:28
  357.6 25.4 %collective-permute-start.32 = (bf16[192,2048]{1,0:T(8,128)(2,1)}, bf16[192,2048]{1,0:T(8,128)(2,1)}, u32[]{:S(2)}, u32[]{:S(2)}) collective-permute-start(bf16[192,2048]{1,0:T(8,128)(2,1)} %add_convert_fusion.3), channel_id=1, source_target_pairs={{0,2},{1,3},{2,0},{3,1},{4,6},{5,7},{6,4},{7,5},{8,10},{9,11},{10,... | collective-permute-start | bytes 2359304 | tf_op jit(solution)/shard_map/ppermute | solution.py:28
  359.6 23.4 %collective-permute-start.28 = (bf16[192,2048]{1,0:T(8,128)(2,1)}, bf16[192,2048]{1,0:T(8,128)(2,1)}, u32[]{:S(2)}, u32[]{:S(2)}) collective-permute-start(bf16[192,2048]{1,0:T(8,128)(2,1)} %add_convert_fusion.5), channel_id=1, source_target_pairs={{0,1},{1,0},{2,3},{3,2},{4,5},{5,4},{6,7},{7,6},{8,9},{9,8},{10,11... | collective-permute-start | bytes 2359304 | tf_op jit(solution)/shard_map/ppermute | solution.py:28
  361.4 21.6 %collective-permute-start.34 = (bf16[192,2048]{1,0:T(8,128)(2,1)}, bf16[192,2048]{1,0:T(8,128)(2,1)}, u32[]{:S(2)}, u32[]{:S(2)}) collective-permute-start(bf16[192,2048]{1,0:T(8,128)(2,1)} %add_convert_fusion.2), channel_id=1, source_target_pairs={{0,1},{1,0},{2,3},{3,2},{4,5},{5,4},{6,7},{7,6},{8,9},{9,8},{10,11... | collective-permute-start | bytes 2359304 | tf_op jit(solution)/shard_map/ppermute | solution.py:28
  399.2 18.7 %collective-permute-start.36 = (bf16[192,2048]{1,0:T(8,128)(2,1)}, bf16[192,2048]{1,0:T(8,128)(2,1)S(1)}, u32[]{:S(2)}, u32[]{:S(2)}) collective-permute-start(bf16[192,2048]{1,0:T(8,128)(2,1)} %get-tuple-element.215.refs_0_), channel_id=1, source_target_pairs={{0,1},{1,0},{2,3},{3,2},{4,5},{5,4},{6,7},{7,6},{8,9},{9,8},{10,11... | collective-permute-start | bytes 2359304 | tf_op jit(solution)/shard_map/ppermute | solution.py:28
  402.8 39.7 %collective-permute-start.40 = (bf16[192,2048]{1,0:T(8,128)(2,1)S(1)}, bf16[192,2048]{1,0:T(8,128)(2,1)S(1)}, u32[]{:S(2)}, u32[]{:S(2)}) collective-permute-start(bf16[192,2048]{1,0:T(8,128)(2,1)S(1)} %get-tuple-element.212.refs_1_), channel_id=1, source_target_pairs={{0,2},{1,3},{2,0},{3,1},{4,6},{5,7},{6,4},{7,5},{8,10},{9,11},{10,... | collective-permute-start | bytes 2359304 | tf_op jit(solution)/shard_map/ppermute | solution.py:28
  403.1 45.4 %collective-permute-start.39 = (bf16[192,2048]{1,0:T(8,128)(2,1)}, bf16[192,2048]{1,0:T(8,128)(2,1)S(1)}, u32[]{:S(2)}, u32[]{:S(2)}) collective-permute-start(bf16[192,2048]{1,0:T(8,128)(2,1)} %get-tuple-element.215.refs_0_), channel_id=1, source_target_pairs={{0,2},{1,3},{2,0},{3,1},{4,6},{5,7},{6,4},{7,5},{8,10},{9,11},{10,... | collective-permute-start | bytes 2359304 | tf_op jit(solution)/shard_map/ppermute | solution.py:28
  434.0 22.4 %collective-permute-start.41 = (bf16[192,2048]{1,0:T(8,128)(2,1)S(1)}, bf16[192,2048]{1,0:T(8,128)(2,1)S(1)}, u32[]{:S(2)}, u32[]{:S(2)}) collective-permute-start(bf16[192,2048]{1,0:T(8,128)(2,1)S(1)} %copy-done.15), channel_id=1, source_target_pairs={{0,2},{1,3},{2,0},{3,1},{4,6},{5,7},{6,4},{7,5},{8,10},{9,11},{10,... | collective-permute-start | bytes 2359304 | tf_op jit(solution)/shard_map/ppermute | solution.py:28
  466.6 207.3 %reduce-scatter.5.cloned.1.call-start = ((), (), s32[]{:S(2)}) async-start(), calls=%async_computation.4 | async-start | bytes 7077888 | tf_op jit(solution)/shard_map/reduce_scatter | solution.py:391
  513.0 163.2 %reduce-scatter.11.cloned.1.call-start = ((), (), s32[]{:S(2)}) async-start(), calls=%async_computation.7 | async-start | bytes 9437184 | tf_op jit(solution)/shard_map/reduce_scatter | solution.py:391
  539.0 225.8 %reduce-scatter.9.cloned.1.call-start = ((), (), s32[]{:S(2)}) async-start(), calls=%async_computation.6 | async-start | bytes 9437184 | tf_op jit(solution)/shard_map/reduce_scatter | solution.py:391
  578.5 19.6 %collective-permute-start.43 = (bf16[192,2048]{1,0:T(8,128)(2,1)}, bf16[192,2048]{1,0:T(8,128)(2,1)S(1)}, u32[]{:S(2)}, u32[]{:S(2)}) collective-permute-start(bf16[192,2048]{1,0:T(8,128)(2,1)} %get-tuple-element.173), channel_id=1, source_target_pairs={{0,1},{1,0},{2,3},{3,2},{4,5},{5,4},{6,7},{7,6},{8,9},{9,8},{10,11... | collective-permute-start | bytes 2359304 | tf_op jit(solution)/shard_map/ppermute | solution.py:28
  585.7 30.5 %collective-permute-start.38 = (bf16[192,2048]{1,0:T(8,128)(2,1)}, bf16[192,2048]{1,0:T(8,128)(2,1)S(1)}, u32[]{:S(2)}, u32[]{:S(2)}) collective-permute-start(bf16[192,2048]{1,0:T(8,128)(2,1)} %get-tuple-element.155), channel_id=1, source_target_pairs={{0,1},{1,0},{2,3},{3,2},{4,5},{5,4},{6,7},{7,6},{8,9},{9,8},{10,11... | collective-permute-start | bytes 2359304 | tf_op jit(solution)/shard_map/ppermute | solution.py:28
  597.0 19.2 %collective-permute-start.47 = (bf16[192,2048]{1,0:T(8,128)(2,1)}, bf16[192,2048]{1,0:T(8,128)(2,1)S(1)}, u32[]{:S(2)}, u32[]{:S(2)}) collective-permute-start(bf16[192,2048]{1,0:T(8,128)(2,1)} %get-tuple-element.177), channel_id=1, source_target_pairs={{0,2},{1,3},{2,0},{3,1},{4,6},{5,7},{6,4},{7,5},{8,10},{9,11},{10,... | collective-permute-start | bytes 2359304 | tf_op jit(solution)/shard_map/ppermute | solution.py:28
  600.4 19.3 %collective-permute-start.44 = (bf16[192,2048]{1,0:T(8,128)(2,1)}, bf16[192,2048]{1,0:T(8,128)(2,1)}, u32[]{:S(2)}, u32[]{:S(2)}) collective-permute-start(bf16[192,2048]{1,0:T(8,128)(2,1)} %add_convert_fusion.1), channel_id=1, source_target_pairs={{0,2},{1,3},{2,0},{3,1},{4,6},{5,7},{6,4},{7,5},{8,10},{9,11},{10,... | collective-permute-start | bytes 2359304 | tf_op jit(solution)/shard_map/ppermute | solution.py:28
  (120 other events, 910.9 us)
Sparse Core Ops, SparseCore 0:
  466.8 36.0 reduce-scatter.6
  513.2 70.0 reduce-scatter.4
  585.6 89.0 reduce-scatter.10
  676.8 87.9 reduce-scatter.8

commit v2 on v1

v2 whole, which is shorter than its diff:
```python
import functools
import math

import jax
import jax.numpy as jnp
from jax import lax
from jax.experimental import pallas as pl
from jax.experimental.pallas import tpu as pltpu
from jax.sharding import PartitionSpec as P

HEAD_DIM = 128
CLIP_MOST = 256
epsilon = 1e-05
masked_score = -1e30
bf16, f32 = jnp.bfloat16, jnp.float32
VMEM_LIMIT = 60 * 1024 * 1024
MESH = pl.DeviceIdType.MESH
COST = 20


def dot(a, b, ca, cb):
    return lax.dot_general(a, b, (((ca,), (cb,)), ((), ())), preferred_element_type=f32)


def shape(dims, kind=bf16):
    return jax.ShapeDtypeStruct(dims, kind)


def call(kernel, args, grid, in_specs, out_specs, outs, *, name, scalars=(), scratch=(), after=(), flops=0, moved=0, **extra):
    lead = len(scalars) + len(args)

    def body(*refs):
        kernel(*refs[:lead], *refs[lead + len(after) :])

    return pl.pallas_call(
        body,
        grid_spec=pltpu.PrefetchScalarGridSpec(
            num_scalar_prefetch=len(scalars),
            grid=grid,
            in_specs=[*in_specs, *[pl.BlockSpec(memory_space=pl.ANY)] * len(after)],
            out_specs=out_specs,
            scratch_shapes=list(scratch),
        ),
        out_shape=outs,
        compiler_params=pltpu.CompilerParams(vmem_limit_bytes=VMEM_LIMIT, **extra),
        cost_estimate=pl.CostEstimate(flops=flops // COST, bytes_accessed=moved // COST, transcendentals=0),
        name=name,
    )(*scalars, *args, *after)


class Group:
    def __init__(self, count):
        self.count = count

    def swap(self, value, r):
        return lax.ppermute(value, "mp", [(m, m ^ r) for m in range(self.count)])

    def gather(self, low, high):
        if self.count == 4:
            low_x, high_y = self.swap(low, 1), self.swap(high, 2)
            high_x, low_y = self.swap(high, 1), self.swap(low, 2)
            low_d, high_d = self.swap(low_x, 2), self.swap(high_y, 1)
            return [(low, high), (low_x, high_x), (low_y, high_y), (low_d, high_d)]
        me = lax.axis_index("mp")
        blocks = lax.all_gather(jnp.concatenate([low, high]), "mp")
        half = low.shape[0]
        out = []
        for r in range(self.count):
            block = lax.dynamic_index_in_dim(blocks, me ^ r, 0, keepdims=False)
            out.append((block[:half], block[half:]))
        return out

    def reduce(self, parts):
        if self.count == 4:
            got_x, got_y = self.swap(parts[3][0], 1), self.swap(parts[3][1], 2)
            early_x, early_y = self.swap(parts[1][0], 1), self.swap(parts[2][1], 2)
            late_x = self.swap(add_rows([parts[1][1], got_y]), 1)
            late_y = self.swap(add_rows([parts[2][0], got_x]), 2)
            return [(parts[0][0], early_x, late_y), (parts[0][1], late_x, early_y)]
        me = lax.axis_index("mp")
        blocks = jnp.stack([jnp.concatenate(p) for p in parts])
        blocks = jnp.take(blocks, jnp.arange(self.count) ^ me, axis=0)
        own = lax.psum_scatter(blocks, "mp", scatter_dimension=0, tiled=False)
        half = own.shape[0] // 2
        return [(own[:half],), (own[half:],)]


def add_rows(values, kind=bf16):
    rows, width = values[0].shape
    tile = rows // 2

    def kernel(*refs):
        out = refs[-1]
        sum_ = refs[0][...].astype(f32)
        for r in refs[1:-1]:
            sum_ = sum_ + r[...].astype(f32)
        out[...] = sum_.astype(out.dtype)

    spec = pl.BlockSpec((tile, width), lambda i: (i, 0))
    return call(
        kernel,
        values,
        (2,),
        [spec] * len(values),
        spec,
        shape((rows, width), kind),
        name="add_rows",
        flops=rows * width,
        moved=2 * rows * width * (len(values) + 1),
    )


def norm_parts(values):
    centred = values - jnp.mean(values, axis=-1, keepdims=True)
    spread = jnp.mean(centred * centred, axis=-1, keepdims=True)
    scale = lax.rsqrt(spread + epsilon)
    return centred * scale, scale


def norm_back(values, gain, grad):
    unit, scale = norm_parts(values)
    q = grad * gain
    back = scale * (
        q - jnp.mean(q, axis=-1, keepdims=True) - unit * jnp.mean(q * unit, axis=-1, keepdims=True)
    )
    return back, jnp.sum(grad * unit, axis=0, keepdims=True)


def row_stage(fn, ins, outs, *, name, after=(), steps=2):
    half, width = next((v[0].shape if k == "pair" else (v.shape[0] // 2, v.shape[1])) for k, v in ins if k != "vec")
    tile = half // steps
    low_map, high_map = (lambda i: (jnp.minimum(i, steps - 1), 0)), (lambda i: (jnp.maximum(i - steps, 0), 0))

    def specs(kind):
        if kind == "pair":
            return [pl.BlockSpec((tile, width), low_map), pl.BlockSpec((tile, width), high_map)]
        if kind == "whole":
            return [pl.BlockSpec((tile, width), lambda i: (i, 0))]
        return [pl.BlockSpec((1, width), lambda i: (0, 0))]

    def side_of(kinds, refs, side):
        out, at = [], 0
        for kind in kinds:
            out.append(refs[at + (side if kind == "pair" else 0)])
            at += 2 if kind == "pair" else 1
        return out

    in_kinds, out_kinds = [k for k, _ in ins], [k for k, _ in outs]
    n_in = sum(2 if k == "pair" else 1 for k in in_kinds)

    def kernel(*refs):
        i = pl.program_id(0)

        def run(side):
            values = fn(*[r[...] for r in side_of(in_kinds, refs[:n_in], side)])
            for kind, ref, value in zip(out_kinds, side_of(out_kinds, refs[n_in:], side), values):
                if kind == "vec":

                    @pl.when(i == 0)
                    def _():
                        ref[...] = value

                    @pl.when(i > 0)
                    def _():
                        ref[...] += value
                else:
                    ref[...] = value.astype(ref.dtype)

        pl.when(i < steps)(lambda: run(0))
        pl.when(i >= steps)(lambda: run(1))

    args, in_specs, out_specs, out_shapes = [], [], [], []
    for kind, value in ins:
        args += list(value) if kind == "pair" else [value]
        in_specs += specs(kind)
    for kind, dtype in outs:
        out_specs += specs(kind)
        out_shapes += {
            "pair": [shape((half, width), dtype)] * 2,
            "whole": [shape((2 * half, width), dtype)],
            "vec": [shape((1, width), dtype)],
        }[kind]
    got = call(
        kernel,
        args,
        (2 * steps,),
        in_specs,
        out_specs,
        out_shapes,
        name=name,
        after=after,
        flops=20 * half * width,
        moved=8 * half * width * (len(ins) + len(outs)),
    )
    out, at = [], 0
    for kind in out_kinds:
        out.append((got[at], got[at + 1]) if kind == "pair" else got[at])
        at += 2 if kind == "pair" else 1
    return out


def terms(rows):
    return [("pair", (low, high)) for low, high in zip(*rows)]


def total(values):
    out = values[0].astype(f32)
    for v in values[1:]:
        out = out + v.astype(f32)
    return out


def mm(blocks, w, *, trans=False, tile=512, scale=None, name="mm", after=()):
    xs = [half for block in blocks for half in block]
    depth = xs[0].shape[1]
    width = w.shape[0] if trans else w.shape[1]
    tile = min(tile, width)
    sizes = [x.shape[0] for x in xs]
    n = len(xs)

    def kernel(*refs):
        outs = refs[-n:]
        x = jnp.concatenate([r[...] for r in refs[:n]], axis=0)
        acc = dot(x, refs[n][...], 1, 1 if trans else 0)
        if scale is not None:
            acc = acc * refs[n + 1][...]
        at = 0
        for o in outs:
            o[...] = acc[at : at + o.shape[0]].astype(o.dtype)
            at += o.shape[0]

    in_specs = [pl.BlockSpec((s, depth), lambda j: (0, 0)) for s in sizes]
    in_specs.append(
        pl.BlockSpec((tile, depth), lambda j: (j, 0)) if trans else pl.BlockSpec((depth, tile), lambda j: (0, j))
    )
    args = [*xs, w]
    if scale is not None:
        in_specs.append(pl.BlockSpec((1, tile), lambda j: (0, j)))
        args.append(scale)
    rows = sum(sizes)
    got = call(
        kernel,
        args,
        (width // tile,),
        in_specs,
        [pl.BlockSpec((s, tile), lambda j: (0, j)) for s in sizes],
        [shape((s, width)) for s in sizes],
        name=name,
        after=after,
        flops=2 * rows * depth * width,
        moved=2 * (rows * depth + depth * width + rows * width),
    )
    return pairs(got)


def pairs(refs):
    return [(refs[i], refs[i + 1]) for i in range(0, len(refs), 2)]


def gelu_both(u):
    c = math.sqrt(2.0 / math.pi)
    square = u * u
    t = jnp.tanh(c * (u + 0.044715 * (u * square)))
    half = 0.5 * (1.0 + t)
    value = u * half
    slope = half + (0.5 * c) * u * (1.0 - t * t) * (1.0 + (3 * 0.044715) * square)
    return value, slope


def feed_kernel(tiles, x0, x1, c0, c1, up, down, hid, pre, y0, y1, g0, g1, acc_y, acc_g):
    j = pl.program_id(0)
    x = jnp.concatenate([x0[...], x1[...]], axis=0)
    c = jnp.concatenate([c0[...], c1[...]], axis=0)
    value, slope = gelu_both(dot(x, up[...], 1, 0))
    value = value.astype(bf16)
    hid[...] = value
    grad = (dot(c, down[...], 1, 1) * slope).astype(bf16)
    pre[...] = grad
    y = dot(value, down[...], 1, 0)
    g = dot(grad, up[...], 1, 1)

    @pl.when(j == 0)
    def _():
        acc_y[...] = y
        acc_g[...] = g

    @pl.when((j > 0) & (j < tiles - 1))
    def _():
        acc_y[...] += y
        acc_g[...] += g

    @pl.when(j == tiles - 1)
    def _():
        half = x0.shape[0]
        last_y, last_g = acc_y[...] + y, acc_g[...] + g
        y0[...] = last_y[:half].astype(bf16)
        y1[...] = last_y[half:].astype(bf16)
        g0[...] = last_g[:half].astype(bf16)
        g1[...] = last_g[half:].astype(bf16)


def feed_block(x, c, up, down, tile=512, after=()):
    half, width = x[0].shape
    units = up.shape[1]
    rows = 2 * half
    tiles = units // tile
    whole = pl.BlockSpec((half, width), lambda j: (0, 0))
    part = pl.BlockSpec((rows, tile), lambda j: (0, j))
    small, big = shape((half, width)), shape((rows, units))
    hid, pre, y0, y1, g0, g1 = call(
        functools.partial(feed_kernel, tiles),
        [*x, *c, up, down],
        (tiles,),
        [
            whole,
            whole,
            whole,
            whole,
            pl.BlockSpec((width, tile), lambda j: (0, j)),
            pl.BlockSpec((tile, width), lambda j: (j, 0)),
        ],
        [part, part, whole, whole, whole, whole],
        [big, big, small, small, small, small],
        scratch=[pltpu.VMEM((rows, width), f32), pltpu.VMEM((rows, width), f32)],
        name="feed_block",
        after=after,
        flops=8 * rows * width * units,
        moved=4 * (2 * rows * width + width * units + rows * units),
    )
    return hid, pre, (y0, y1), (g0, g1)


def load_blocks(order, blocks, target):
    rows = blocks[0][0].shape[0] * 2
    for r, (low, high) in enumerate(blocks):
        at = pl.multiple_of((order[0] ^ r) * rows, rows)
        target[pl.ds(at, rows // 2), :] = low[...]
        target[pl.ds(at + rows // 2, rows // 2), :] = high[...]


def store_blocks(order, source, blocks, column=None):
    rows = blocks[0][0].shape[0] * 2
    for r, block in enumerate(blocks):
        at = pl.multiple_of((order[0] ^ r) * rows, rows)
        for i, ref in enumerate(block):
            value = source[pl.ds(at + i * (rows // 2), rows // 2), :].astype(ref.dtype)
            if column is None:
                ref[...] = value
            else:
                ref[:, pl.ds(column, HEAD_DIM)] = value


def allowed_of(seg_col, seg_row, q0, k0, k1, rows):
    same = seg_col[q0 : q0 + rows, :] == seg_row[:, k0:k1]
    dims = (rows, k1 - k0)
    i = lax.broadcasted_iota(jnp.int32, dims, 0) + q0
    j = lax.broadcasted_iota(jnp.int32, dims, 1) + k0
    return same & (j <= i)


def attend_kernel(nb, order, seg_col, seg_row, *refs):
    q_in, k_in, v_in = (pairs(refs[i * 2 * nb : (i + 1) * 2 * nb]) for i in range(3))
    out = pairs(refs[6 * nb : 8 * nb])
    q, k, v, o = refs[8 * nb :]
    load_blocks(order, q_in, q)
    load_blocks(order, k_in, k)
    load_blocks(order, v_in, v)
    step = CLIP_MOST
    for q0 in range(0, q.shape[0], step):
        k0, k1 = max(0, q0 - step), q0 + step
        s = dot(q[q0:k1, :], k[k0:k1, :], 1, 1)
        s = jnp.where(allowed_of(seg_col, seg_row, q0, k0, k1, step), s, masked_score)
        e = jnp.exp(s - jnp.max(s, axis=-1, keepdims=True))
        p = (e * (1.0 / jnp.sum(e, axis=-1, keepdims=True))).astype(bf16)
        o[q0:k1, :] = dot(p, v[k0:k1, :], 1, 0)
    store_blocks(order, o, out)


def attend_specs(blocks, heads, seg):
    half = blocks[0][0].shape[0]
    length = seg.shape[0]
    specs = [pl.BlockSpec((length, 1), lambda h, o: (0, 0)), pl.BlockSpec((1, length), lambda h, o: (0, 0))]
    args = [seg.reshape(length, 1), seg.reshape(1, length)]
    for which in range(3):
        for block in blocks:
            for value in block:
                specs.append(pl.BlockSpec((half, HEAD_DIM), lambda h, o, w=which: (0, w * heads + h)))
                args.append(value)
    return specs, args


def attend(order, seg, blocks, after=()):
    nb = len(blocks)
    half = blocks[0][0].shape[0]
    heads = blocks[0][0].shape[1] // (3 * HEAD_DIM)
    length = seg.shape[0]
    specs, args = attend_specs(blocks, heads, seg)
    outs = call(
        functools.partial(attend_kernel, nb),
        args,
        (heads,),
        specs,
        [pl.BlockSpec((half, HEAD_DIM), lambda h, o: (0, h))] * (2 * nb),
        [shape((half, heads * HEAD_DIM))] * (2 * nb),
        scalars=[order],
        scratch=[pltpu.VMEM((length, HEAD_DIM), bf16)] * 3 + [pltpu.VMEM((length, HEAD_DIM), f32)],
        name="attend",
        after=after,
        flops=4 * heads * length * 512 * HEAD_DIM,
        moved=8 * heads * length * HEAD_DIM,
    )
    return pairs(outs)


def attend_back_kernel(nb, heads, scale, order, seg_col, seg_row, *refs):
    q_in, k_in, v_in, c_in = (pairs(refs[i * 2 * nb : (i + 1) * 2 * nb]) for i in range(4))
    out = pairs(refs[8 * nb : 10 * nb])
    q, k, v, c, dq, dk, dv = refs[10 * nb :]
    load_blocks(order, q_in, q)
    load_blocks(order, k_in, k)
    load_blocks(order, v_in, v)
    load_blocks(order, c_in, c)
    step = CLIP_MOST
    for q0 in range(0, q.shape[0], step):
        k0, k1 = max(0, q0 - step), q0 + step
        qb, cb, kb, vb = q[q0:k1, :], c[q0:k1, :], k[k0:k1, :], v[k0:k1, :]
        s = dot(qb, kb, 1, 1)
        s = jnp.where(allowed_of(seg_col, seg_row, q0, k0, k1, step), s, masked_score)
        e = jnp.exp(s - jnp.max(s, axis=-1, keepdims=True))
        p = e * (1.0 / jnp.sum(e, axis=-1, keepdims=True))
        dp = dot(cb, vb, 1, 1)
        inner = jnp.sum(p * dp, axis=-1, keepdims=True)
        ds = (p * (dp - inner)).astype(bf16)
        dq[q0:k1, :] = dot(ds, kb, 1, 0) * scale
        dkb = dot(ds, qb, 0, 0)
        dvb = dot(p.astype(bf16), cb, 0, 0)
        if q0 > 0:
            dk[k0:q0, :] += dkb[:step]
            dv[k0:q0, :] += dvb[:step]
            dkb, dvb = dkb[step:], dvb[step:]
        dk[q0:k1, :] = dkb
        dv[q0:k1, :] = dvb
    column = pl.multiple_of(pl.program_id(0) * HEAD_DIM, HEAD_DIM)
    for which, source in enumerate((dq, dk, dv)):
        store_blocks(order, source, out, column + which * heads * HEAD_DIM)


def attend_back(order, seg, blocks, grads, scale, after=()):
    nb = len(blocks)
    half, width = blocks[0][0].shape
    heads = width // (3 * HEAD_DIM)
    length = seg.shape[0]
    specs, args = attend_specs(blocks, heads, seg)
    for low, high in grads:
        specs += [pl.BlockSpec((half, HEAD_DIM), lambda h, o: (0, h))] * 2
        args += [low, high]
    outs = call(
        functools.partial(attend_back_kernel, nb, heads, scale),
        args,
        (heads,),
        specs,
        [pl.BlockSpec((half, width), lambda h, o: (0, 0))] * (2 * nb),
        [shape((half, width))] * (2 * nb),
        scalars=[order],
        scratch=[pltpu.VMEM((length, HEAD_DIM), bf16)] * 4 + [pltpu.VMEM((length, HEAD_DIM), f32)] * 3,
        name="attend_back",
        after=after,
        flops=10 * heads * length * 512 * HEAD_DIM,
        moved=14 * heads * length * HEAD_DIM,
    )
    return pairs(outs)


class Shares:
    def __init__(self, count):
        self.count = count
        self.split = count == 8
        me = lax.axis_index("dp")
        self.core, self.z = (me % 2).astype(jnp.int32), (me // 2).astype(jnp.int32)

    def product(self, lefts, rights, by_left, which=None, plus=None, after=(), name="weight_grad"):
        rows, right_rows = [l.shape[0] for l in lefts], [r.shape[0] for r in rights]
        depth, width = lefts[0].shape[1], rights[0].shape[1]
        n, count = len(rows), self.count
        both = n + len(rights)
        stack = count // 2 if which is not None else count
        left_tile = depth // count if by_left else min(512, depth)
        right_tile = width if by_left else width // count
        dims = (stack, left_tile if by_left else depth, right_tile)
        scalars = [which.reshape(1)] if which is not None else []
        share = (lambda s, w: 2 * s + w[0][0]) if which is not None else (lambda s, w: s)
        if by_left:
            grid = (stack,)
            left_map = lambda s, *w: (0, share(s, w))
            right_map = lambda s, *w: (0, 0)
            out_spec = pl.BlockSpec((1, left_tile, right_tile), lambda s, *w: (s, 0, 0))
            scratch = []
        else:
            grid = (depth // left_tile, stack)
            left_map = lambda i, s, *w: (0, i)
            right_map = lambda i, s, *w: (0, share(s, w))
            out_spec = pl.BlockSpec((1, left_tile, right_tile), lambda i, s, *w: (s, i, 0))
            scratch = [pltpu.VMEM((left_tile, sum(rows)), bf16)]

        def kernel(*refs):
            refs = refs[len(scalars) :]
            ls, rs = refs[:n], refs[n:both]
            out = refs[both + (plus is not None)]
            right = jnp.concatenate([r[...] for r in rs], axis=0)
            if by_left:
                left = jnp.concatenate([l[...] for l in ls], axis=0)
                acc = dot(left, right, 0, 0)
            else:
                turned = refs[-1]

                @pl.when(pl.program_id(1) == 0)
                def _():
                    at = 0
                    for l in ls:
                        turned[:, at : at + l.shape[0]] = l[...].T
                        at += l.shape[0]

                acc = dot(turned[...], right, 1, 0)
            if plus is not None:
                acc = acc + refs[both][0].astype(f32)
            out[0] = acc.astype(bf16)

        return call(
            kernel,
            [*lefts, *rights, *([plus] if plus is not None else [])],
            grid,
            [pl.BlockSpec((r, left_tile), left_map) for r in rows]
            + [pl.BlockSpec((r, right_tile), right_map) for r in right_rows]
            + ([out_spec] if plus is not None else []),
            out_spec,
            shape(dims),
            scalars=scalars,
            scratch=scratch,
            name=name,
            after=after,
            flops=2 * sum(rows) * depth * width * stack // count,
            moved=2 * (sum(rows) * (depth + width) + depth * width),
        )

    def send(self, value, moves):
        return lax.ppermute(value, "dp", moves)

    def first(self, lefts, rights, by_left, after=(), name="weight_grad"):
        if not self.split:
            return None
        other = self.product(lefts, rights, by_left, 1 - self.core, after=after, name=name)
        return self.send(other, [(d, d ^ 1) for d in range(8)])

    def second(self, lefts, rights, by_left, got, after=(), name="weight_grad"):
        if not self.split:
            return self.product(lefts, rights, by_left, after=after, name=name)
        return self.product(lefts, rights, by_left, self.core, plus=got, after=after, name=name)

    def along(self, step, sources):
        return [(2 * z + c, 2 * (z + step) + c) for z in sources for c in range(2)]

    def line(self, mine, columns):
        if not self.split:
            summed = lax.psum_scatter(mine, "dp", scatter_dimension=0, tiled=False)
            return share_sum(summed[None], jnp.zeros((1,), jnp.int32), [], f32, columns)
        z = self.z
        right = self.send(mine[3], self.along(1, [0]))
        left = self.send(mine[0], self.along(-1, [3]))
        pick = lambda at: jnp.clip(at, 0, 3).reshape(1)
        right = self.send(share_sum(mine, pick(z + 2), [right], bf16), self.along(1, [0, 1]))
        left = self.send(share_sum(mine, pick(z - 2), [left], bf16), self.along(-1, [3, 2]))
        right = self.send(share_sum(mine, pick(z + 1), [right], bf16), self.along(1, [0, 1, 2]))
        left = self.send(share_sum(mine, pick(z - 1), [left], bf16), self.along(-1, [3, 2, 1]))
        return share_sum(mine, z.reshape(1), [right, left], f32, columns)


def share_sum(stack, at, others, kind, columns=None):
    _, rows, width = stack.shape
    tile = rows // 2 if rows % 32 == 0 else rows
    cuts = columns or [width]

    def kernel(_, own, *refs):
        value = own[0].astype(f32)
        for r in refs[: len(others)]:
            value = value + r[...].astype(f32)
        at = 0
        for out in refs[len(others) :]:
            out[...] = value[:, at : at + out.shape[1]].astype(out.dtype)
            at += out.shape[1]

    spec = pl.BlockSpec((tile, width), lambda i, a: (i, 0))
    got = call(
        kernel,
        [stack, *others],
        (rows // tile,),
        [pl.BlockSpec((1, tile, width), lambda i, a: (a[0], i, 0))] + [spec] * len(others),
        [pl.BlockSpec((tile, c), lambda i, a: (i, 0)) for c in cuts],
        [shape((rows, c), kind) for c in cuts],
        scalars=[at],
        name="share_sum",
        flops=rows * width,
        moved=rows * width * 6,
    )
    return got if columns else got[0]


def everyone_kernel(mp, dp, x, out, near, far, sum_, send_near, recv_near, send_far, recv_far):
    m, d = lax.axis_index("mp"), lax.axis_index("dp")
    barrier = pltpu.get_barrier_semaphore()
    for r in range(1, mp):
        pl.semaphore_signal(barrier, inc=1, device_id={"mp": lax.rem(m + r, mp)}, device_id_type=MESH)
    for r in range(1, dp):
        pl.semaphore_signal(barrier, inc=1, device_id={"dp": lax.rem(d + r, dp)}, device_id_type=MESH)
    pl.semaphore_wait(barrier, mp + dp - 2)

    def exchange(source, slots, me, count, axis, send, recv):
        copies = []
        for r in range(1, count):
            copy = pltpu.make_async_remote_copy(
                src_ref=source,
                dst_ref=slots.at[me],
                send_sem=send.at[r],
                recv_sem=recv.at[r],
                device_id={axis: lax.rem(me + r, count)},
                device_id_type=MESH,
            )
            copy.start()
            copies.append(copy)
        slots[pl.ds(me, 1)] = source[...][None]
        for copy in copies:
            copy.wait()
        value = slots[0]
        for r in range(1, count):
            value = value + slots[r]
        return value

    sum_[...] = exchange(x, near, m, mp, "mp", send_near, recv_near)
    out[...] = exchange(sum_, far, d, dp, "dp", send_far, recv_far)


def everyone(x, mp, dp):
    vmem = pl.BlockSpec(memory_space=pltpu.VMEM)
    return pl.pallas_call(
        functools.partial(everyone_kernel, mp, dp),
        in_specs=[vmem],
        out_specs=vmem,
        out_shape=jax.ShapeDtypeStruct(x.shape, f32),
        scratch_shapes=[
            pltpu.VMEM((mp, *x.shape), f32),
            pltpu.VMEM((dp, *x.shape), f32),
            pltpu.VMEM(x.shape, f32),
            pltpu.SemaphoreType.DMA((mp,)),
            pltpu.SemaphoreType.DMA((mp,)),
            pltpu.SemaphoreType.DMA((dp,)),
            pltpu.SemaphoreType.DMA((dp,)),
        ],
        compiler_params=pltpu.CompilerParams(collective_id=0, has_side_effects=True),
        name="everyone",
    )(x)


def halves_of(blocks):
    return [half for block in blocks for half in block]


def local(
    mp,
    dp,
    tokens,
    segment_ids,
    query_weight,
    key_weight,
    value_weight,
    out_weight,
    up_weight,
    down_weight,
    attn_gain,
    mlp_gain,
    out_cotangent,
):
    group, shares = Group(mp), Shares(dp)
    seq_count, length = segment_ids.shape
    per_seq = mp // seq_count
    score_scale = 1.0 / math.sqrt(HEAD_DIM)
    me = lax.axis_index("mp")
    order = (me % per_seq).astype(jnp.int32).reshape(1)
    half, width = tokens.shape[0] // 2, tokens.shape[1]
    columns = query_weight.shape[1]
    attn_gain, mlp_gain = attn_gain.reshape(1, width), mlp_gain.reshape(1, width)
    segs = [
        lax.dynamic_index_in_dim(segment_ids, (me // per_seq) ^ s, 0, keepdims=False)
        for s in range(seq_count)
    ]

    def seq(s):
        return slice(s * per_seq, (s + 1) * per_seq)

    (normed,) = row_stage(
        lambda v, g: (norm_parts(v.astype(f32))[0] * g,),
        [("whole", tokens), ("vec", attn_gain)],
        [("pair", bf16)],
        name="norm_first",
    )
    attn_in = group.gather(*normed)
    cot = group.gather(out_cotangent[:half], out_cotangent[half:])
    parts = lax.optimization_barrier((query_weight, key_weight, value_weight, normed[0]))
    qkv_weight = jnp.concatenate(parts[:3], axis=1)
    qkv_scale = jnp.concatenate(
        [jnp.full((1, columns), score_scale, f32), jnp.ones((1, 2 * columns), f32)], axis=1
    )
    project = functools.partial(mm, w=qkv_weight, scale=qkv_scale, name="qkv")
    last = mp - 1
    qkv = project(attn_in[:1])
    qkv += project(attn_in[1:last], after=[qkv[0][0]])
    context = []
    if seq_count > 1:
        context += attend(order, segs[0], qkv[seq(0)])
        qkv += project(attn_in[last:], after=[context[0][0]])
    else:
        qkv += project(attn_in[last:])
    for s in range(len(context) // per_seq, seq_count):
        context += attend(order, segs[s], qkv[seq(s)])
    part_d = mm(context[last:], out_weight, tile=1024, name="out_proj")
    part_rest = mm(context[:last], out_weight, name="out_proj", after=[part_d[0][0]])
    attn_rows = group.reduce(part_rest + part_d)

    residual_mid, normed_mid = row_stage(
        lambda v, g, *t: (lambda r: (r, norm_parts(r)[0] * g))(v.astype(f32) + total(t)),
        [("whole", tokens), ("vec", mlp_gain), *terms(attn_rows)],
        [("whole", f32), ("pair", bf16)],
        name="norm_second",
    )
    mlp_in = group.gather(*normed_mid)
    fed = []
    for r in range(mp):
        fed.append(feed_block(mlp_in[r], cot[r], up_weight, down_weight, after=[f[0] for f in fed[-1:]]))
    mid_rows = group.reduce([f[3] for f in fed])
    hidden, pre_grad = [f[0] for f in fed], [f[1] for f in fed]
    cot_halves, mlp_halves = halves_of(cot), halves_of(mlp_in)
    down_args = (hidden, cot_halves, False)
    down_got = shares.first(*down_args, name="down_grad")
    down_mine = shares.second(*down_args, down_got, name="down_grad")
    down_grad = shares.line(down_mine, [width // dp])[0]

    mlp_rows = group.reduce([f[2] for f in fed])
    middle, middle_low, mlp_gain_grad = row_stage(
        lambda r, g, c, *t: (lambda b: (c.astype(f32) + b[0], c.astype(f32) + b[0], b[1]))(norm_back(r, g, total(t))),
        [("whole", residual_mid), ("vec", mlp_gain), ("whole", out_cotangent), *terms(mid_rows)],
        [("whole", f32), ("pair", bf16), ("vec", f32)],
        name="norm_second_back",
        after=[down_mine],
    )
    middle_all = group.gather(*middle_low)
    up_args = (mlp_halves, pre_grad, True)
    up_got = shares.first(*up_args, after=[middle_low[0]], name="up_grad")
    up_mine = shares.second(*up_args, up_got, name="up_grad")
    up_grad = shares.line(up_mine, [up_weight.shape[1]])[0]
    (layer_output,) = row_stage(
        lambda r, *t: (r + total(t),),
        [("whole", residual_mid), *terms(mlp_rows)],
        [("whole", bf16)],
        name="output",
        after=[up_mine],
    )

    back = functools.partial(mm, w=out_weight, trans=True, name="context_grad")
    context_grad = back(middle_all[:1], after=[up_mine])
    context_grad += back(middle_all[1:last], after=[context_grad[0][0]])
    qkv_grad = []
    for s in range(seq_count):
        if s == seq_count - 1:
            context_grad += back(middle_all[last:], after=[g[0] for g in qkv_grad[:1]])
        qkv_grad += attend_back(order, segs[s], qkv[seq(s)], context_grad[seq(s)], score_scale)
    part_d = mm(qkv_grad[last:], qkv_weight, trans=True, tile=1024, name="qkv_back")
    qkv_args = (halves_of(attn_in), halves_of(qkv_grad), True)
    qkv_got = shares.first(*qkv_args, after=[part_d[0][0]], name="qkv_grad")
    part_rest = mm(qkv_grad[:last], qkv_weight, trans=True, name="qkv_back", after=[qkv_got] if qkv_got is not None else [])
    qkv_mine = shares.second(*qkv_args, qkv_got, name="qkv_grad", after=[part_rest[0][0]])
    attn_back_rows = group.reduce(part_rest + part_d)
    out_args = (halves_of(context), halves_of(middle_all), False)
    out_got = shares.first(*out_args, after=[qkv_mine], name="out_grad")
    out_mine = shares.second(*out_args, out_got, name="out_grad")
    qkv_weight_grads = shares.line(qkv_mine, [columns] * 3)
    out_grad = shares.line(out_mine, [width // dp])[0]

    tokens_grad, attn_gain_grad = row_stage(
        lambda v, m, g, *t: (lambda b: (m + b[0], b[1]))(norm_back(v.astype(f32), g, total(t))),
        [("whole", tokens), ("whole", middle), ("vec", attn_gain), *terms(attn_back_rows)],
        [("whole", f32), ("vec", f32)],
        name="norm_first_back",
    )
    gains = jnp.concatenate([attn_gain_grad, mlp_gain_grad], axis=0).reshape(8, width // 4)
    gains = everyone(gains, mp, dp).reshape(2, width)
    return (layer_output, tokens_grad, *qkv_weight_grads, out_grad, up_grad, down_grad, gains[0], gains[1])


def solution(mesh):
    return jax.shard_map(
        functools.partial(local, mesh.shape["mp"], mesh.shape["dp"]),
        mesh=mesh,
        in_specs=(
            P(("dp", "mp"), None),
            P("dp", None),
            P(None, "mp"),
            P(None, "mp"),
            P(None, "mp"),
            P("mp", None),
            P(None, "mp"),
            P("mp", None),
            P(),
            P(),
            P(("dp", "mp"), None),
        ),
        out_specs=(
            P(("dp", "mp"), None),
            P(("dp", "mp"), None),
            P("dp", "mp"),
            P("dp", "mp"),
            P("dp", "mp"),
            P("mp", "dp"),
            P("dp", "mp"),
            P("mp", "dp"),
            P(),
            P(),
        ),
        check_vma=False,
    )
```

time: 779 us -> 777 us (level)
  Pallas kernels: 211 us -> 396 us
  starting transfers between devices: 53 us -> 143 us
  other arithmetic: 68.1 us -> 0.02 us
  matrix products: 57.1 us -> 0 us
  local copies, waits for them, and re-layouts: 88 us -> 35.8 us
  waiting for transfers between devices: 241 us -> 190 us
  blocking collectives: 41.6 us -> 0 us
  between operations: 14.9 us -> 1.55 us
    pallas_call x24 -> x60, Pallas kernels: 211 us -> 396 us  [the longest x59 383 us: call(): pl.pallas_call(body, grid_spec=pltpu.PrefetchScalarGridSpec(num_scalar_pr...]
    ppermute x0 -> x28, starting transfers between devices: none -> 96.1 us  [send(): return lax.ppermute(value, 'dp', moves)]
    reduce_scatter x4 -> x0, waiting for transfers between devices: 85.8 us -> none  [scatter_sum(): lax.psum_scatter(value, 'dp', scatter_dimension=dim, tiled=True).astype(f32)]
    dot_general x4 -> x0, matrix products: 57.1 us -> none  [weight_grad(): lax.dot_general(left, right, (((0,), (0,)), ((), ())), preferred_element_...]
    unnamed x285 -> x99, local copies, waits for them, and re-layouts: 74.2 us -> 21.1 us
    psum x1 -> x0, blocking collectives: 41.6 us -> none  [local(): lax.psum((attn_gain_grad, mlp_gain_grad), ('dp', 'mp'))]
    convert_element_type x11 -> x0, other arithmetic: 23.7 us -> none  [the longest x8 16.4 us: add(): return (a.astype(f32) + b.astype(f32)).astype(bf16)]
    ppermute x48, waiting for transfers between devices: 155 us -> 176 us  [swap(): return lax.ppermute(value, 'mp', [(m, m ^ r) for m in range(self.count)])]
  transfers between devices with their start and end apart: 52 -> 76, of which waited for: 18 -> 22; matrix products, arithmetic and copies ran while one was open for 22% -> 3% of each run, Pallas kernels for 27% -> 40%
where the time goes in v2:
time: 777 us; the launch traced here: 766 us
  Pallas kernels  396 us (51%)
  waiting for transfers between devices  190 us (24%)
  starting transfers between devices  143 us (18%)
  local copies, waits for them, and re-layouts  35.8 us (5%)
    pallas_call x59, Pallas kernels, call(): pl.pallas_call(body, grid_spec=pltpu.PrefetchScalarGridSpec(num_scalar_pr...  383 us
    ppermute x48, waiting for transfers between devices, swap(): return lax.ppermute(value, 'mp', [(m, m ^ r) for m in range(self.count)])  176 us
    ppermute x28, starting transfers between devices, send(): return lax.ppermute(value, 'dp', moves)  96.1 us
    ppermute x48, starting transfers between devices, swap(): return lax.ppermute(value, 'mp', [(m, m ^ r) for m in range(self.count)])  46.6 us
    unnamed x99, local copies, waits for them, and re-layouts  21.1 us
  transfers between devices with their start and end apart: 76, of which 22 were waited for; matrix products, arithmetic and copies ran while one was open for 3% of the time, Pallas kernels for 40%

profile of v2, /device:TPU:0, one launch (start us, length us, event | category | flops | bytes accessed | tf_op | source)
XLA Modules:
  0.0 766.2 jit_solution(6047392253717666094)
XLA Ops:
  12.7 13.8 %collective-permute-done.refs_0_.refs_3_ = bf16[192,2048]{1,0:T(8,128)(2,1)S(1)} collective-permute-done((bf16[192,2048]{1,0:T(8,128)(2,1)}, bf16[192,2048]{1,0:T(8,128)(2,1)S(1)}, u32[]{:S(2)}, u32[]{:S(2)}) %collective-permute-start) | collective-permute-done | bytes 786464 | tf_op jit(solution)/shard_map/ppermute | solution.py:56
  36.2 6.4 qkv.3
  46.4 8.7 %qkv.4 = (bf16[192,1536]{1,0:T(8,128)(2,1)}, bf16[192,1536]{1,0:T(8,128)(2,1)}, bf16[192,1536]{1,0:T(8,128)(2,1)}, bf16[192,1536]{1,0:T(8,128)(2,1)}) custom-call(bf16[192,2048]{1,0:T(8,128)(2,1)} %copy-done.9, bf16[192,2048]{1,0:T(8,128)(2,1)} %copy-done.11, bf16[192,2048]{1,0:T(8,128)(2,1)} %copy-done.12, bf16[192,2048]{1,0:T(8,128)(2,1)} %copy-done.10, ...), custom_call_target="tpu_custom_call" | custom-call | flops 241591904 | bytes 589824 | tf_op jit(solution)/shard_map/qkv/pallas_call | solution.py:35
  55.1 8.2 %attend.2 = (bf16[192,512]{1,0:T(8,128)(2,1)}, bf16[192,512]{1,0:T(8,128)(2,1)}, bf16[192,512]{1,0:T(8,128)(2,1)}, bf16[192,512]{1,0:T(8,128)(2,1)}) custom-call(s32[1]{0:T(128)} %bitcast.1.refs_0_, s32[768,1]{1,0:T(8,128)} %copy.21.refs_1_, s32[1,768]{1,0:T(1,128)} %copy-done.43, bf16[192,1536]{1,0:T(8,128)(2,1)} %get-tuple-element.104.refs_6_.refs_3_.refs_7_.refs_11_, ...), custom_call_target="tpu_custom_call" | custom-call | flops 40265320 | bytes 157286 | tf_op jit(solution)/shard_map/attend/pallas_call | solution.py:35
  63.3 6.4 qkv.5
  69.8 8.3 %attend.3 = (bf16[192,512]{1,0:T(8,128)(2,1)}, bf16[192,512]{1,0:T(8,128)(2,1)}, bf16[192,512]{1,0:T(8,128)(2,1)}, bf16[192,512]{1,0:T(8,128)(2,1)}) custom-call(s32[1]{0:T(128)} %bitcast.1.refs_0_, s32[768,1]{1,0:T(8,128)} %copy.22.refs_1_, s32[1,768]{1,0:T(1,128)} %copy-done.42, bf16[192,1536]{1,0:T(8,128)(2,1)} %get-tuple-element.112.refs_3_.refs_7_.refs_11_, ...), custom_call_target="tpu_custom_call" | custom-call | flops 40265320 | bytes 157286 | tf_op jit(solution)/shard_map/attend/pallas_call | solution.py:35
  83.4 5.9 out_proj.3
  91.4 10.7 %collective-permute-done.7.refs_1_ = bf16[192,2048]{1,0:T(8,128)(2,1)S(1)} collective-permute-done((bf16[192,2048]{1,0:T(8,128)(2,1)}, bf16[192,2048]{1,0:T(8,128)(2,1)S(1)}, u32[]{:S(2)}, u32[]{:S(2)}) %collective-permute-start.7) | collective-permute-done | bytes 786464 | tf_op jit(solution)/shard_map/ppermute | solution.py:56
  111.9 8.6 %collective-permute-done.6.refs_4_ = bf16[192,2048]{1,0:T(8,128)(2,1)} collective-permute-done((bf16[192,2048]{1,0:T(8,128)(2,1)}, bf16[192,2048]{1,0:T(8,128)(2,1)}, u32[]{:S(2)}, u32[]{:S(2)}) %collective-permute-start.6) | collective-permute-done | bytes 786464 | tf_op jit(solution)/shard_map/ppermute | solution.py:56
  121.3 16.1 %collective-permute-done.8.refs_5_ = bf16[192,2048]{1,0:T(8,128)(2,1)} collective-permute-done((bf16[192,2048]{1,0:T(8,128)(2,1)}, bf16[192,2048]{1,0:T(8,128)(2,1)}, u32[]{:S(2)}, u32[]{:S(2)}) %collective-permute-start.8) | collective-permute-done | bytes 786464 | tf_op jit(solution)/shard_map/ppermute | solution.py:56
  137.9 6.3 norm_second.1
  144.5 9.6 %collective-permute-done.14.refs_2_.refs_7_ = bf16[192,2048]{1,0:T(8,128)(2,1)S(1)} collective-permute-done((bf16[192,2048]{1,0:T(8,128)(2,1)S(1)}, bf16[192,2048]{1,0:T(8,128)(2,1)S(1)}, u32[]{:S(2)}, u32[]{:S(2)}) %collective-permute-start.14) | collective-permute-done | bytes 786464 | tf_op jit(solution)/shard_map/ppermute | solution.py:56
  155.6 15.5 %collective-permute-done.15.refs_3_.refs_8_ = bf16[192,2048]{1,0:T(8,128)(2,1)} collective-permute-done((bf16[192,2048]{1,0:T(8,128)(2,1)S(1)}, bf16[192,2048]{1,0:T(8,128)(2,1)}, u32[]{:S(2)}, u32[]{:S(2)}) %collective-permute-start.15) | collective-permute-done | bytes 786464 | tf_op jit(solution)/shard_map/ppermute | solution.py:56
  173.6 14.2 %collective-permute-done.12.refs_0_.refs_3_ = bf16[192,2048]{1,0:T(8,128)(2,1)S(1)} collective-permute-done((bf16[192,2048]{1,0:T(8,128)(2,1)}, bf16[192,2048]{1,0:T(8,128)(2,1)S(1)}, u32[]{:S(2)}, u32[]{:S(2)}) %collective-permute-start.12) | collective-permute-done | bytes 786464 | tf_op jit(solution)/shard_map/ppermute | solution.py:56
  188.4 16.3 %collective-permute-done.13.refs_1_.refs_4_ = bf16[192,2048]{1,0:T(8,128)(2,1)S(1)} collective-permute-done((bf16[192,2048]{1,0:T(8,128)(2,1)}, bf16[192,2048]{1,0:T(8,128)(2,1)S(1)}, u32[]{:S(2)}, u32[]{:S(2)}) %collective-permute-start.13) | collective-permute-done | bytes 786464 | tf_op jit(solution)/shard_map/ppermute | solution.py:56
  205.4 21.8 %feed_block.4 = (bf16[384,2048]{1,0:T(8,128)(2,1)}, bf16[384,2048]{1,0:T(8,128)(2,1)}, bf16[192,2048]{1,0:T(8,128)(2,1)}, bf16[192,2048]{1,0:T(8,128)(2,1)}, bf1...) custom-call(bf16[192,2048]{1,0:T(8,128)(2,1)} %get-tuple-element.129.refs_0_.refs_1_, ...), custom_call_target="tpu_custom_call" | custom-call | flops 644245120 | bytes 1310720 | tf_op jit(solution)/shard_map/feed_block/pallas_call | solution.py:35
  227.3 21.4 %feed_block.5 = (bf16[384,2048]{1,0:T(8,128)(2,1)}, bf16[384,2048]{1,0:T(8,128)(2,1)}, bf16[192,2048]{1,0:T(8,128)(2,1)}, bf16[192,2048]{1,0:T(8,128)(2,1)}, bf1...) custom-call(bf16[192,2048]{1,0:T(8,128)(2,1)} %copy-done.4, bf16[192,2048]{1,0:T(8,128)(2,1)} %copy-done.5, ...), custom_call_target="tpu_custom_call" | custom-call | flops 644245120 | bytes 1310720 | tf_op jit(solution)/shard_map/feed_block/pallas_call | solution.py:35
  249.6 21.5 %feed_block.6 = (bf16[384,2048]{1,0:T(8,128)(2,1)}, bf16[384,2048]{1,0:T(8,128)(2,1)}, bf16[192,2048]{1,0:T(8,128)(2,1)}, bf16[192,2048]{1,0:T(8,128)(2,1)}, bf1...) custom-call(bf16[192,2048]{1,0:T(8,128)(2,1)} %copy-done.6, bf16[192,2048]{1,0:T(8,128)(2,1)} %collective-permute-done.18.refs_1_.refs_6_, ...), custom_call_target="tpu_custom_call" | custom-call | flops 644245120 | bytes 1310720 | tf_op jit(solution)/shard_map/feed_block/pallas_call | solution.py:35
  272.0 21.5 %feed_block.7 = (bf16[384,2048]{1,0:T(8,128)(2,1)}, bf16[384,2048]{1,0:T(8,128)(2,1)}, bf16[192,2048]{1,0:T(8,128)(2,1)}, bf16[192,2048]{1,0:T(8,128)(2,1)}, bf1...) custom-call(bf16[192,2048]{1,0:T(8,128)(2,1)} %copy-done.7, bf16[192,2048]{1,0:T(8,128)(2,1)} %collective-permute-done.19.refs_1_.refs_8_, ...), custom_call_target="tpu_custom_call" | custom-call | flops 644245120 | bytes 1310720 | tf_op jit(solution)/shard_map/feed_block/pallas_call | solution.py:35
  293.4 20.7 %down_grad.2 = bf16[4,2048,256]{2,1,0:T(8,128)(2,1)} custom-call(s32[1]{0:T(128)} %bitcast.6.refs_0_, bf16[384,2048]{1,0:T(8,128)(2,1)} %get-tuple-element.133.refs_6_.refs_1_, bf16[384,2048]{1,0:T(8,128)(2,1)} %get-tuple-element.136.refs_6_.refs_2_, bf16[384,2048]{1,0:T(8,128)(2,1)} %get-tuple-element.137.refs_6_.refs_3_, ...), custom_call_target="tpu_custom_call" | custom-call | flops 322122560 | bytes 1048576 | tf_op jit(solution)/shard_map/down_grad/pallas_call | solution.py:35
  318.3 16.5 %collective-permute-done.31.refs_1_ = bf16[192,2048]{1,0:T(8,128)(2,1)S(1)} collective-permute-done((bf16[192,2048]{1,0:T(8,128)(2,1)}, bf16[192,2048]{1,0:T(8,128)(2,1)S(1)}, u32[]{:S(2)}, u32[]{:S(2)}) %collective-permute-start.31) | collective-permute-done | bytes 786464 | tf_op jit(solution)/shard_map/ppermute | solution.py:56
  344.3 21.5 %down_grad.3.refs_9_.refs_1_ = bf16[4,2048,256]{2,1,0:T(8,128)(2,1)} custom-call(s32[1]{0:T(128)} %bitcast.5.refs_0_, bf16[384,2048]{1,0:T(8,128)(2,1)} %get-tuple-element.133.refs_6_.refs_1_, bf16[384,2048]{1,0:T(8,128)(2,1)} %get-tuple-element.136.refs_6_.refs_2_, bf16[384,2048]{1,0:T(8,128)(2,1)} %get-tuple-element.137.refs_6_.refs_3_, ...), custom_call_target="tpu_custom_call" | custom-call | flops 322122560 | bytes 1048576 | tf_op jit(solution)/shard_map/down_grad/pallas_call | solution.py:35
  370.8 7.5 norm_second_back.1
  378.3 12.0 %up_grad.2 = bf16[4,256,2048]{2,1,0:T(8,128)(2,1)} custom-call(s32[1]{0:T(128)} %bitcast.6.refs_0_, bf16[192,2048]{1,0:T(8,128)(2,1)} %get-tuple-element.129.refs_0_.refs_1_, bf16[192,2048]{1,0:T(8,128)(2,1)} %get-tuple-element.130.refs_1_.refs_2_, bf16[192,2048]{1,0:T(8,128)(2,1)} %copy-done.4, bf16[192,2048]{1,0:T(8,128)(2,1)} %copy-done.5, ...), custom_call_target="tpu_custom_call" | custom-call | flops 322122560 | bytes 1048576 | tf_op jit(solution)/shard_map/up_grad/pallas_call | solution.py:35
  394.5 16.3 %collective-permute-done.38.refs_0_.refs_11_ = bf16[192,2048]{1,0:T(8,128)(2,1)S(1)} collective-permute-done((bf16[192,2048]{1,0:T(8,128)(2,1)S(1)}, bf16[192,2048]{1,0:T(8,128)(2,1)S(1)}, u32[]{:S(2)}, u32[]{:S(2)}) %collective-permute-start.38) | collective-permute-done | bytes 786464 | tf_op jit(solution)/shard_map/ppermute | solution.py:56
  416.0 4.4 collective-permute-start.70
  420.5 12.7 %up_grad.3.refs_7_.refs_3_.refs_1_ = bf16[4,256,2048]{2,1,0:T(8,128)(2,1)} custom-call(s32[1]{0:T(128)} %bitcast.5.refs_0_, bf16[192,2048]{1,0:T(8,128)(2,1)} %get-tuple-element.129.refs_0_.refs_1_, bf16[192,2048]{1,0:T(8,128)(2,1)} %get-tuple-element.130.refs_1_.refs_2_, bf16[192,2048]{1,0:T(8,128)(2,1)} %copy-done.4, bf16[192,2048]{1,0:T(8,128)(2,1)} %copy-done.5, ...), custom_call_target="tpu_custom_call" | custom-call | flops 322122560 | bytes 1048576 | tf_op jit(solution)/shard_map/up_grad/pallas_call | solution.py:35
  437.0 5.1 context_grad.4
  442.1 12.1 %attend_back.2 = (bf16[192,1536]{1,0:T(8,128)(2,1)}, bf16[192,1536]{1,0:T(8,128)(2,1)}, bf16[192,1536]{1,0:T(8,128)(2,1)}, bf16[192,1536]{1,0:T(8,128)(2,1)}) custom-call(s32[1]{0:T(128)} %bitcast.1.refs_0_, s32[768,1]{1,0:T(8,128)} %copy.21.refs_1_, s32[1,768]{1,0:T(1,128)} %copy-done.43, ...), custom_call_target="tpu_custom_call" | custom-call | flops 100663296 | bytes 275251 | tf_op jit(solution)/shard_map/attend_back/pallas_call | solution.py:35
  459.2 12.1 %attend_back.3 = (bf16[192,1536]{1,0:T(8,128)(2,1)}, bf16[192,1536]{1,0:T(8,128)(2,1)}, bf16[192,1536]{1,0:T(8,128)(2,1)}, bf16[192,1536]{1,0:T(8,128)(2,1)}) custom-call(s32[1]{0:T(128)} %bitcast.1.refs_0_, s32[768,1]{1,0:T(8,128)} %copy.22.refs_1_, s32[1,768]{1,0:T(1,128)} %copy-done.42, bf16[192,1536]{1,0:T(8,128)(2,1)} %get-tuple-element.112.refs_3_.refs_7_.refs_11_, ...), custom_call_target="tpu_custom_call" | custom-call | flops 100663296 | bytes 275251 | tf_op jit(solution)/shard_map/attend_back/pallas_call | solution.py:35
  471.3 5.9 qkv_back.2
  477.2 9.7 %qkv_grad.2 = bf16[4,256,1536]{2,1,0:T(8,128)(2,1)} custom-call(s32[1]{0:T(128)} %bitcast.6.refs_0_, bf16[192,2048]{1,0:T(8,128)(2,1)} %get-tuple-element.99.refs_0_.refs_1_, bf16[192,2048]{1,0:T(8,128)(2,1)} %get-tuple-element.100.refs_1_.refs_2_, bf16[192,2048]{1,0:T(8,128)(2,1)} %copy-done.9, bf16[192,2048]{1,0:T(8,128)(2,1)} %copy-done.11, ...), custom_call_target="tpu_custom_call" | custom-call | flops 241591904 | bytes 865075 | tf_op jit(solution)/shard_map/qkv_grad/pallas_call | solution.py:35
  490.6 16.7 %collective-permute-done.16.refs_3_ = bf16[192,2048]{1,0:T(8,128)(2,1)} collective-permute-done((bf16[192,2048]{1,0:T(8,128)(2,1)}, bf16[192,2048]{1,0:T(8,128)(2,1)}, u32[]{:S(2)}, u32[]{:S(2)}) %collective-permute-start.16) | collective-permute-done | bytes 786464 | tf_op jit(solution)/shard_map/ppermute | solution.py:56
  518.2 7.1 collective-permute-done.25.refs_1_
  542.1 6.8 collective-permute-done.26.refs_4_
  553.6 6.9 collective-permute-done.64.refs_2_
  563.4 5.4 collective-permute-start.65
  577.0 11.6 %qkv_back.3 = (bf16[192,2048]{1,0:T(8,128)(2,1)}, bf16[192,2048]{1,0:T(8,128)(2,1)}, bf16[192,2048]{1,0:T(8,128)(2,1)}, bf16[192,2048]{1,0:T(8,128)(2,1)}, bf16[...) custom-call(bf16[192,1536]{1,0:T(8,128)(2,1)} %get-tuple-element.162.refs_3_.refs_9_.refs_0_, ...), custom_call_target="tpu_custom_call" | custom-call | flops 362387872 | bytes 727449 | tf_op jit(solution)/shard_map/qkv_back/pallas_call | solution.py:35
  590.2 10.2 %qkv_grad.3.refs_1_.refs_17_ = bf16[4,256,1536]{2,1,0:T(8,128)(2,1)} custom-call(s32[1]{0:T(128)} %bitcast.5.refs_0_, bf16[192,2048]{1,0:T(8,128)(2,1)} %get-tuple-element.99.refs_0_.refs_1_, bf16[192,2048]{1,0:T(8,128)(2,1)} %get-tuple-element.100.refs_1_.refs_2_, bf16[192,2048]{1,0:T(8,128)(2,1)} %copy-done.9, bf16[192,2048]{1,0:T(8,128)(2,1)} %copy-done.11, ...), custom_call_target="tpu_custom_call" | custom-call | flops 241591904 | bytes 865075 | tf_op jit(solution)/shard_map/qkv_grad/pallas_call | solution.py:35
  617.6 6.8 out_grad.2
  629.9 15.1 %collective-permute-start.52 = (bf16[256,1536]{1,0:T(8,128)(2,1)}, bf16[256,1536]{1,0:T(8,128)(2,1)S(1)}, u32[]{:S(2)}, u32[]{:S(2)}) collective-permute-start(bf16[256,1536]{1,0:T(8,128)(2,1)} %share_sum.20), channel_id=1, source_target_pairs={{0,8},{4,12},{8,16},{12,20},{1,9},{5,13},{9,17},{13,21},{2,10},{6,... | collective-permute-start | bytes 2359304 | tf_op jit(solution)/shard_map/ppermute | solution.py:546
  655.9 7.1 out_grad.3.refs_1_
  665.0 30.4 %collective-permute-start.58 = (bf16[512,256]{1,0:T(8,128)(2,1)S(1)}, bf16[512,256]{1,0:T(8,128)(2,1)}, u32[]{:S(2)}, u32[]{:S(2)}) collective-permute-start(bf16[512,256]{1,0:T(8,128)(2,1)S(1)} %get-tuple-element.197), channel_id=1, source_target_pairs={{0,8},{4,12},{1,9},{5,13},{2,10},{6,14},{3,11},{7,15}} | collective-permute-start | bytes 786440 | tf_op jit(solution)/shard_map/ppermute | solution.py:546
  705.1 5.1 collective-permute-start.59
  715.7 5.2 output.1
  724.0 7.3 norm_first_back.1
  733.8 5.2 collective-permute-start.60
  743.4 13.0 %everyone.1 = f32[8,512]{1,0:T(8,128)} custom-call(f32[8,512]{1,0:T(8,128)} %reshape.105.x), custom_call_target="tpu_custom_call" | custom-call | tf_op jit(solution)/shard_map/everyone/pallas_call | solution.py:643
  (274 shorter events, 207.1 us)
Async XLA Ops:
  9.5 33.9 %collective-permute-start.1 = (bf16[192,2048]{1,0:T(8,128)(2,1)}, bf16[192,2048]{1,0:T(8,128)(2,1)S(1)}, u32[]{:S(2)}, u32[]{:S(2)}) collective-permute-start(bf16[192,2048]{1,0:T(8,128)(2,1)} %get-tuple-element.100.refs_1_.refs_2_), channel_id=1, source_target_pairs={{0,1},{1,0},{2,3},{3,2},{4,5},{5,4},{6,7},{7,6},{8,9},{9,8},{10,11... | collective-permute-start | bytes 2359304 | tf_op jit(solution)/shard_map/ppermute | solution.py:56
  10.0 35.5 %collective-permute-start.2 = (bf16[192,2048]{1,0:T(8,128)(2,1)}, bf16[192,2048]{1,0:T(8,128)(2,1)S(1)}, u32[]{:S(2)}, u32[]{:S(2)}) collective-permute-start(bf16[192,2048]{1,0:T(8,128)(2,1)} %get-tuple-element.99.refs_0_.refs_1_), channel_id=1, source_target_pairs={{0,2},{1,3},{2,0},{3,1},{4,6},{5,7},{6,4},{7,5},{8,10},{9,11},{10,... | collective-permute-start | bytes 2359304 | tf_op jit(solution)/shard_map/ppermute | solution.py:56
  26.5 36.8 %collective-permute-start.4 = (bf16[192,2048]{1,0:T(8,128)(2,1)S(1)}, bf16[192,2048]{1,0:T(8,128)(2,1)}, u32[]{:S(2)}, u32[]{:S(2)}) collective-permute-start(bf16[192,2048]{1,0:T(8,128)(2,1)S(1)} %collective-permute-done.refs_0_.refs_3_), channel_id=1, source_target_pairs={{0,2},{1,3},{2,0},{3,1},{4,6},{5,7},{6,4},{7,5},{8,10},{9,11},{10,... | collective-permute-start | bytes 2359304 | tf_op jit(solution)/shard_map/ppermute | solution.py:56
  28.6 34.7 %collective-permute-start.5 = (bf16[192,2048]{1,0:T(8,128)(2,1)S(1)}, bf16[192,2048]{1,0:T(8,128)(2,1)}, u32[]{:S(2)}, u32[]{:S(2)}) collective-permute-start(bf16[192,2048]{1,0:T(8,128)(2,1)S(1)} %collective-permute-done.3.refs_3_.refs_6_), channel_id=1, source_target_pairs={{0,1},{1,0},{2,3},{3,2},{4,5},{5,4},{6,7},{7,6},{8,9},{9,8},{10,11... | collective-permute-start | bytes 2359304 | tf_op jit(solution)/shard_map/ppermute | solution.py:56
  89.3 31.2 %collective-permute-start.6 = (bf16[192,2048]{1,0:T(8,128)(2,1)}, bf16[192,2048]{1,0:T(8,128)(2,1)}, u32[]{:S(2)}, u32[]{:S(2)}) collective-permute-start(bf16[192,2048]{1,0:T(8,128)(2,1)} %get-tuple-element.123), channel_id=1, source_target_pairs={{0,1},{1,0},{2,3},{3,2},{4,5},{5,4},{6,7},{7,6},{8,9},{9,8},{10,11... | collective-permute-start | bytes 2359304 | tf_op jit(solution)/shard_map/ppermute | solution.py:56
  90.9 30.2 %collective-permute-start.11 = (bf16[192,2048]{1,0:T(8,128)(2,1)}, bf16[192,2048]{1,0:T(8,128)(2,1)}, u32[]{:S(2)}, u32[]{:S(2)}) collective-permute-start(bf16[192,2048]{1,0:T(8,128)(2,1)} %get-tuple-element.127), channel_id=1, source_target_pairs={{0,2},{1,3},{2,0},{3,1},{4,6},{5,7},{6,4},{7,5},{8,10},{9,11},{10,... | collective-permute-start | bytes 2359304 | tf_op jit(solution)/shard_map/ppermute | solution.py:56
  105.1 32.2 %collective-permute-start.8 = (bf16[192,2048]{1,0:T(8,128)(2,1)}, bf16[192,2048]{1,0:T(8,128)(2,1)}, u32[]{:S(2)}, u32[]{:S(2)}) collective-permute-start(bf16[192,2048]{1,0:T(8,128)(2,1)} %add_rows.8), channel_id=1, source_target_pairs={{0,1},{1,0},{2,3},{3,2},{4,5},{5,4},{6,7},{7,6},{8,9},{9,8},{10,11... | collective-permute-start | bytes 2359304 | tf_op jit(solution)/shard_map/ppermute | solution.py:56
  110.4 43.7 %collective-permute-start.14 = (bf16[192,2048]{1,0:T(8,128)(2,1)S(1)}, bf16[192,2048]{1,0:T(8,128)(2,1)S(1)}, u32[]{:S(2)}, u32[]{:S(2)}) collective-permute-start(bf16[192,2048]{1,0:T(8,128)(2,1)S(1)} %get-tuple-element.195.refs_2_.refs_5_), channel_id=1, source_target_pairs={{0,1},{1,0},{2,3},{3,2},{4,5},{5,4},{6,7},{7,6},{8,9},{9,8},{10,11... | collective-permute-start | bytes 2359304 | tf_op jit(solution)/shard_map/ppermute | solution.py:56
  120.5 50.6 %collective-permute-start.15 = (bf16[192,2048]{1,0:T(8,128)(2,1)S(1)}, bf16[192,2048]{1,0:T(8,128)(2,1)}, u32[]{:S(2)}, u32[]{:S(2)}) collective-permute-start(bf16[192,2048]{1,0:T(8,128)(2,1)S(1)} %get-tuple-element.194.refs_3_.refs_6_), channel_id=1, source_target_pairs={{0,1},{1,0},{2,3},{3,2},{4,5},{5,4},{6,7},{7,6},{8,9},{9,8},{10,11... | collective-permute-start | bytes 2359304 | tf_op jit(solution)/shard_map/ppermute | solution.py:56
  121.0 50.5 %collective-permute-start.21 = (bf16[192,2048]{1,0:T(8,128)(2,1)S(1)}, bf16[192,2048]{1,0:T(8,128)(2,1)}, u32[]{:S(2)}, u32[]{:S(2)}) collective-permute-start(bf16[192,2048]{1,0:T(8,128)(2,1)S(1)} %get-tuple-element.194.refs_3_.refs_6_), channel_id=1, source_target_pairs={{0,2},{1,3},{2,0},{3,1},{4,6},{5,7},{6,4},{7,5},{8,10},{9,11},{10,... | collective-permute-start | bytes 2359304 | tf_op jit(solution)/shard_map/ppermute | solution.py:56
  137.4 35.7 %collective-permute-start.24 = (bf16[192,2048]{1,0:T(8,128)(2,1)S(1)}, bf16[192,2048]{1,0:T(8,128)(2,1)}, u32[]{:S(2)}, u32[]{:S(2)}) collective-permute-start(bf16[192,2048]{1,0:T(8,128)(2,1)S(1)} %get-tuple-element.195.refs_2_.refs_5_), channel_id=1, source_target_pairs={{0,2},{1,3},{2,0},{3,1},{4,6},{5,7},{6,4},{7,5},{8,10},{9,11},{10,... | collective-permute-start | bytes 2359304 | tf_op jit(solution)/shard_map/ppermute | solution.py:56
  144.2 43.6 %collective-permute-start.12 = (bf16[192,2048]{1,0:T(8,128)(2,1)}, bf16[192,2048]{1,0:T(8,128)(2,1)S(1)}, u32[]{:S(2)}, u32[]{:S(2)}) collective-permute-start(bf16[192,2048]{1,0:T(8,128)(2,1)} %get-tuple-element.129.refs_0_.refs_1_), channel_id=1, source_target_pairs={{0,1},{1,0},{2,3},{3,2},{4,5},{5,4},{6,7},{7,6},{8,9},{9,8},{10,11... | collective-permute-start | bytes 2359304 | tf_op jit(solution)/shard_map/ppermute | solution.py:56
  155.0 49.6 %collective-permute-start.13 = (bf16[192,2048]{1,0:T(8,128)(2,1)}, bf16[192,2048]{1,0:T(8,128)(2,1)S(1)}, u32[]{:S(2)}, u32[]{:S(2)}) collective-permute-start(bf16[192,2048]{1,0:T(8,128)(2,1)} %get-tuple-element.130.refs_1_.refs_2_), channel_id=1, source_target_pairs={{0,1},{1,0},{2,3},{3,2},{4,5},{5,4},{6,7},{7,6},{8,9},{9,8},{10,11... | collective-permute-start | bytes 2359304 | tf_op jit(solution)/shard_map/ppermute | solution.py:56
  171.1 34.1 %collective-permute-start.18 = (bf16[192,2048]{1,0:T(8,128)(2,1)}, bf16[192,2048]{1,0:T(8,128)(2,1)}, u32[]{:S(2)}, u32[]{:S(2)}) collective-permute-start(bf16[192,2048]{1,0:T(8,128)(2,1)} %get-tuple-element.130.refs_1_.refs_2_), channel_id=1, source_target_pairs={{0,2},{1,3},{2,0},{3,1},{4,6},{5,7},{6,4},{7,5},{8,10},{9,11},{10,... | collective-permute-start | bytes 2359304 | tf_op jit(solution)/shard_map/ppermute | solution.py:56
  171.6 77.1 %collective-permute-start.23 = (bf16[192,2048]{1,0:T(8,128)(2,1)}, bf16[192,2048]{1,0:T(8,128)(2,1)S(1)}, u32[]{:S(2)}, u32[]{:S(2)}) collective-permute-start(bf16[192,2048]{1,0:T(8,128)(2,1)} %get-tuple-element.129.refs_0_.refs_1_), channel_id=1, source_target_pairs={{0,2},{1,3},{2,0},{3,1},{4,6},{5,7},{6,4},{7,5},{8,10},{9,11},{10,... | collective-permute-start | bytes 2359304 | tf_op jit(solution)/shard_map/ppermute | solution.py:56
  173.1 97.9 %collective-permute-start.20 = (bf16[192,2048]{1,0:T(8,128)(2,1)}, bf16[192,2048]{1,0:T(8,128)(2,1)}, u32[]{:S(2)}, u32[]{:S(2)}) collective-permute-start(bf16[192,2048]{1,0:T(8,128)(2,1)} %copy-done.8), channel_id=1, source_target_pairs={{0,2},{1,3},{2,0},{3,1},{4,6},{5,7},{6,4},{7,5},{8,10},{9,11},{10,... | collective-permute-start | bytes 2359304 | tf_op jit(solution)/shard_map/ppermute | solution.py:56
  187.8 83.2 %collective-permute-start.22 = (bf16[192,2048]{1,0:T(8,128)(2,1)}, bf16[192,2048]{1,0:T(8,128)(2,1)}, u32[]{:S(2)}, u32[]{:S(2)}) collective-permute-start(bf16[192,2048]{1,0:T(8,128)(2,1)} %collective-permute-done.21.refs_3_.refs_10_), channel_id=1, source_target_pairs={{0,1},{1,0},{2,3},{3,2},{4,5},{5,4},{6,7},{7,6},{8,9},{9,8},{10,11... | collective-permute-start | bytes 2359304 | tf_op jit(solution)/shard_map/ppermute | solution.py:56
  204.7 66.4 %collective-permute-start.17 = (bf16[192,2048]{1,0:T(8,128)(2,1)S(1)}, bf16[192,2048]{1,0:T(8,128)(2,1)S(1)}, u32[]{:S(2)}, u32[]{:S(2)}) collective-permute-start(bf16[192,2048]{1,0:T(8,128)(2,1)S(1)} %collective-permute-done.12.refs_0_.refs_3_), channel_id=1, source_target_pairs={{0,2},{1,3},{2,0},{3,1},{4,6},{5,7},{6,4},{7,5},{8,10},{9,11},{10,... | collective-permute-start | bytes 2359304 | tf_op jit(solution)/shard_map/ppermute | solution.py:56
  205.2 65.9 %collective-permute-start.19 = (bf16[192,2048]{1,0:T(8,128)(2,1)}, bf16[192,2048]{1,0:T(8,128)(2,1)}, u32[]{:S(2)}, u32[]{:S(2)}) collective-permute-start(bf16[192,2048]{1,0:T(8,128)(2,1)} %collective-permute-done.18.refs_1_.refs_6_), channel_id=1, source_target_pairs={{0,1},{1,0},{2,3},{3,2},{4,5},{5,4},{6,7},{7,6},{8,9},{9,8},{10,11... | collective-permute-start | bytes 2359304 | tf_op jit(solution)/shard_map/ppermute | solution.py:56
  314.1 30.2 %collective-permute-start.36 = (bf16[4,2048,256]{2,1,0:T(8,128)(2,1)}, bf16[4,2048,256]{2,1,0:T(8,128)(2,1)}, u32[]{:S(2)}, u32[]{:S(2)}) collective-permute-start(bf16[4,2048,256]{2,1,0:T(8,128)(2,1)} %down_grad.2), channel_id=1, source_target_pairs={{0,4},{4,0},{8,12},{12,8},{16,20},{20,16},{24,28},{28,24},{1,5},{5... | collective-permute-start | bytes 12582920 | tf_op jit(solution)/shard_map/ppermute | solution.py:546
  317.6 48.3 %collective-permute-start.30 = (bf16[192,2048]{1,0:T(8,128)(2,1)S(1)}, bf16[192,2048]{1,0:T(8,128)(2,1)S(1)}, u32[]{:S(2)}, u32[]{:S(2)}) collective-permute-start(bf16[192,2048]{1,0:T(8,128)(2,1)S(1)} %copy-done.46), channel_id=1, source_target_pairs={{0,1},{1,0},{2,3},{3,2},{4,5},{5,4},{6,7},{7,6},{8,9},{9,8},{10,11... | collective-permute-start | bytes 2359304 | tf_op jit(solution)/shard_map/ppermute | solution.py:56
  318.1 47.7 %collective-permute-start.35 = (bf16[192,2048]{1,0:T(8,128)(2,1)}, bf16[192,2048]{1,0:T(8,128)(2,1)S(1)}, u32[]{:S(2)}, u32[]{:S(2)}) collective-permute-start(bf16[192,2048]{1,0:T(8,128)(2,1)} %get-tuple-element.153), channel_id=1, source_target_pairs={{0,2},{1,3},{2,0},{3,1},{4,6},{5,7},{6,4},{7,5},{8,10},{9,11},{10,... | collective-permute-start | bytes 2359304 | tf_op jit(solution)/shard_map/ppermute | solution.py:56
  337.9 31.7 %collective-permute-start.32 = (bf16[192,2048]{1,0:T(8,128)(2,1)}, bf16[192,2048]{1,0:T(8,128)(2,1)S(1)}, u32[]{:S(2)}, u32[]{:S(2)}) collective-permute-start(bf16[192,2048]{1,0:T(8,128)(2,1)} %add_rows.12), channel_id=1, source_target_pairs={{0,1},{1,0},{2,3},{3,2},{4,5},{5,4},{6,7},{7,6},{8,9},{9,8},{10,11... | collective-permute-start | bytes 2359304 | tf_op jit(solution)/shard_map/ppermute | solution.py:56
  392.4 44.6 %collective-permute-start.39 = (bf16[192,2048]{1,0:T(8,128)(2,1)}, bf16[192,2048]{1,0:T(8,128)(2,1)}, u32[]{:S(2)}, u32[]{:S(2)}) collective-permute-start(bf16[192,2048]{1,0:T(8,128)(2,1)} %get-tuple-element.157.refs_1_.refs_10_), channel_id=1, source_target_pairs={{0,1},{1,0},{2,3},{3,2},{4,5},{5,4},{6,7},{7,6},{8,9},{9,8},{10,11... | collective-permute-start | bytes 2359304 | tf_op jit(solution)/shard_map/ppermute | solution.py:56
  392.7 44.3 %collective-permute-start.40 = (bf16[192,2048]{1,0:T(8,128)(2,1)S(1)}, bf16[192,2048]{1,0:T(8,128)(2,1)}, u32[]{:S(2)}, u32[]{:S(2)}) collective-permute-start(bf16[192,2048]{1,0:T(8,128)(2,1)S(1)} %copy-done.2), channel_id=1, source_target_pairs={{0,2},{1,3},{2,0},{3,1},{4,6},{5,7},{6,4},{7,5},{8,10},{9,11},{10,... | collective-permute-start | bytes 2359304 | tf_op jit(solution)/shard_map/ppermute | solution.py:56
  410.8 43.4 %collective-permute-start.42 = (bf16[192,2048]{1,0:T(8,128)(2,1)S(1)}, bf16[192,2048]{1,0:T(8,128)(2,1)S(1)}, u32[]{:S(2)}, u32[]{:S(2)}) collective-permute-start(bf16[192,2048]{1,0:T(8,128)(2,1)S(1)} %collective-permute-done.38.refs_0_.refs_11_), channel_id=1, source_target_pairs={{0,2},{1,3},{2,0},{3,1},{4,6},{5,7},{6,4},{7,5},{8,10},{9,11},{10,... | collective-permute-start | bytes 2359304 | tf_op jit(solution)/shard_map/ppermute | solution.py:56
  412.5 41.7 %collective-permute-start.43 = (bf16[192,2048]{1,0:T(8,128)(2,1)S(1)}, bf16[192,2048]{1,0:T(8,128)(2,1)S(1)}, u32[]{:S(2)}, u32[]{:S(2)}) collective-permute-start(bf16[192,2048]{1,0:T(8,128)(2,1)S(1)} %collective-permute-done.41.refs_3_.refs_14_), channel_id=1, source_target_pairs={{0,1},{1,0},{2,3},{3,2},{4,5},{5,4},{6,7},{7,6},{8,9},{9,8},{10,11... | collective-permute-start | bytes 2359304 | tf_op jit(solution)/shard_map/ppermute | solution.py:56
  416.0 92.8 %collective-permute-start.70 = (bf16[2048,256]{1,0:T(8,128)(2,1)}, bf16[2048,256]{1,0:T(8,128)(2,1)}, u32[]{:S(2)}, u32[]{:S(2)}) collective-permute-start(bf16[2048,256]{1,0:T(8,128)(2,1)} %get-tuple-element.189), channel_id=1, source_target_pairs={{0,8},{4,12},{1,9},{5,13},{2,10},{6,14},{3,11},{7,15}} | collective-permute-start | bytes 3145736 | tf_op jit(solution)/shard_map/ppermute | solution.py:546
  486.9 88.4 %collective-permute-start.44 = (bf16[4,256,1536]{2,1,0:T(8,128)(2,1)}, bf16[4,256,1536]{2,1,0:T(8,128)(2,1)S(1)}, u32[]{:S(2)}, u32[]{:S(2)}) collective-permute-start(bf16[4,256,1536]{2,1,0:T(8,128)(2,1)} %qkv_grad.2), channel_id=1, source_target_pairs={{0,4},{4,0},{8,12},{12,8},{16,20},{20,16},{24,28},{28,24},{1,5},{5... | collective-permute-start | bytes 9437192 | tf_op jit(solution)/shard_map/ppermute | solution.py:546
  489.1 36.3 %collective-permute-start.25 = (bf16[192,2048]{1,0:T(8,128)(2,1)}, bf16[192,2048]{1,0:T(8,128)(2,1)}, u32[]{:S(2)}, u32[]{:S(2)}) collective-permute-start(bf16[192,2048]{1,0:T(8,128)(2,1)} %get-tuple-element.138), channel_id=1, source_target_pairs={{0,2},{1,3},{2,0},{3,1},{4,6},{5,7},{6,4},{7,5},{8,10},{9,11},{10,... | collective-permute-start | bytes 2359304 | tf_op jit(solution)/shard_map/ppermute | solution.py:56
  525.4 35.1 %collective-permute-start.64 = (bf16[256,2048]{1,0:T(8,128)(2,1)}, bf16[256,2048]{1,0:T(8,128)(2,1)}, u32[]{:S(2)}, u32[]{:S(2)}) collective-permute-start(bf16[256,2048]{1,0:T(8,128)(2,1)} %get-tuple-element.191), channel_id=1, source_target_pairs={{0,8},{4,12},{1,9},{5,13},{2,10},{6,14},{3,11},{7,15}} | collective-permute-start | bytes 3145736 | tf_op jit(solution)/shard_map/ppermute | solution.py:546
  530.4 33.1 %collective-permute-start.67 = (bf16[256,2048]{1,0:T(8,128)(2,1)}, bf16[256,2048]{1,0:T(8,128)(2,1)}, u32[]{:S(2)}, u32[]{:S(2)}) collective-permute-start(bf16[256,2048]{1,0:T(8,128)(2,1)} %get-tuple-element.190), channel_id=1, source_target_pairs={{24,16},{28,20},{25,17},{29,21},{26,18},{30,22},{27,19},{31,23}} | collective-permute-start | bytes 3145736 | tf_op jit(solution)/shard_map/ppermute | solution.py:546
  538.0 33.2 %collective-permute-start.74 = (bf16[2048,256]{1,0:T(8,128)(2,1)}, bf16[2048,256]{1,0:T(8,128)(2,1)}, u32[]{:S(2)}, u32[]{:S(2)}) collective-permute-start(bf16[2048,256]{1,0:T(8,128)(2,1)} %share_sum.37), channel_id=1, source_target_pairs={{24,16},{28,20},{16,8},{20,12},{25,17},{29,21},{17,9},{21,13},{26,... | collective-permute-start | bytes 3145736 | tf_op jit(solution)/shard_map/ppermute | solution.py:546
  548.9 51.5 %collective-permute-start.72 = (bf16[2048,256]{1,0:T(8,128)(2,1)}, bf16[2048,256]{1,0:T(8,128)(2,1)}, u32[]{:S(2)}, u32[]{:S(2)}) collective-permute-start(bf16[2048,256]{1,0:T(8,128)(2,1)} %share_sum.36), channel_id=1, source_target_pairs={{0,8},{4,12},{8,16},{12,20},{16,24},{20,28},{1,9},{5,13},{9,17},{1... | collective-permute-start | bytes 3145736 | tf_op jit(solution)/shard_map/ppermute | solution.py:546
  563.4 40.7 %collective-permute-start.65 = (bf16[256,2048]{1,0:T(8,128)(2,1)}, bf16[256,2048]{1,0:T(8,128)(2,1)}, u32[]{:S(2)}, u32[]{:S(2)}) collective-permute-start(bf16[256,2048]{1,0:T(8,128)(2,1)} %share_sum.30), channel_id=1, source_target_pairs={{0,8},{4,12},{8,16},{12,20},{1,9},{5,13},{9,17},{13,21},{2,10},{6,... | collective-permute-start | bytes 3145736 | tf_op jit(solution)/shard_map/ppermute | solution.py:546
  571.2 39.7 %collective-permute-start.68 = (bf16[256,2048]{1,0:T(8,128)(2,1)}, bf16[256,2048]{1,0:T(8,128)(2,1)}, u32[]{:S(2)}, u32[]{:S(2)}) collective-permute-start(bf16[256,2048]{1,0:T(8,128)(2,1)} %share_sum.32), channel_id=1, source_target_pairs={{24,16},{28,20},{16,8},{20,12},{25,17},{29,21},{17,9},{21,13},{26,... | collective-permute-start | bytes 3145736 | tf_op jit(solution)/shard_map/ppermute | solution.py:546
  575.3 39.4 %collective-permute-start.75 = (bf16[2048,256]{1,0:T(8,128)(2,1)}, bf16[2048,256]{1,0:T(8,128)(2,1)}, u32[]{:S(2)}, u32[]{:S(2)}) collective-permute-start(bf16[2048,256]{1,0:T(8,128)(2,1)} %share_sum.38), channel_id=1, source_target_pairs={{24,16},{28,20},{16,8},{20,12},{8,0},{12,4},{25,17},{29,21},{17,9}... | collective-permute-start | bytes 3145736 | tf_op jit(solution)/shard_map/ppermute | solution.py:546
  611.0 37.0 %collective-permute-start.66 = (bf16[256,2048]{1,0:T(8,128)(2,1)}, bf16[256,2048]{1,0:T(8,128)(2,1)S(1)}, u32[]{:S(2)}, u32[]{:S(2)}) collective-permute-start(bf16[256,2048]{1,0:T(8,128)(2,1)} %share_sum.31), channel_id=1, source_target_pairs={{0,8},{4,12},{8,16},{12,20},{16,24},{20,28},{1,9},{5,13},{9,17},{1... | collective-permute-start | bytes 3145736 | tf_op jit(solution)/shard_map/ppermute | solution.py:546
  614.8 37.0 %collective-permute-start.69 = (bf16[256,2048]{1,0:T(8,128)(2,1)}, bf16[256,2048]{1,0:T(8,128)(2,1)S(1)}, u32[]{:S(2)}, u32[]{:S(2)}) collective-permute-start(bf16[256,2048]{1,0:T(8,128)(2,1)} %share_sum.33), channel_id=1, source_target_pairs={{24,16},{28,20},{16,8},{20,12},{8,0},{12,4},{25,17},{29,21},{17,9}... | collective-permute-start | bytes 3145736 | tf_op jit(solution)/shard_map/ppermute | solution.py:546
  626.8 36.2 %collective-permute-start.45 = (bf16[192,2048]{1,0:T(8,128)(2,1)}, bf16[192,2048]{1,0:T(8,128)(2,1)}, u32[]{:S(2)}, u32[]{:S(2)}) collective-permute-start(bf16[192,2048]{1,0:T(8,128)(2,1)} %get-tuple-element.177), channel_id=1, source_target_pairs={{0,1},{1,0},{2,3},{3,2},{4,5},{5,4},{6,7},{7,6},{8,9},{9,8},{10,11... | collective-permute-start | bytes 2359304 | tf_op jit(solution)/shard_map/ppermute | solution.py:56
  629.9 35.1 %collective-permute-start.52 = (bf16[256,1536]{1,0:T(8,128)(2,1)}, bf16[256,1536]{1,0:T(8,128)(2,1)S(1)}, u32[]{:S(2)}, u32[]{:S(2)}) collective-permute-start(bf16[256,1536]{1,0:T(8,128)(2,1)} %share_sum.20), channel_id=1, source_target_pairs={{0,8},{4,12},{8,16},{12,20},{1,9},{5,13},{9,17},{13,21},{2,10},{6,... | collective-permute-start | bytes 2359304 | tf_op jit(solution)/shard_map/ppermute | solution.py:546
  648.0 47.4 %collective-permute-start.55 = (bf16[256,1536]{1,0:T(8,128)(2,1)}, bf16[256,1536]{1,0:T(8,128)(2,1)}, u32[]{:S(2)}, u32[]{:S(2)}) collective-permute-start(bf16[256,1536]{1,0:T(8,128)(2,1)} %share_sum.22), channel_id=1, source_target_pairs={{24,16},{28,20},{16,8},{20,12},{25,17},{29,21},{17,9},{21,13},{26,... | collective-permute-start | bytes 2359304 | tf_op jit(solution)/shard_map/ppermute | solution.py:546
  651.8 48.8 %collective-permute-start.47 = (bf16[192,2048]{1,0:T(8,128)(2,1)}, bf16[192,2048]{1,0:T(8,128)(2,1)}, u32[]{:S(2)}, u32[]{:S(2)}) collective-permute-start(bf16[192,2048]{1,0:T(8,128)(2,1)} %add_rows.14), channel_id=1, source_target_pairs={{0,1},{1,0},{2,3},{3,2},{4,5},{5,4},{6,7},{7,6},{8,9},{9,8},{10,11... | collective-permute-start | bytes 2359304 | tf_op jit(solution)/shard_map/ppermute | solution.py:56
  654.5 57.5 %collective-permute-start.49 = (bf16[192,2048]{1,0:T(8,128)(2,1)}, bf16[192,2048]{1,0:T(8,128)(2,1)}, u32[]{:S(2)}, u32[]{:S(2)}) collective-permute-start(bf16[192,2048]{1,0:T(8,128)(2,1)} %add_rows.15), channel_id=1, source_target_pairs={{0,2},{1,3},{2,0},{3,1},{4,6},{5,7},{6,4},{7,5},{8,10},{9,11},{10,... | collective-permute-start | bytes 2359304 | tf_op jit(solution)/shard_map/ppermute | solution.py:56
  663.0 61.0 %collective-permute-start.50 = (bf16[192,2048]{1,0:T(8,128)(2,1)}, bf16[192,2048]{1,0:T(8,128)(2,1)}, u32[]{:S(2)}, u32[]{:S(2)}) collective-permute-start(bf16[192,2048]{1,0:T(8,128)(2,1)} %get-tuple-element.181), channel_id=1, source_target_pairs={{0,2},{1,3},{2,0},{3,1},{4,6},{5,7},{6,4},{7,5},{8,10},{9,11},{10,... | collective-permute-start | bytes 2359304 | tf_op jit(solution)/shard_map/ppermute | solution.py:56
  665.0 37.0 %collective-permute-start.58 = (bf16[512,256]{1,0:T(8,128)(2,1)S(1)}, bf16[512,256]{1,0:T(8,128)(2,1)}, u32[]{:S(2)}, u32[]{:S(2)}) collective-permute-start(bf16[512,256]{1,0:T(8,128)(2,1)S(1)} %get-tuple-element.197), channel_id=1, source_target_pairs={{0,8},{4,12},{1,9},{5,13},{2,10},{6,14},{3,11},{7,15}} | collective-permute-start | bytes 786440 | tf_op jit(solution)/shard_map/ppermute | solution.py:546
  700.6 61.1 %collective-permute-start.53 = (bf16[256,1536]{1,0:T(8,128)(2,1)S(1)}, bf16[256,1536]{1,0:T(8,128)(2,1)S(1)}, u32[]{:S(2)}, u32[]{:S(2)}) collective-permute-start(bf16[256,1536]{1,0:T(8,128)(2,1)S(1)} %copy-done.25), channel_id=1, source_target_pairs={{0,8},{4,12},{8,16},{12,20},{16,24},{20,28},{1,9},{5,13},{9,17},{1... | collective-permute-start | bytes 2359304 | tf_op jit(solution)/shard_map/ppermute | solution.py:546
  702.0 59.8 %collective-permute-start.56 = (bf16[256,1536]{1,0:T(8,128)(2,1)}, bf16[256,1536]{1,0:T(8,128)(2,1)S(1)}, u32[]{:S(2)}, u32[]{:S(2)}) collective-permute-start(bf16[256,1536]{1,0:T(8,128)(2,1)} %share_sum.23), channel_id=1, source_target_pairs={{24,16},{28,20},{16,8},{20,12},{8,0},{12,4},{25,17},{29,21},{17,9}... | collective-permute-start | bytes 2359304 | tf_op jit(solution)/shard_map/ppermute | solution.py:546
  (75 other events, 1097.8 us)

commit v3 on v0

--- a/solution.py
+++ b/solution.py
@@ -1,15 +1,823 @@
+import functools
 import math
+from types import SimpleNamespace as Names
 
 import jax
 import jax.numpy as jnp
 from jax import lax
+from jax.experimental import pallas as pl
+from jax.experimental.pallas import tpu as pltpu
 from jax.sharding import PartitionSpec as P
 
 HEAD_DIM = 128
-
-
+CLIP_MOST = 256
 epsilon = 1e-05
 masked_score = -1e30
+bf16, f32 = jnp.bfloat16, jnp.float32
+VMEM_LIMIT = 60 * 1024 * 1024
+MESH = pl.DeviceIdType.MESH
+WHOLE, VEC = range(2)
+DP, MP = BOTH = ("dp", "mp")
+
+
+def dot(a, b, ca, cb):
+    return lax.dot_general(a, b, (((ca,), (cb,)), ((), ())), preferred_element_type=f32)
+
+
+def shape(dims, kind=bf16):
+    return jax.ShapeDtypeStruct(dims, kind)
+
+
+def call(kernel, args, grid, in_specs, out_specs, outs, *, name, scalars=(), scratch=(), after=(), flops=0, moved=0, **extra):
+    lead = len(scalars) + len(args)
+
+    def body(*refs):
+        kernel(*refs[:lead], *refs[lead + len(after) :])
+
+    return pl.pallas_call(
+        body,
+        grid_spec=pltpu.PrefetchScalarGridSpec(
+            num_scalar_prefetch=len(scalars),
+            grid=grid,
+            in_specs=[*in_specs, *[pl.BlockSpec(memory_space=pl.ANY)] * len(after)],
+            out_specs=out_specs,
+            scratch_shapes=list(scratch),
+        ),
+        out_shape=outs,
+        compiler_params=pltpu.CompilerParams(vmem_limit_bytes=VMEM_LIMIT, **extra),
+        cost_estimate=pl.CostEstimate(flops=flops, bytes_accessed=moved, transcendentals=0),
+        name=name,
+    )(*scalars, *args, *after)
+
+
+def norm_parts(values):
+    centred = values - jnp.mean(values, axis=-1, keepdims=True)
+    spread = jnp.mean(centred * centred, axis=-1, keepdims=True)
+    scale = lax.rsqrt(spread + epsilon)
+    return centred * scale, scale
+
+
+def norm_back(values, gain, grad):
+    unit, scale = norm_parts(values)
+    q = grad * gain
+    back = scale * (
+        q - jnp.mean(q, axis=-1, keepdims=True) - unit * jnp.mean(q * unit, axis=-1, keepdims=True)
+    )
+    return back, jnp.sum(grad * unit, axis=0, keepdims=True)
+
+
+def row_stage(fn, ins, outs, *, name, steps=4):
+    rows, width = ins[0][1].shape
+    tile = rows // steps
+
+    def spec(kind):
+        return pl.BlockSpec((tile, width), lambda i: (i, 0)) if kind == WHOLE else pl.BlockSpec((1, width), lambda i: (0, 0))
+
+    def kernel(*refs):
+        i = pl.program_id(0)
+        for (kind, _), ref, value in zip(outs, refs[len(ins) :], fn(*[r[...] for r in refs[: len(ins)]])):
+            if kind == VEC:
+                value = jnp.where(i == 0, value, ref[...] + value)
+            ref[...] = value.astype(ref.dtype)
+
+    return call(
+        kernel,
+        [v for _, v in ins],
+        (steps,),
+        [spec(k) for k, _ in ins],
+        [spec(k) for k, _ in outs],
+        [shape((rows, width) if k == WHOLE else (1, width), t) for k, t in outs],
+        name=name,
+        flops=20 * rows * width,
+        moved=4 * rows * width * (len(ins) + len(outs)),
+    )
+
+
+def total(values):
+    out = values[0].astype(f32)
+    for v in values[1:]:
+        out = out + v.astype(f32)
+    return out
+
+
+def gelu_both(u):
+    c = math.sqrt(2.0 / math.pi)
+    square = u * u
+    t = jnp.tanh(c * (u + 0.044715 * (u * square)))
+    half = 0.5 * (1.0 + t)
+    value = u * half
+    slope = half + (0.5 * c) * u * (1.0 - t * t) * (1.0 + (3 * 0.044715) * square)
+    return value, slope
+
+
+def allowed_of(seg_col, seg_row, q0, k0, k1, rows):
+    same = seg_col[q0 : q0 + rows, :] == seg_row[:, k0:k1]
+    dims = (rows, k1 - k0)
+    i = lax.broadcasted_iota(jnp.int32, dims, 0) + q0
+    j = lax.broadcasted_iota(jnp.int32, dims, 1) + k0
+    return same & (j <= i)
+
+
+def everyone_kernel(mp, dp, x, out, near, far, sum_, send_near, recv_near, send_far, recv_far):
+    m, d = lax.axis_index(MP), lax.axis_index(DP)
+    barrier = pltpu.get_barrier_semaphore()
+    for r in range(1, mp):
+        pl.semaphore_signal(barrier, inc=1, device_id={MP: lax.rem(m + r, mp)}, device_id_type=MESH)
+    for r in range(1, dp):
+        pl.semaphore_signal(barrier, inc=1, device_id={DP: lax.rem(d + r, dp)}, device_id_type=MESH)
+    pl.semaphore_wait(barrier, mp + dp - 2)
+
+    def exchange(source, slots, me, count, axis, send, recv):
+        copies = []
+        for r in range(1, count):
+            copy = pltpu.make_async_remote_copy(
+                src_ref=source,
+                dst_ref=slots.at[me],
+                send_sem=send.at[r],
+                recv_sem=recv.at[r],
+                device_id={axis: lax.rem(me + r, count)},
+                device_id_type=MESH,
+            )
+            copy.start()
+            copies.append(copy)
+        slots[pl.ds(me, 1)] = source[...][None]
+        for copy in copies:
+            copy.wait()
+        value = slots[0]
+        for r in range(1, count):
+            value = value + slots[r]
+        return value
+
+    sum_[...] = exchange(x, near, m, mp, MP, send_near, recv_near)
+    out[...] = exchange(sum_, far, d, dp, DP, send_far, recv_far)
+
+
+def everyone(x, mp, dp):
+    vmem = pl.BlockSpec(memory_space=pltpu.VMEM)
+    return pl.pallas_call(
+        functools.partial(everyone_kernel, mp, dp),
+        in_specs=[vmem],
+        out_specs=vmem,
+        out_shape=jax.ShapeDtypeStruct(x.shape, f32),
+        scratch_shapes=[
+            pltpu.VMEM((mp, *x.shape), f32),
+            pltpu.VMEM((dp, *x.shape), f32),
+            pltpu.VMEM(x.shape, f32),
+            pltpu.SemaphoreType.DMA((mp,)),
+            pltpu.SemaphoreType.DMA((mp,)),
+            pltpu.SemaphoreType.DMA((dp,)),
+            pltpu.SemaphoreType.DMA((dp,)),
+        ],
+        compiler_params=pltpu.CompilerParams(collective_id=0, has_side_effects=True),
+        name="everyone",
+    )(x)
+
+
+class Wire:
+    def __init__(self, send, recv):
+        self.send, self.recv, self.count, self.ends = send, recv, 0, []
+
+    def slot(self):
+        self.count += 1
+        return self.count - 1
+
+    def copy(self, slot, source, target, to):
+        return pltpu.make_async_remote_copy(
+            src_ref=source,
+            dst_ref=target,
+            send_sem=self.send.at[slot],
+            recv_sem=self.recv.at[slot],
+            device_id=to,
+            device_id_type=MESH,
+        )
+
+    def go(self, source, target, to):
+        copy = self.copy(self.slot(), source, target, to)
+        copy.start()
+        self.ends.append(copy)
+        return copy
+
+    def sent(self, *copies):
+        for copy in copies:
+            copy.wait_send()
+            self.ends = [c for c in self.ends if c is not copy]
+
+    def finish(self):
+        self.sent(*list(self.ends))
+
+
+def stage(body, grid, ins, outs):
+    pltpu.emit_pipeline(
+        body,
+        grid=grid,
+        in_specs=[pl.BlockSpec(b, f) for _, b, f in ins],
+        out_specs=[pl.BlockSpec(b, f) for _, b, f in outs],
+    )(*[r for r, _, _ in ins], *[r for r, _, _ in outs])
+
+
+def layer_kernel(dims, tree, *refs):
+    half, width, columns, units, length = dims
+    full = 2 * half
+    rows = 4 * full
+    r = named(jax.tree.unflatten(tree, refs))
+    m, d = lax.axis_index(MP), lax.axis_index(DP)
+    core, z = lax.rem(d, 2), d // 2
+    parity = lax.rem(m, 2)
+    to_x = {MP: m + 1 - 2 * parity}
+    to_y = {MP: m + 2 - 4 * (m // 2)}
+    to_core = {DP: d + 1 - 2 * core}
+    wire = Wire(r.send, r.recv)
+    heads = columns // HEAD_DIM
+    score_scale = 1.0 / math.sqrt(HEAD_DIM)
+
+    barrier = pltpu.get_barrier_semaphore()
+    for peer in (to_x, to_y, to_core):
+        pl.semaphore_signal(barrier, inc=1, device_id=peer, device_id_type=MESH)
+    for step in (1, -1):
+
+        @pl.when((z + step >= 0) & (z + step < 4))
+        def _():
+            pl.semaphore_signal(barrier, inc=1, device_id={DP: d + 2 * step}, device_id_type=MESH)
+
+    pl.semaphore_wait(barrier, jnp.where((z == 0) | (z == 3), 4, 5))
+
+    def at(ref, block):
+        return ref.at[pl.ds(block * half, half)]
+
+    qkv_w = r.qkv_w
+    loads = [
+        pltpu.make_async_copy(w, qkv_w.at[:, pl.ds(i * columns, columns)], r.load.at[i])
+        for i, w in enumerate((r.query_weight, r.key_weight, r.value_weight))
+    ]
+    for load in loads:
+        load.start()
+
+    tile = half // 2
+
+    def row_ins(*values):
+        out = []
+        for v in values:
+            ref, f = v if isinstance(v, tuple) else (v, lambda i: (i, 0))
+            out.append((ref, (1 if ref.shape[0] == 1 else tile, width), (lambda i: (0, 0)) if ref.shape[0] == 1 else f))
+        return out
+
+    def row_wise(fn, ins, outs):
+        n = len(ins)
+
+        def body(*refs):
+            for ref, value in zip(refs[n:], fn(*[x[...] for x in refs[:n]])):
+                ref[...] = value.astype(ref.dtype)
+
+        stage(body, (4,), row_ins(*ins), row_ins(*outs))
+
+    def spread(ref):
+        return {
+            2: wire.go(at(ref, 0), at(ref, 2), to_x),
+            5: wire.go(at(ref, 1), at(ref, 5), to_y),
+            3: wire.go(at(ref, 1), at(ref, 3), to_x),
+            4: wire.go(at(ref, 0), at(ref, 4), to_y),
+        }
+
+    def relay(ref):
+        return {6: wire.go(at(ref, 2), at(ref, 6), to_y), 7: wire.go(at(ref, 5), at(ref, 7), to_x)}
+
+    def send_far(into, terms):
+        return [wire.go(at(terms, 6), at(into.far, 0), to_x), wire.go(at(terms, 7), at(into.far, 1), to_y)]
+
+    def send_early(into, terms):
+        return [wire.go(at(terms, 2), at(into.early, 0), to_x), wire.go(at(terms, 5), at(into.early, 1), to_y)]
+
+    def send_late(into, terms, far, sums):
+        for copy in far:
+            copy.wait_recv()
+        row_wise(
+            lambda a, b: (a.astype(f32) + b.astype(f32),),
+            [(terms, lambda i: (jnp.where(i < 2, 8 + i, 4 + i), 0)), into.far],
+            [sums],
+        )
+        return [wire.go(at(sums, 0), at(into.late, 0), to_y), wire.go(at(sums, 1), at(into.late, 1), to_x)]
+
+    def arrive(*copies):
+        for copy in copies:
+            copy.wait_recv()
+
+    def product(source, target, blocks, weight, size, count, trans=False, scale=None):
+        n = len(blocks)
+        depth = source.shape[1]
+        ref, ref_block, ref_map = weight if isinstance(weight, tuple) else (None, None, None)
+
+        def body(*refs):
+            j = pl.program_id(0)
+            x = jnp.concatenate([b[...] for b in refs[:n]], axis=0) if n > 1 else refs[0][...]
+            w = refs[n][...] if ref is not None else weight(j)
+            acc = dot(x, w, 1, 1 if trans else 0)
+            if scale is not None:
+                acc = acc * scale(j)
+            for i, out in enumerate(refs[-n:]):
+                out[...] = acc[i * half : (i + 1) * half].astype(bf16)
+
+        stage(
+            body,
+            (count,),
+            [(source, (half, depth), lambda j, b=b: (b, 0)) for b in blocks]
+            + ([(ref, ref_block, ref_map)] if ref is not None else []),
+            [(target, (half, size), lambda j, b=b: (b, j)) for b in blocks],
+        )
+
+    def project(*blocks):
+        product(
+            r.attn_in,
+            r.qkv,
+            blocks,
+            lambda j: qkv_w[:, pl.ds(pl.multiple_of(j * columns, columns), columns)],
+            columns,
+            3,
+            scale=lambda j: jnp.where(j == 0, score_scale, 1.0),
+        )
+
+    def out_project(*blocks):
+        product(
+            r.context,
+            r.out_terms,
+            blocks,
+            (r.out_weight, (columns, width // 2), lambda j: (0, j)),
+            width // 2,
+            2,
+        )
+
+    def context_back(*blocks):
+        product(
+            r.middle_all,
+            r.context_grad,
+            blocks,
+            (r.out_weight, (columns // 2, width), lambda j: (j, 0)),
+            columns // 2,
+            2,
+            trans=True,
+        )
+
+    def project_back(*blocks):
+        size = width // 4
+        product(
+            r.qkv_grad,
+            r.out_terms,
+            blocks,
+            lambda j: qkv_w[pl.ds(pl.multiple_of(j * size, size), size), :],
+            size,
+            4,
+            trans=True,
+        )
+
+    def turn(block, target):
+        for b in range(2):
+            to = pl.multiple_of(lax.rem(parity + b, 2) * full, full)
+            target[pl.ds(to, full), :] = block[b * full : (b + 1) * full, :]
+
+    def turn_back(source, block):
+        for b in range(2):
+            come = pl.multiple_of(lax.rem(parity + b, 2) * full, full)
+            block[b * full : (b + 1) * full, :] = source[pl.ds(come, full), :].astype(bf16)
+
+    q, k, v, c = r.q, r.k, r.v, r.c
+    f0, f1, f2 = r.f0, r.f1, r.f2
+
+    def head_ins(s):
+        ins = [
+            (r.seg_col, (1, length, 1), lambda h: (s, 0, 0)),
+            (r.seg_row, (1, 1, length), lambda h: (s, 0, 0)),
+        ]
+        for which in range(3):
+            ins.append((r.qkv, (length, HEAD_DIM), lambda h, w=which: (s, w * heads + h)))
+        return ins
+
+    def scores_of(seg_col, seg_row, q0, k0, k1):
+        s = dot(q[q0:k1, :], k[k0:k1, :], 1, 1)
+        keep = allowed_of(seg_col.at[0], seg_row.at[0], q0, k0, k1, CLIP_MOST)
+        s = jnp.where(keep, s, masked_score)
+        e = jnp.exp(s - jnp.max(s, axis=-1, keepdims=True))
+        return e * (1.0 / jnp.sum(e, axis=-1, keepdims=True))
+
+    def attend(s):
+        def body(seg_col, seg_row, q_in, k_in, v_in, out):
+            turn(q_in, q)
+            turn(k_in, k)
+            turn(v_in, v)
+            for q0 in range(0, length, CLIP_MOST):
+                k0, k1 = max(0, q0 - CLIP_MOST), q0 + CLIP_MOST
+                p = scores_of(seg_col, seg_row, q0, k0, k1).astype(bf16)
+                f0[q0:k1, :] = dot(p, v[k0:k1, :], 1, 0)
+            turn_back(f0, out)
+
+        stage(body, (heads,), head_ins(s), [(r.context, (length, HEAD_DIM), lambda h: (s, h))])
+
+    def attend_back(s):
+        def body(seg_col, seg_row, q_in, k_in, v_in, c_in, dq_out, dk_out, dv_out):
+            turn(q_in, q)
+            turn(k_in, k)
+            turn(v_in, v)
+            turn(c_in, c)
+            for q0 in range(0, length, CLIP_MOST):
+                k0, k1 = max(0, q0 - CLIP_MOST), q0 + CLIP_MOST
+                p = scores_of(seg_col, seg_row, q0, k0, k1)
+                qb, cb, kb, vb = q[q0:k1, :], c[q0:k1, :], k[k0:k1, :], v[k0:k1, :]
+                dp = dot(cb, vb, 1, 1)
+                inner = jnp.sum(p * dp, axis=-1, keepdims=True)
+                ds = (p * (dp - inner)).astype(bf16)
+                f0[q0:k1, :] = dot(ds, kb, 1, 0) * score_scale
+                dk, dv = dot(ds, qb, 0, 0), dot(p.astype(bf16), cb, 0, 0)
+                if q0 > 0:
+                    f1[k0:q0, :] += dk[:CLIP_MOST]
+                    f2[k0:q0, :] += dv[:CLIP_MOST]
+                    dk, dv = dk[CLIP_MOST:], dv[CLIP_MOST:]
+                f1[q0:k1, :] = dk
+                f2[q0:k1, :] = dv
+            turn_back(f0, dq_out)
+            turn_back(f1, dk_out)
+            turn_back(f2, dv_out)
+
+        stage(
+            body,
+            (heads,),
+            [*head_ins(s), (r.context_grad, (length, HEAD_DIM), lambda h: (s, h))],
+            [(r.qkv_grad, (length, HEAD_DIM), lambda h, w=w: (s, w * heads + h)) for w in range(3)],
+        )
+
+    acc_y, acc_g = r.acc_y, r.acc_g
+
+    def feed(a, b):
+        size = 512
+        tiles = units // size
+
+        def body(x0, x1, c0, c1, up, down, h0, h1, p0, p1, y0, y1, g0, g1):
+            j = pl.program_id(0)
+            x = jnp.concatenate([x0[...], x1[...]], axis=0)
+            cot = jnp.concatenate([c0[...], c1[...]], axis=0)
+            value, slope = gelu_both(dot(x, up[...], 1, 0))
+            value = value.astype(bf16)
+            h0[...], h1[...] = value[:half], value[half:]
+            grad = (dot(cot, down[...], 1, 1) * slope).astype(bf16)
+            p0[...], p1[...] = grad[:half], grad[half:]
+            y = dot(value, down[...], 1, 0)
+            g = dot(grad, up[...], 1, 1)
+
+            @pl.when(j == 0)
+            def _():
+                acc_y[...] = y
+                acc_g[...] = g
+
+            @pl.when((j > 0) & (j < tiles - 1))
+            def _():
+                acc_y[...] += y
+                acc_g[...] += g
+
+            @pl.when(j == tiles - 1)
+            def _():
+                last_y, last_g = acc_y[...] + y, acc_g[...] + g
+                y0[...], y1[...] = last_y[:half].astype(bf16), last_y[half:].astype(bf16)
+                g0[...], g1[...] = last_g[:half].astype(bf16), last_g[half:].astype(bf16)
+
+        both = (a, b)
+        whole = lambda ref: [(ref, (half, width), lambda j, i=i: (i, 0)) for i in both]
+        part = lambda ref: [(ref, (half, size), lambda j, i=i: (i, j)) for i in both]
+        stage(
+            body,
+            (tiles,),
+            [
+                *whole(r.mlp_in),
+                *whole(r.cot_all),
+                (r.up_weight, (width, size), lambda j: (0, j)),
+                (r.down_weight, (size, width), lambda j: (j, 0)),
+            ],
+            [*part(r.hidden), *part(r.pre_grad), *whole(r.mlp_terms), *whole(r.mid_terms)],
+        )
+
+    def grad_product(left, right, which, target, plus=None):
+        share = left.shape[1] // 8
+        size = min(1024, right.shape[1]) if right.shape[1] % 1024 == 0 else right.shape[1] // (2 if right.shape[1] > 512 else 1)
+
+        def body(a, b, *rest):
+            acc = dot(a[...], b[...], 0, 0)
+            if plus is not None:
+                acc = acc + rest[0][0].astype(f32)
+            rest[-1][0] = acc.astype(bf16)
+
+        block = (1, share, size)
+        place = lambda n, s: (s, 0, n)
+        stage(
+            body,
+            (right.shape[1] // size, 4),
+            [
+                (left, (rows, share), lambda n, s: (0, 2 * s + which)),
+                (right, (rows, size), lambda n, s: (0, n)),
+                *([(plus, block, place)] if plus is not None else []),
+            ],
+            [(target, block, place)],
+        )
+
+    def grad_first(into, left, right):
+        grad_product(left, right, 1 - core, into.mine)
+        return wire.go(into.mine, into.got, to_core)
+
+    def line(mine, got, sums, step, place):
+        pick = lambda at: jnp.clip(at if step > 0 else 3 - at, 0, 3)
+        slots = [wire.slot() for _ in range(3)]
+        to = {DP: jnp.clip(d + 2 * step, 0, 7)}
+
+        def copy(t, source):
+            return wire.copy(slots[t], source, got.at[t], to)
+
+        @pl.when(place == 0)
+        def _():
+            for t in range(3):
+                copy(t, mine.at[pick(3 - t)]).start()
+
+        def forward(t):
+            @pl.when((place >= 1) & (place <= t + 1))
+            def _():
+                copy(t, mine.at[0]).wait_recv()
+                n = mine.shape[2]
+                size = mine.shape[1] // 2
+
+                def body(a, b, out):
+                    out[...] = (a[0].astype(f32) + b[...].astype(f32)).astype(bf16)
+
+                stage(
+                    body,
+                    (2,),
+                    [
+                        (mine, (1, size, n), lambda i: (pick(place + 2 - t), i, 0)),
+                        (got.at[t], (size, n), lambda i: (i, 0)),
+                    ],
+                    [(sums.at[t], (size, n), lambda i: (i, 0))],
+                )
+                copy(t + 1, sums.at[t]).start()
+
+        def end():
+            @pl.when(place >= 1)
+            def _():
+                copy(2, mine.at[0]).wait_recv()
+
+            for t in range(3):
+
+                @pl.when((place <= t) & (place < 3))
+                def _():
+                    copy(t, mine.at[0]).wait_send()
+
+        return forward, end
+
+    def grad_second(into, left, right, swap):
+        swap.wait_recv()
+        wire.sent(swap)
+        grad_product(left, right, core, into.mine, into.got)
+        up = line(into.mine, into.right, into.right_sums, 1, z)
+        down = line(into.mine, into.left, into.left_sums, -1, 3 - z)
+
+        def forward(t):
+            up[0](t)
+            down[0](t)
+
+        def end():
+            up[1]()
+            down[1]()
+
+        return forward, end
+
+    attn_in, cot_all, mlp_in, middle_all = r.attn_in, r.cot_all, r.mlp_in, r.middle_all
+    row_wise(
+        lambda x, g: (norm_parts(x.astype(f32))[0] * g,), [r.tokens, r.attn_gain], [attn_in]
+    )
+    near = spread(attn_in)
+    row_wise(lambda x: (x,), [r.out_cotangent], [cot_all])
+    for load in loads:
+        load.wait()
+    project(0, 1)
+    arrive(near[2], near[5])
+    far = relay(attn_in)
+    arrive(near[3], near[4])
+    cot_near = {2: wire.go(at(cot_all, 0), at(cot_all, 2), to_x), 5: wire.go(at(cot_all, 1), at(cot_all, 5), to_y)}
+    project(2, 3, 4, 5)
+    attend(0)
+    arrive(far[6], far[7])
+    project(6, 7)
+    attend(1)
+    out_terms = r.out_terms
+    out_project(6, 7)
+    attn_far = send_far(r.attn, out_terms)
+    out_project(2, 3, 4, 5)
+    attn_early = send_early(r.attn, out_terms)
+    out_project(0, 1)
+    attn_late = send_late(r.attn, out_terms, attn_far, r.sums_a)
+    cot_near[3] = wire.go(at(cot_all, 1), at(cot_all, 3), to_x)
+    cot_near[4] = wire.go(at(cot_all, 0), at(cot_all, 4), to_y)
+    arrive(*attn_early, *attn_late)
+
+    def second(x, g, a, b, c_):
+        mid = x.astype(f32) + a.astype(f32) + b.astype(f32) + c_.astype(f32)
+        return mid, norm_parts(mid)[0] * g
+
+    row_wise(
+        second,
+        [r.tokens, r.mlp_gain, out_terms, r.attn.early, r.attn.late],
+        [r.residual_mid, mlp_in],
+    )
+    near = spread(mlp_in)
+    arrive(cot_near[2], cot_near[5])
+    cot_far = relay(cot_all)
+    feed(0, 1)
+    arrive(near[2], near[5])
+    far = relay(mlp_in)
+    feed(2, 5)
+    mid_terms = r.mid_terms
+    mid_early = send_early(r.mid, mid_terms)
+    arrive(near[3], near[4], cot_near[3], cot_near[4])
+    feed(3, 4)
+    arrive(far[6], far[7], cot_far[6], cot_far[7])
+    feed(6, 7)
+    mid_far = send_far(r.mid, mid_terms)
+    swap = grad_first(r.down_grad, cot_all, r.hidden)
+    mid_late = send_late(r.mid, mid_terms, mid_far, r.sums_b)
+    down_forward, down_end = grad_second(r.down_grad, cot_all, r.hidden, swap)
+    arrive(*mid_early, *mid_late)
+    gain_sum = r.mlp_gain_grad
+    gain_sum[...] = jnp.zeros_like(gain_sum)
+
+    def second_back(mid, g, cot, a, b, c_):
+        back, gain = norm_back(mid, g, a.astype(f32) + b.astype(f32) + c_.astype(f32))
+        gain_sum[...] += gain
+        value = cot.astype(f32) + back
+        return value, value
+
+    row_wise(
+        second_back,
+        [r.residual_mid, r.mlp_gain, r.out_cotangent, mid_terms, r.mid.early, r.mid.late],
+        [r.middle, middle_all],
+    )
+    near = spread(middle_all)
+    swap = grad_first(r.up_grad, mlp_in, r.pre_grad)
+    arrive(near[2], near[5])
+    far = relay(middle_all)
+    down_forward(0)
+    up_forward, up_end = grad_second(r.up_grad, mlp_in, r.pre_grad, swap)
+
+    context_back(0, 1)
+    arrive(near[3], near[4])
+    down_forward(1)
+    context_back(2, 3, 4, 5)
+    attend_back(0)
+    arrive(far[6], far[7])
+    mlp_terms = r.mlp_terms
+    mlp_far = send_far(r.mlp, mlp_terms)
+    context_back(6, 7)
+    up_forward(0)
+    attend_back(1)
+    wire.sent(*attn_far, *attn_early)
+    project_back(6, 7)
+    back_far = send_far(r.back, out_terms)
+    swap = grad_first(r.qkv_w_grad, attn_in, r.qkv_grad)
+    project_back(2, 3, 4, 5)
+    back_early = send_early(r.back, out_terms)
+    up_forward(1)
+    qkv_forward, qkv_end = grad_second(r.qkv_w_grad, attn_in, r.qkv_grad, swap)
+    wire.sent(*mid_late)
+    back_late = send_late(r.back, out_terms, back_far, r.sums_b)
+    mlp_early = send_early(r.mlp, mlp_terms)
+    swap = grad_first(r.out_grad, middle_all, r.context)
+    wire.sent(*attn_late)
+    mlp_late = send_late(r.mlp, mlp_terms, mlp_far, r.sums_a)
+    project_back(0, 1)
+    out_forward, out_end = grad_second(r.out_grad, middle_all, r.context, swap)
+    qkv_forward(0)
+    qkv_forward(1)
+    out_forward(0)
+    out_forward(1)
+    arrive(*back_early, *back_late, *mlp_early, *mlp_late)
+    down_end()
+    up_end()
+    qkv_end()
+    out_end()
+    wire.finish()
+
+
+def named(tree):
+    return Names(**{k: named(v) for k, v in tree.items()}) if isinstance(tree, dict) else tree
+
+
+def layer(ins, half, width, columns, units, length):
+    full, rows = 2 * half, 8 * half
+    share = width // 8
+    big, own = shape((rows, width)), shape((full, width))
+    arrivals = dict(far=own, early=own, late=own)
+
+    def grad(n):
+        line, sums = shape((3, share, n)), shape((2, share, n))
+        stack = shape((4, share, n))
+        return dict(mine=stack, got=stack, right=line, left=line, right_sums=sums, left_sums=sums)
+
+    outs = dict(
+        attn_in=big,
+        cot_all=big,
+        mlp_in=big,
+        middle_all=big,
+        out_terms=big,
+        mlp_terms=big,
+        mid_terms=big,
+        hidden=shape((rows, units)),
+        pre_grad=shape((rows, units)),
+        qkv=shape((rows, 3 * columns)),
+        qkv_grad=shape((rows, 3 * columns)),
+        context=shape((rows, columns)),
+        context_grad=shape((rows, columns)),
+        attn=arrivals,
+        mid=arrivals,
+        mlp=arrivals,
+        back=arrivals,
+        sums_a=own,
+        sums_b=own,
+        down_grad=grad(units),
+        up_grad=grad(units),
+        qkv_w_grad=grad(3 * columns),
+        out_grad=grad(columns),
+        residual_mid=shape((full, width), f32),
+        middle=shape((full, width), f32),
+    )
+    any_, vmem = pl.BlockSpec(memory_space=pl.ANY), pl.BlockSpec(memory_space=pltpu.VMEM)
+    places = dict(jax.tree.map(lambda _: any_, outs), mlp_gain_grad=vmem)
+    outs = dict(outs, mlp_gain_grad=shape((1, width), f32))
+    head, head_sum = pltpu.VMEM((length, HEAD_DIM), bf16), pltpu.VMEM((length, HEAD_DIM), f32)
+    acc = pltpu.VMEM((full, width), f32)
+    scratch = dict(
+        qkv_w=pltpu.VMEM((width, 3 * columns), bf16),
+        acc_y=acc,
+        acc_g=acc,
+        q=head,
+        k=head,
+        v=head,
+        c=head,
+        f0=head_sum,
+        f1=head_sum,
+        f2=head_sum,
+        send=pltpu.SemaphoreType.DMA((96,)),
+        recv=pltpu.SemaphoreType.DMA((96,)),
+        load=pltpu.SemaphoreType.DMA((3,)),
+    )
+    parts = [jax.tree.flatten(t) for t in (ins, outs, scratch)]
+    kinds = [jax.tree.unflatten(t, range(len(v))) for v, t in parts]
+    starts = (0, len(parts[0][0]), len(parts[0][0]) + len(parts[1][0]))
+    place_of = {}
+    for kind, begin in zip(kinds, starts):
+        place_of.update(jax.tree.map(lambda i, b=begin: b + i, kind))
+    order, tree = jax.tree.flatten(place_of)
+
+    def kernel(*refs):
+        layer_kernel((half, width, columns, units, length), tree, *[refs[i] for i in order])
+
+    got = pl.pallas_call(
+        kernel,
+        in_specs=[any_] * len(parts[0][0]),
+        out_specs=jax.tree.leaves(places),
+        out_shape=parts[1][0],
+        scratch_shapes=parts[2][0],
+        compiler_params=pltpu.CompilerParams(
+            collective_id=1, has_side_effects=True, vmem_limit_bytes=VMEM_LIMIT
+        ),
+        name="layer",
+    )(*parts[0][0])
+    return named(jax.tree.unflatten(parts[1][1], got))
+
+
+def share_total(got, z, turned, columns=None):
+    mine, right, left = got.mine, got.right, got.left
+    _, rows, width = mine.shape
+    cuts = columns or [width]
+    tile = 128
+
+    def kernel(place, own, a, b, *outs):
+        value = own[0].astype(f32)
+        value = value + jnp.where(place[0] > 0, a[0].astype(f32), 0.0)
+        value = value + jnp.where(place[0] < 3, b[0].astype(f32), 0.0)
+        if turned:
+            outs[0][...] = value.T
+            return
+        at = 0
+        for out in outs:
+            out[...] = value[:, at : at + out.shape[1]]
+            at += out.shape[1]
+
+    return call(
+        kernel,
+        [mine, right, left],
+        (rows // tile,),
+        [pl.BlockSpec((1, tile, width), lambda i, p: (p[0], i, 0))]
+        + [pl.BlockSpec((1, tile, width), lambda i, p: (2, i, 0))] * 2,
+        [pl.BlockSpec((width, tile), lambda i, p: (0, i))]
+        if turned
+        else [pl.BlockSpec((tile, c), lambda i, p: (i, 0)) for c in cuts],
+        [shape((width, rows), f32)] if turned else [shape((rows, c), f32) for c in cuts],
+        scalars=[z.astype(jnp.int32).reshape(1)],
+        name="share_total",
+        flops=rows * width,
+        moved=rows * width * 10,
+    )
 
 
 def norm_rows(values, gain):
@@ -85,7 +893,7 @@
     )
 
 
-def local(
+def local_plain(
     tokens,
     segment_ids,
     query_weight,
@@ -106,7 +914,7 @@
     flat_shape = (group_rows, head_count * HEAD_DIM)
     residual_in = tokens.astype(jnp.float32)
     normed_attn, attn_norm_back = jax.vjp(norm_rows, residual_in, attn_gain)
-    gathered_attn = lax.all_gather(normed_attn.astype(jnp.bfloat16), "mp", axis=0, tiled=True)
+    gathered_attn = lax.all_gather(normed_attn.astype(jnp.bfloat16), MP, axis=0, tiled=True)
     queries = (
         jnp.dot(gathered_attn, query_weight, preferred_element_type=jnp.float32) * score_scale
     ).astype(jnp.bfloat16)
@@ -123,21 +931,21 @@
     context_flat = context.reshape(flat_shape)
     attn_rows = lax.psum_scatter(
         rows_times(context_flat, out_weight).astype(jnp.bfloat16),
-        "mp",
+        MP,
         scatter_dimension=0,
         tiled=True,
     ).astype(jnp.float32)
     residual_mid = residual_in + attn_rows
     normed_mlp, mlp_norm_back = jax.vjp(norm_rows, residual_mid, mlp_gain)
-    gathered_mlp = lax.all_gather(normed_mlp.astype(jnp.bfloat16), "mp", axis=0, tiled=True)
+    gathered_mlp = lax.all_gather(normed_mlp.astype(jnp.bfloat16), MP, axis=0, tiled=True)
     pre_act = jnp.dot(gathered_mlp, up_weight, preferred_element_type=jnp.float32)
     activated, gelu_back = jax.vjp(gelu_tanh, pre_act)
     hidden = activated.astype(jnp.bfloat16)
     mlp_rows = lax.psum_scatter(
-        rows_times(hidden, down_weight).astype(jnp.bfloat16), "mp", scatter_dimension=0, tiled=True
+        rows_times(hidden, down_weight).astype(jnp.bfloat16), MP, scatter_dimension=0, tiled=True
     ).astype(jnp.float32)
     layer_output = (residual_mid + mlp_rows).astype(jnp.bfloat16)
-    cotangent_all = lax.all_gather(out_cotangent, "mp", axis=0, tiled=True)
+    cotangent_all = lax.all_gather(out_cotangent, MP, axis=0, tiled=True)
     down_weight_grad = jnp.einsum(
         "rf,rd->fd", hidden, cotangent_all, preferred_element_type=jnp.float32
     )
@@ -150,13 +958,13 @@
     )
     normed_mlp_grad = lax.psum_scatter(
         rows_times_back(pre_grad, up_weight).astype(jnp.bfloat16),
-        "mp",
+        MP,
         scatter_dimension=0,
         tiled=True,
     ).astype(jnp.float32)
     middle_back, mlp_gain_grad = mlp_norm_back(normed_mlp_grad)
     middle_grad = out_cotangent.astype(jnp.float32) + middle_back
-    middle_all_grad = lax.all_gather(middle_grad.astype(jnp.bfloat16), "mp", axis=0, tiled=True)
+    middle_all_grad = lax.all_gather(middle_grad.astype(jnp.bfloat16), MP, axis=0, tiled=True)
     out_weight_grad = jnp.einsum(
         "rc,rd->cd", context_flat, middle_all_grad, preferred_element_type=jnp.float32
     )
@@ -190,13 +998,13 @@
             value_weight,
             score_scale,
         ).astype(jnp.bfloat16),
-        "mp",
+        MP,
         scatter_dimension=0,
         tiled=True,
     ).astype(jnp.float32)
     token_back, attn_gain_grad = attn_norm_back(normed_attn_grad)
     tokens_grad = middle_grad + token_back
-    attn_gain_grad, mlp_gain_grad = lax.psum((attn_gain_grad, mlp_gain_grad), ("dp", "mp"))
+    attn_gain_grad, mlp_gain_grad = lax.psum((attn_gain_grad, mlp_gain_grad), (DP, MP))
     (
         query_weight_grad,
         key_weight_grad,
@@ -206,22 +1014,22 @@
         down_weight_grad,
     ) = (
         lax.psum_scatter(
-            query_weight_grad.astype(jnp.bfloat16), "dp", scatter_dimension=0, tiled=True
+            query_weight_grad.astype(jnp.bfloat16), DP, scatter_dimension=0, tiled=True
         ).astype(jnp.float32),
         lax.psum_scatter(
-            key_weight_grad.astype(jnp.bfloat16), "dp", scatter_dimension=0, tiled=True
+            key_weight_grad.astype(jnp.bfloat16), DP, scatter_dimension=0, tiled=True
         ).astype(jnp.float32),
         lax.psum_scatter(
-            value_weight_grad.astype(jnp.bfloat16), "dp", scatter_dimension=0, tiled=True
+            value_weight_grad.astype(jnp.bfloat16), DP, scatter_dimension=0, tiled=True
         ).astype(jnp.float32),
         lax.psum_scatter(
-            out_weight_grad.astype(jnp.bfloat16), "dp", scatter_dimension=1, tiled=True
+            out_weight_grad.astype(jnp.bfloat16), DP, scatter_dimension=1, tiled=True
         ).astype(jnp.float32),
         lax.psum_scatter(
-            up_weight_grad.astype(jnp.bfloat16), "dp", scatter_dimension=0, tiled=True
+            up_weight_grad.astype(jnp.bfloat16), DP, scatter_dimension=0, tiled=True
         ).astype(jnp.float32),
         lax.psum_scatter(
-            down_weight_grad.astype(jnp.bfloat16), "dp", scatter_dimension=1, tiled=True
+            down_weight_grad.astype(jnp.bfloat16), DP, scatter_dimension=1, tiled=True
         ).astype(jnp.float32),
     )
     return (
@@ -238,32 +1046,101 @@
     )
 
 
+def local(
+    mp,
+    dp,
+    tokens,
+    segment_ids,
+    query_weight,
+    key_weight,
+    value_weight,
+    out_weight,
+    up_weight,
+    down_weight,
+    attn_gain,
+    mlp_gain,
+    out_cotangent,
+):
+    width, columns = query_weight.shape
+    length = segment_ids.shape[1]
+    half = tokens.shape[0] // 2
+    z = lax.axis_index(DP) // 2
+    attn_gain, mlp_gain = attn_gain.reshape(1, width), mlp_gain.reshape(1, width)
+    flip = lax.axis_index(MP) // 2
+    segs = jnp.where(flip == 0, segment_ids, segment_ids[::-1])
+    got = layer(
+        dict(
+            tokens=tokens,
+            seg_col=segs.reshape(2, length, 1),
+            seg_row=segs.reshape(2, 1, length),
+            query_weight=query_weight,
+            key_weight=key_weight,
+            value_weight=value_weight,
+            out_weight=out_weight,
+            up_weight=up_weight,
+            down_weight=down_weight,
+            attn_gain=attn_gain,
+            mlp_gain=mlp_gain,
+            out_cotangent=out_cotangent,
+        ),
+        half,
+        width,
+        columns,
+        up_weight.shape[1],
+        length,
+    )
+
+    def own_terms(terms, more):
+        return [(WHOLE, terms), (WHOLE, more.early), (WHOLE, more.late)]
+
+    tokens_grad, attn_gain_grad = row_stage(
+        lambda v, m, g, *t: (lambda b: (m + b[0], b[1]))(norm_back(v.astype(f32), g, total(t))),
+        [(WHOLE, tokens), (WHOLE, got.middle), (VEC, attn_gain), *own_terms(got.out_terms, got.back)],
+        [(WHOLE, f32), (VEC, f32)],
+        name="norm_first_back",
+    )
+    gains = jnp.concatenate([attn_gain_grad, got.mlp_gain_grad], axis=0).reshape(8, width // 4)
+    gains = everyone(gains, mp, dp).reshape(2, width)
+    (layer_output,) = row_stage(
+        lambda m, *t: (m + total(t),),
+        [(WHOLE, got.residual_mid), *own_terms(got.mlp_terms, got.mlp)],
+        [(WHOLE, bf16)],
+        name="output",
+    )
+    qkv_grads = share_total(got.qkv_w_grad, z, False, [columns] * 3)
+    out_grad = share_total(got.out_grad, z, True)[0]
+    up_grad = share_total(got.up_grad, z, False)[0]
+    down_grad = share_total(got.down_grad, z, True)[0]
+    return (layer_output, tokens_grad, *qkv_grads, out_grad, up_grad, down_grad, gains[0], gains[1])
+
+
 def solution(mesh):
+    mp, dp = mesh.shape[MP], mesh.shape[DP]
     return jax.shard_map(
-        local,
+        functools.partial(local, mp, dp) if (mp, dp) == (4, 8) else local_plain,
         mesh=mesh,
         in_specs=(
-            P(("dp", "mp"), None),
-            P("dp", None),
-            P(None, "mp"),
-            P(None, "mp"),
-            P(None, "mp"),
-            P("mp", None),
-            P(None, "mp"),
-            P("mp", None),
+            P(BOTH, None),
+            P(DP, None),
+            P(None, MP),
+            P(None, MP),
+            P(None, MP),
+            P(MP, None),
+            P(None, MP),
+            P(MP, None),
             P(),
             P(),
-            P(("dp", "mp"), None),
+            P(BOTH, None),
         ),
         out_specs=(
-            P(("dp", "mp"), None),
-            P(("dp", "mp"), None),
-            P("dp", "mp"),
-            P("dp", "mp"),
-            P("dp", "mp"),
-            P("mp", "dp"),
-            P("dp", "mp"),
-            P("mp", "dp"),
+            P(BOTH, None),
+            P(BOTH, None),
+            P(DP, MP),
+            P(DP, MP),
+            P(DP, MP),
+            P(MP, DP),
+            P(DP, MP),
+            P(MP, DP),
             P(),
             P(),
         ),

time: 1110 us -> 562 us (0.51)
  waiting for transfers between devices: 616 us -> 0 us
  Pallas kernels: 0 us -> 542 us
  matrix products: 285 us -> 0 us
  local copies, waits for them, and re-layouts: 78.1 us -> 6.53 us
  other arithmetic: 71.6 us -> 1.42 us
  blocking collectives: 39.5 us -> 0 us
  between operations: 14.6 us -> 1.19 us
    pallas_call x0 -> x8, Pallas kernels: none -> 542 us  [the longest x1 509 us: layer(): pl.pallas_call(kernel, in_specs=[any_] * len(parts[0][0]), out_specs=jax....]
    reduce_scatter x10 -> x0, waiting for transfers between devices: 394 us -> none  [the longest x1 70 us: local(): lax.psum_scatter(attn_input_back(queries_grad, keys_grad, values_grad, qu...]
    dot_general x32 -> x0, matrix products: 285 us -> none  [the longest x4 51.6 us: rows_times_back(): lax.dot_general(left_rows, right_matrix, (((1,), (1,)), ((), ())), prefer...]
    all_gather x4 -> x0, waiting for transfers between devices: 221 us -> none  [the longest x1 73 us: local(): lax.all_gather(normed_attn.astype(jnp.bfloat16), 'mp', axis=0, tiled=True)]
    convert_element_type x11 -> x0, other arithmetic: 40.1 us -> none  [the longest x2 22.3 us: attend_backward(): scores_grad = (attn_probs * (probs_grad - inner_sum)).astype(jnp.bfloat16)]
    psum x1 -> x0, blocking collectives: 39.5 us -> none  [local(): lax.psum((attn_gain_grad, mlp_gain_grad), ('dp', 'mp'))]
    dynamic_update_slice x14 -> x0, local copies, waits for them, and re-layouts: 27.5 us -> none  [local(): lax.map(attend_forward, (queries_seq, keys_seq, values_seq, segment_ids))]
    reduce_sum x10 -> x0, other arithmetic: 24.7 us -> none  [the longest x3 8.71 us: norm_rows(): return centred * lax.rsqrt(spread + epsilon) * gain]
  transfers between devices with their start and end apart: 14 -> 0, of which waited for: 12 -> 0; matrix products, arithmetic and copies ran while one was open for 25% -> 0% of each run, Pallas kernels for 0% -> 0%
where the time goes in v3:
time: 562 us; the launch traced here: 551 us
  Pallas kernels  542 us (96%)
  local copies, waits for them, and re-layouts  6.53 us (1%)
    pallas_call x1, Pallas kernels, layer(): pl.pallas_call(kernel, in_specs=[any_] * len(parts[0][0]), out_specs=jax....  509 us
    pallas_call x6, Pallas kernels, call(): pl.pallas_call(body, grid_spec=pltpu.PrefetchScalarGridSpec(num_scalar_pr...  23 us

profile of v3, /device:TPU:0, one launch (start us, length us, event | category | flops | bytes accessed | tf_op | source)
XLA Modules:
  0.0 551.3 jit_solution(725693010655094179)
XLA Ops:
  0.7 2.1 rev.3
  2.8 0.7 broadcast_select_fusion
  3.5 0.6 reshape.49.refs_8_
  4.1 1.2 copy.21.refs_7_
  5.3 508.8 %layer.1 = (bf16[384,2048]{1,0:T(8,128)(2,1)}, bf16[384,2048]{1,0:T(8,128)(2,1)}, bf16[384,2048]{1,0:T(8,128)(2,1)}, bf16[1536,2048]{1,0:T(8,128)(2,1)}, bf16[38...) custom-call(f32[1,2048]{1,0:T(1,128)} %bitcast.11, ...), custom_call_target="tpu_custom_call" | custom-call | tf_op jit(solution)/shard_map/layer/pallas_call | solution.py:774
  514.1 5.0 output.1
  519.1 2.1 share_total.5
  521.2 2.5 share_total.4
  523.7 3.1 share_total.6
  526.8 3.1 share_total.7
  529.9 0.0 copy-start
  529.9 7.2 %norm_first_back.1 = (f32[384,2048]{1,0:T(8,128)}, f32[1,2048]{1,0:T(1,128)}) custom-call(bf16[384,2048]{1,0:T(8,128)(2,1)} %refs_0_.1, f32[384,2048]{1,0:T(8,128)} %get-tuple-element.40.refs_1_, f32[1,2048]{1,0:T(1,128)} %bitcast.12, bf16[1536,2048]{1,0:T(8,128)(2,1)} %get-tuple-element.41.refs_3_, bf16[384,2048]{1,0:T(8,128)(2,1)} %get-tuple-element.42.refs_4_, ...), custom_call_target="tpu_custom_call" | custom-call | flops 15728640 | bytes 25165824 | tf_op jit(solution)/shard_map/norm_first_back/pallas_call | solution.py:37
  537.1 0.0 copy-done
  537.1 0.7 pad_maximum_fusion
  537.8 0.6 reshape.51.x
  538.4 10.3 %everyone.1 = f32[8,512]{1,0:T(8,128)} custom-call(f32[8,512]{1,0:T(8,128)} %reshape.51.x), custom_call_target="tpu_custom_call" | custom-call | tf_op jit(solution)/shard_map/everyone/pallas_call | solution.py:157
  548.8 0.8 slice_bitcast_fusion
  549.6 0.6 copy.23
  550.2 0.6 copy.22
Async XLA Ops:
  529.9 7.2 %copy-start = (f32[1,2048]{1,0:T(1,128)S(1)}, f32[1,2048]{1,0:T(1,128)}, u32[]{:S(2)}) copy-start(f32[1,2048]{1,0:T(1,128)} %get-tuple-element.61) | copy-start | bytes 24580

commit v4 on v3

--- a/solution.py
+++ b/solution.py
@@ -66,33 +66,6 @@
     return back, jnp.sum(grad * unit, axis=0, keepdims=True)
 
 
-def row_stage(fn, ins, outs, *, name, steps=4):
-    rows, width = ins[0][1].shape
-    tile = rows // steps
-
-    def spec(kind):
-        return pl.BlockSpec((tile, width), lambda i: (i, 0)) if kind == WHOLE else pl.BlockSpec((1, width), lambda i: (0, 0))
-
-    def kernel(*refs):
-        i = pl.program_id(0)
-        for (kind, _), ref, value in zip(outs, refs[len(ins) :], fn(*[r[...] for r in refs[: len(ins)]])):
-            if kind == VEC:
-                value = jnp.where(i == 0, value, ref[...] + value)
-            ref[...] = value.astype(ref.dtype)
-
-    return call(
-        kernel,
-        [v for _, v in ins],
-        (steps,),
-        [spec(k) for k, _ in ins],
-        [spec(k) for k, _ in outs],
-        [shape((rows, width) if k == WHOLE else (1, width), t) for k, t in outs],
-        name=name,
-        flops=20 * rows * width,
-        moved=4 * rows * width * (len(ins) + len(outs)),
-    )
-
-
 def total(values):
     out = values[0].astype(f32)
     for v in values[1:]:
@@ -116,61 +89,6 @@
     i = lax.broadcasted_iota(jnp.int32, dims, 0) + q0
     j = lax.broadcasted_iota(jnp.int32, dims, 1) + k0
     return same & (j <= i)
-
-
-def everyone_kernel(mp, dp, x, out, near, far, sum_, send_near, recv_near, send_far, recv_far):
-    m, d = lax.axis_index(MP), lax.axis_index(DP)
-    barrier = pltpu.get_barrier_semaphore()
-    for r in range(1, mp):
-        pl.semaphore_signal(barrier, inc=1, device_id={MP: lax.rem(m + r, mp)}, device_id_type=MESH)
-    for r in range(1, dp):
-        pl.semaphore_signal(barrier, inc=1, device_id={DP: lax.rem(d + r, dp)}, device_id_type=MESH)
-    pl.semaphore_wait(barrier, mp + dp - 2)
-
-    def exchange(source, slots, me, count, axis, send, recv):
-        copies = []
-        for r in range(1, count):
-            copy = pltpu.make_async_remote_copy(
-                src_ref=source,
-                dst_ref=slots.at[me],
-                send_sem=send.at[r],
-                recv_sem=recv.at[r],
-                device_id={axis: lax.rem(me + r, count)},
-                device_id_type=MESH,
-            )
-            copy.start()
-            copies.append(copy)
-        slots[pl.ds(me, 1)] = source[...][None]
-        for copy in copies:
-            copy.wait()
-        value = slots[0]
-        for r in range(1, count):
-            value = value + slots[r]
-        return value
-
-    sum_[...] = exchange(x, near, m, mp, MP, send_near, recv_near)
-    out[...] = exchange(sum_, far, d, dp, DP, send_far, recv_far)
-
-
-def everyone(x, mp, dp):
-    vmem = pl.BlockSpec(memory_space=pltpu.VMEM)
-    return pl.pallas_call(
-        functools.partial(everyone_kernel, mp, dp),
-        in_specs=[vmem],
-        out_specs=vmem,
-        out_shape=jax.ShapeDtypeStruct(x.shape, f32),
-        scratch_shapes=[
-            pltpu.VMEM((mp, *x.shape), f32),
-            pltpu.VMEM((dp, *x.shape), f32),
-            pltpu.VMEM(x.shape, f32),
-            pltpu.SemaphoreType.DMA((mp,)),
-            pltpu.SemaphoreType.DMA((mp,)),
-            pltpu.SemaphoreType.DMA((dp,)),
-            pltpu.SemaphoreType.DMA((dp,)),
-        ],
-        compiler_params=pltpu.CompilerParams(collective_id=0, has_side_effects=True),
-        name="everyone",
-    )(x)
 
 
 class Wire:
@@ -231,15 +149,10 @@
     score_scale = 1.0 / math.sqrt(HEAD_DIM)
 
     barrier = pltpu.get_barrier_semaphore()
-    for peer in (to_x, to_y, to_core):
+    others = [{MP: lax.rem(m + i, 4)} for i in range(1, 4)] + [{DP: lax.rem(d + i, 8)} for i in range(1, 8)]
+    for peer in others:
         pl.semaphore_signal(barrier, inc=1, device_id=peer, device_id_type=MESH)
-    for step in (1, -1):
-
-        @pl.when((z + step >= 0) & (z + step < 4))
-        def _():
-            pl.semaphore_signal(barrier, inc=1, device_id={DP: d + 2 * step}, device_id_type=MESH)
-
-    pl.semaphore_wait(barrier, jnp.where((z == 0) | (z == 3), 4, 5))
+    pl.semaphore_wait(barrier, len(others))
 
     def at(ref, block):
         return ref.at[pl.ds(block * half, half)]
@@ -383,8 +296,8 @@
 
     def head_ins(s):
         ins = [
-            (r.seg_col, (1, length, 1), lambda h: (s, 0, 0)),
-            (r.seg_row, (1, 1, length), lambda h: (s, 0, 0)),
+            (r.seg_col, (1, length, 1), lambda h: (lax.rem(m // 2 + s, 2), 0, 0)),
+            (r.seg_row, (1, 1, length), lambda h: (lax.rem(m // 2 + s, 2), 0, 0)),
         ]
         for which in range(3):
             ins.append((r.qkv, (length, HEAD_DIM), lambda h, w=which: (s, w * heads + h)))
@@ -442,73 +355,124 @@
             [(r.qkv_grad, (length, HEAD_DIM), lambda h, w=w: (s, w * heads + h)) for w in range(3)],
         )
 
-    acc_y, acc_g = r.acc_y, r.acc_g
-
-    def feed(a, b):
-        size = 512
-        tiles = units // size
-
-        def body(x0, x1, c0, c1, up, down, h0, h1, p0, p1, y0, y1, g0, g1):
-            j = pl.program_id(0)
-            x = jnp.concatenate([x0[...], x1[...]], axis=0)
-            cot = jnp.concatenate([c0[...], c1[...]], axis=0)
-            value, slope = gelu_both(dot(x, up[...], 1, 0))
+    acc_g, slopes = r.acc_g, r.slopes
+    size = 512
+    tiles = units // size
+    up_tile = (r.up_weight, (width, size), lambda j: (0, j))
+    down_tile = (r.down_weight, (size, width), lambda j: (j, 0))
+
+    def whole(ref, both):
+        return [(ref, (half, width), lambda j, i=i: (i, 0)) for i in both]
+
+    def part(ref, both):
+        return [(ref, (half, size), lambda j, i=i: (i, j)) for i in both]
+
+    def rows_of(a, b):
+        return jnp.concatenate([a[...], b[...]], axis=0)
+
+    def grads_of(grad, up, p0, p1, g0, g1):
+        j = pl.program_id(0)
+        grad = grad.astype(bf16)
+        p0[...], p1[...] = grad[:half], grad[half:]
+        g = dot(grad, up[...], 1, 1)
+
+        @pl.when(j == 0)
+        def _():
+            acc_g[...] = g
+
+        @pl.when((j > 0) & (j < tiles - 1))
+        def _():
+            acc_g[...] += g
+
+        @pl.when(j == tiles - 1)
+        def _():
+            last = acc_g[...] + g
+            g0[...], g1[...] = last[:half].astype(bf16), last[half:].astype(bf16)
+
+    def feed(*both):
+        def body(x0, x1, c0, c1, up, down, h0, h1, *outs):
+            value, slope = gelu_both(dot(rows_of(x0, x1), up[...], 1, 0))
             value = value.astype(bf16)
             h0[...], h1[...] = value[:half], value[half:]
-            grad = (dot(cot, down[...], 1, 1) * slope).astype(bf16)
-            p0[...], p1[...] = grad[:half], grad[half:]
-            y = dot(value, down[...], 1, 0)
-            g = dot(grad, up[...], 1, 1)
-
-            @pl.when(j == 0)
-            def _():
-                acc_y[...] = y
-                acc_g[...] = g
-
-            @pl.when((j > 0) & (j < tiles - 1))
-            def _():
-                acc_y[...] += y
-                acc_g[...] += g
-
-            @pl.when(j == tiles - 1)
-            def _():
-                last_y, last_g = acc_y[...] + y, acc_g[...] + g
-                y0[...], y1[...] = last_y[:half].astype(bf16), last_y[half:].astype(bf16)
-                g0[...], g1[...] = last_g[:half].astype(bf16), last_g[half:].astype(bf16)
-
-        both = (a, b)
-        whole = lambda ref: [(ref, (half, width), lambda j, i=i: (i, 0)) for i in both]
-        part = lambda ref: [(ref, (half, size), lambda j, i=i: (i, j)) for i in both]
+            grads_of(dot(rows_of(c0, c1), down[...], 1, 1) * slope, up, *outs)
+
         stage(
             body,
             (tiles,),
-            [
-                *whole(r.mlp_in),
-                *whole(r.cot_all),
-                (r.up_weight, (width, size), lambda j: (0, j)),
-                (r.down_weight, (size, width), lambda j: (j, 0)),
-            ],
-            [*part(r.hidden), *part(r.pre_grad), *whole(r.mlp_terms), *whole(r.mid_terms)],
+            [*whole(r.mlp_in, both), *whole(r.cot_all, both), up_tile, down_tile],
+            [*part(r.hidden, both), *part(r.pre_grad, both), *whole(r.mid_terms, both)],
+        )
+
+    def feed_forward(*both):
+        def body(x0, x1, up, h0, h1):
+            value, slope = gelu_both(dot(rows_of(x0, x1), up[...], 1, 0))
+            value = value.astype(bf16)
+            h0[...], h1[...] = value[:half], value[half:]
+            slopes[pl.program_id(0)] = slope
+
+        stage(body, (tiles,), [*whole(r.mlp_in, both), up_tile], part(r.hidden, both))
+
+    def feed_back(*both):
+        def body(c0, c1, up, down, *outs):
+            grads_of(dot(rows_of(c0, c1), down[...], 1, 1) * slopes[pl.program_id(0)], up, *outs)
+
+        stage(
+            body,
+            (tiles,),
+            [*whole(r.cot_all, both), up_tile, down_tile],
+            [*part(r.pre_grad, both), *whole(r.mid_terms, both)],
+        )
+
+    down_acc = r.down_acc
+    share = width // 8
+
+    def down_some(first, count, both, target=None, plus=None):
+        begin = 0 in both
+        n = len(both)
+
+        def body(*refs):
+            s = pl.program_id(0)
+            left, right = ([b[...] for b in refs[i * n : (i + 1) * n]] for i in range(2))
+            acc = dot(jnp.concatenate(left, axis=0), jnp.concatenate(right, axis=0), 0, 0)
+            if not begin:
+                acc = acc + down_acc[first + s]
+            if target is None:
+                down_acc[first + s] = acc
+                return
+            if plus is not None:
+                acc = acc + refs[2 * n][0].astype(f32)
+            refs[-1][0] = acc.astype(bf16)
+
+        def column(s):
+            k = first + s
+            return 2 * lax.rem(k, 4) + jnp.where(k < 4, 1 - core, core)
+
+        block = (1, share, units)
+        stage(
+            body,
+            (count,),
+            [(r.cot_all, (half, share), lambda s, i=i: (i, column(s))) for i in both]
+            + [(r.hidden, (half, units), lambda s, i=i: (i, 0)) for i in both]
+            + ([(plus, block, lambda s: (s, 0, 0))] if plus is not None else []),
+            [(target, block, lambda s: (s, 0, 0))] if target is not None else [],
         )
 
     def grad_product(left, right, which, target, plus=None):
-        share = left.shape[1] // 8
-        size = min(1024, right.shape[1]) if right.shape[1] % 1024 == 0 else right.shape[1] // (2 if right.shape[1] > 512 else 1)
-
         def body(a, b, *rest):
             acc = dot(a[...], b[...], 0, 0)
             if plus is not None:
                 acc = acc + rest[0][0].astype(f32)
             rest[-1][0] = acc.astype(bf16)
 
-        block = (1, share, size)
-        place = lambda n, s: (s, 0, n)
+        n = right.shape[1]
+        block = (1, share, n)
+        place = lambda s: (s, 0, 0)
         stage(
             body,
-            (right.shape[1] // size, 4),
+            (4,),
             [
-                (left, (rows, share), lambda n, s: (0, 2 * s + which)),
-                (right, (rows, size), lambda n, s: (0, n)),
+                (left, (rows, share), lambda s: (0, 2 * s + which)),
+                (right, (rows, n), lambda s: (0, 0)),
                 *([(plus, block, place)] if plus is not None else []),
             ],
             [(target, block, place)],
@@ -569,6 +533,9 @@
         swap.wait_recv()
         wire.sent(swap)
         grad_product(left, right, core, into.mine, into.got)
+        return start_line(into)
+
+    def start_line(into):
         up = line(into.mine, into.right, into.right_sums, 1, z)
         down = line(into.mine, into.left, into.left_sums, -1, 3 - z)
 
@@ -576,11 +543,38 @@
             up[0](t)
             down[0](t)
 
-        def end():
+        def end(turned=None):
             up[1]()
             down[1]()
+            if turned is not None:
+                share_total(into, turned)
 
         return forward, end
+
+    def share_total(into, target):
+        turned = target.shape[1] == share
+        n = into.mine.shape[2]
+        tile = 128
+
+        def body(own, right, left, out):
+            value = own[0].astype(f32)
+            value = value + jnp.where(z > 0, right[0].astype(f32), 0.0)
+            value = value + jnp.where(z < 3, left[0].astype(f32), 0.0)
+            out[...] = value.T if turned else value
+
+        block = (1, tile, n)
+        stage(
+            body,
+            (share // tile,),
+            [(into.mine, block, lambda i: (z, i, 0)), (into.right, block, lambda i: (2, i, 0)), (into.left, block, lambda i: (2, i, 0))],
+            [(target, (n, tile), lambda i: (0, i)) if turned else (target, (tile, n), lambda i: (i, 0))],
+        )
+
+    def over_all(slots, value, me, axis, count):
+        copies = [wire.go(value, slots.at[me], {axis: lax.rem(me + i, count)}) for i in range(1, count)]
+        slots[pl.ds(me, 1)] = value[...][None]
+        arrive(*copies)
+        return functools.reduce(lambda a, i: a + slots[i], range(1, count), slots[0])
 
     attn_in, cot_all, mlp_in, middle_all = r.attn_in, r.cot_all, r.mlp_in, r.middle_all
     row_wise(
@@ -622,28 +616,39 @@
     )
     near = spread(mlp_in)
     arrive(cot_near[2], cot_near[5])
-    cot_far = relay(cot_all)
     feed(0, 1)
     arrive(near[2], near[5])
     far = relay(mlp_in)
+    cot_far = relay(cot_all)
     feed(2, 5)
     mid_terms = r.mid_terms
     mid_early = send_early(r.mid, mid_terms)
+    down_some(0, 8, (0, 1, 2, 5))
     arrive(near[3], near[4], cot_near[3], cot_near[4])
     feed(3, 4)
-    arrive(far[6], far[7], cot_far[6], cot_far[7])
-    feed(6, 7)
+    arrive(far[6], far[7])
+    feed_forward(6, 7)
+    arrive(cot_far[6], cot_far[7])
+    down, last = r.down_grad, (3, 4, 6, 7)
+    down_some(0, 4, last, down.mine)
+    swap = wire.go(down.mine, down.got, to_core)
+    arrive(swap)
+    wire.sent(swap)
+    down_some(4, 4, last, down.mine, down.got)
+    down_forward, down_end = start_line(down)
+    feed_back(6, 7)
     mid_far = send_far(r.mid, mid_terms)
-    swap = grad_first(r.down_grad, cot_all, r.hidden)
+    swap = grad_first(r.up_grad, mlp_in, r.pre_grad)
     mid_late = send_late(r.mid, mid_terms, mid_far, r.sums_b)
-    down_forward, down_end = grad_second(r.down_grad, cot_all, r.hidden, swap)
+    up_forward, up_end = grad_second(r.up_grad, mlp_in, r.pre_grad, swap)
+    down_forward(0)
     arrive(*mid_early, *mid_late)
-    gain_sum = r.mlp_gain_grad
+    gain_sum = r.gain_sum
     gain_sum[...] = jnp.zeros_like(gain_sum)
 
     def second_back(mid, g, cot, a, b, c_):
         back, gain = norm_back(mid, g, a.astype(f32) + b.astype(f32) + c_.astype(f32))
-        gain_sum[...] += gain
+        gain_sum[1:2, :] += gain
         value = cot.astype(f32) + back
         return value, value
 
@@ -653,48 +658,70 @@
         [r.middle, middle_all],
     )
     near = spread(middle_all)
-    swap = grad_first(r.up_grad, mlp_in, r.pre_grad)
+
+    mlp_terms = r.mlp_terms
+
+    def down_project(*blocks):
+        product(r.hidden, mlp_terms, blocks, (r.down_weight, (units, size), lambda j: (0, j)), size, width // size)
+
+    context_back(0, 1)
+    down_project(6, 7, 2, 3)
     arrive(near[2], near[5])
     far = relay(middle_all)
-    down_forward(0)
-    up_forward, up_end = grad_second(r.up_grad, mlp_in, r.pre_grad, swap)
-
-    context_back(0, 1)
+    down_project(4, 5, 0, 1)
+    mlp_far = send_far(r.attn, mlp_terms)
     arrive(near[3], near[4])
+    context_back(2, 3, 4, 5)
     down_forward(1)
-    context_back(2, 3, 4, 5)
     attend_back(0)
+    up_forward(0)
     arrive(far[6], far[7])
-    mlp_terms = r.mlp_terms
-    mlp_far = send_far(r.mlp, mlp_terms)
     context_back(6, 7)
-    up_forward(0)
+    swap = grad_first(r.out_grad, middle_all, r.context)
     attend_back(1)
     wire.sent(*attn_far, *attn_early)
     project_back(6, 7)
-    back_far = send_far(r.back, out_terms)
+    back_far = send_far(r.mid, out_terms)
+    out_forward, out_end = grad_second(r.out_grad, middle_all, r.context, swap)
     swap = grad_first(r.qkv_w_grad, attn_in, r.qkv_grad)
     project_back(2, 3, 4, 5)
-    back_early = send_early(r.back, out_terms)
+    back_early = send_early(r.mid, out_terms)
     up_forward(1)
     qkv_forward, qkv_end = grad_second(r.qkv_w_grad, attn_in, r.qkv_grad, swap)
     wire.sent(*mid_late)
-    back_late = send_late(r.back, out_terms, back_far, r.sums_b)
-    mlp_early = send_early(r.mlp, mlp_terms)
-    swap = grad_first(r.out_grad, middle_all, r.context)
+    back_late = send_late(r.mid, out_terms, back_far, r.sums_b)
+    mlp_early = send_early(r.attn, mlp_terms)
     wire.sent(*attn_late)
-    mlp_late = send_late(r.mlp, mlp_terms, mlp_far, r.sums_a)
+    mlp_late = send_late(r.attn, mlp_terms, mlp_far, r.sums_a)
     project_back(0, 1)
-    out_forward, out_end = grad_second(r.out_grad, middle_all, r.context, swap)
+    out_forward(0)
+    down_end(r.down_total)
+    arrive(*back_early, *back_late)
+
+    def first_back(x, mid, g, a, b, c_):
+        back, gain = norm_back(x.astype(f32), g, a.astype(f32) + b.astype(f32) + c_.astype(f32))
+        gain_sum[0:1, :] += gain
+        return (mid + back,)
+
+    row_wise(
+        first_back,
+        [r.tokens, r.middle, r.attn_gain, out_terms, r.mid.early, r.mid.late],
+        [r.tokens_grad],
+    )
     qkv_forward(0)
+    out_forward(1)
+    up_end(r.up_total)
+    r.gain_near_sum[...] = over_all(r.gain_near, gain_sum, m, MP, 4)
+    r.gains[...] = over_all(r.gain_far, r.gain_near_sum, d, DP, 8)
     qkv_forward(1)
-    out_forward(0)
-    out_forward(1)
-    arrive(*back_early, *back_late, *mlp_early, *mlp_late)
-    down_end()
-    up_end()
+    out_end(r.out_total)
+    arrive(*mlp_early, *mlp_late)
+    row_wise(
+        lambda mid, *t: (mid + total(t),),
+        [r.residual_mid, mlp_terms, r.attn.early, r.attn.late],
+        [r.layer_output],
+    )
     qkv_end()
-    out_end()
     wire.finish()
 
 
@@ -729,8 +756,6 @@
         context_grad=shape((rows, columns)),
         attn=arrivals,
         mid=arrivals,
-        mlp=arrivals,
-        back=arrivals,
         sums_a=own,
         sums_b=own,
         down_grad=grad(units),
@@ -739,16 +764,26 @@
         out_grad=grad(columns),
         residual_mid=shape((full, width), f32),
         middle=shape((full, width), f32),
+        layer_output=own,
+        tokens_grad=shape((full, width), f32),
+        down_total=shape((units, share), f32),
+        up_total=shape((share, units), f32),
+        out_total=shape((columns, share), f32),
     )
     any_, vmem = pl.BlockSpec(memory_space=pl.ANY), pl.BlockSpec(memory_space=pltpu.VMEM)
-    places = dict(jax.tree.map(lambda _: any_, outs), mlp_gain_grad=vmem)
-    outs = dict(outs, mlp_gain_grad=shape((1, width), f32))
+    places = dict(jax.tree.map(lambda _: any_, outs), gains=vmem)
+    outs = dict(outs, gains=shape((2, width), f32))
     head, head_sum = pltpu.VMEM((length, HEAD_DIM), bf16), pltpu.VMEM((length, HEAD_DIM), f32)
     acc = pltpu.VMEM((full, width), f32)
     scratch = dict(
         qkv_w=pltpu.VMEM((width, 3 * columns), bf16),
-        acc_y=acc,
         acc_g=acc,
+        slopes=pltpu.VMEM((units // 512, full, 512), f32),
+        down_acc=pltpu.VMEM((8, share, units), f32),
+        gain_sum=pltpu.VMEM((2, width), f32),
+        gain_near_sum=pltpu.VMEM((2, width), f32),
+        gain_near=pltpu.VMEM((4, 2, width), f32),
+        gain_far=pltpu.VMEM((8, 2, width), f32),
         q=head,
         k=head,
         v=head,
@@ -785,19 +820,15 @@
     return named(jax.tree.unflatten(parts[1][1], got))
 
 
-def share_total(got, z, turned, columns=None):
+def share_total(got, z, columns):
     mine, right, left = got.mine, got.right, got.left
     _, rows, width = mine.shape
-    cuts = columns or [width]
     tile = 128
 
     def kernel(place, own, a, b, *outs):
         value = own[0].astype(f32)
         value = value + jnp.where(place[0] > 0, a[0].astype(f32), 0.0)
         value = value + jnp.where(place[0] < 3, b[0].astype(f32), 0.0)
-        if turned:
-            outs[0][...] = value.T
-            return
         at = 0
         for out in outs:
             out[...] = value[:, at : at + out.shape[1]]
@@ -809,10 +840,8 @@
         (rows // tile,),
         [pl.BlockSpec((1, tile, width), lambda i, p: (p[0], i, 0))]
         + [pl.BlockSpec((1, tile, width), lambda i, p: (2, i, 0))] * 2,
-        [pl.BlockSpec((width, tile), lambda i, p: (0, i))]
-        if turned
-        else [pl.BlockSpec((tile, c), lambda i, p: (i, 0)) for c in cuts],
-        [shape((width, rows), f32)] if turned else [shape((rows, c), f32) for c in cuts],
+        [pl.BlockSpec((tile, c), lambda i, p: (i, 0)) for c in columns],
+        [shape((rows, c), f32) for c in columns],
         scalars=[z.astype(jnp.int32).reshape(1)],
         name="share_total",
         flops=rows * width,
@@ -1066,13 +1095,11 @@
     half = tokens.shape[0] // 2
     z = lax.axis_index(DP) // 2
     attn_gain, mlp_gain = attn_gain.reshape(1, width), mlp_gain.reshape(1, width)
-    flip = lax.axis_index(MP) // 2
-    segs = jnp.where(flip == 0, segment_ids, segment_ids[::-1])
     got = layer(
         dict(
             tokens=tokens,
-            seg_col=segs.reshape(2, length, 1),
-            seg_row=segs.reshape(2, 1, length),
+            seg_col=segment_ids.reshape(2, length, 1),
+            seg_row=segment_ids.reshape(2, 1, length),
             query_weight=query_weight,
             key_weight=key_weight,
             value_weight=value_weight,
@@ -1090,28 +1117,17 @@
         length,
     )
 
-    def own_terms(terms, more):
-        return [(WHOLE, terms), (WHOLE, more.early), (WHOLE, more.late)]
-
-    tokens_grad, attn_gain_grad = row_stage(
-        lambda v, m, g, *t: (lambda b: (m + b[0], b[1]))(norm_back(v.astype(f32), g, total(t))),
-        [(WHOLE, tokens), (WHOLE, got.middle), (VEC, attn_gain), *own_terms(got.out_terms, got.back)],
-        [(WHOLE, f32), (VEC, f32)],
-        name="norm_first_back",
-    )
-    gains = jnp.concatenate([attn_gain_grad, got.mlp_gain_grad], axis=0).reshape(8, width // 4)
-    gains = everyone(gains, mp, dp).reshape(2, width)
-    (layer_output,) = row_stage(
-        lambda m, *t: (m + total(t),),
-        [(WHOLE, got.residual_mid), *own_terms(got.mlp_terms, got.mlp)],
-        [(WHOLE, bf16)],
-        name="output",
-    )
-    qkv_grads = share_total(got.qkv_w_grad, z, False, [columns] * 3)
-    out_grad = share_total(got.out_grad, z, True)[0]
-    up_grad = share_total(got.up_grad, z, False)[0]
-    down_grad = share_total(got.down_grad, z, True)[0]
-    return (layer_output, tokens_grad, *qkv_grads, out_grad, up_grad, down_grad, gains[0], gains[1])
+    qkv_grads = share_total(got.qkv_w_grad, z, [columns] * 3)
+    return (
+        got.layer_output,
+        got.tokens_grad,
+        *qkv_grads,
+        got.out_total,
+        got.up_total,
+        got.down_total,
+        got.gains[0],
+        got.gains[1],
+    )
 
 
 def solution(mesh):

time: 562 us -> 546 us (0.972)
  Pallas kernels: 542 us -> 522 us
  local copies, waits for them, and re-layouts: 6.53 us -> 12.4 us
    pallas_call x6 -> x1, Pallas kernels: 23 us -> 2.66 us  [call(): pl.pallas_call(body, grid_spec=pltpu.PrefetchScalarGridSpec(num_scalar_pr...]
    pallas_call x1, Pallas kernels: 509 us -> 520 us  [layer(): pl.pallas_call(kernel, in_specs=[any_] * len(parts[0][0]), out_specs=jax....]
    pallas_call x1 -> x0, Pallas kernels: 10.3 us -> none  [everyone(): pl.pallas_call(functools.partial(everyone_kernel, mp, dp), in_specs=[vmem...]
    unnamed x5 -> x17, local copies, waits for them, and re-layouts: 2.01 us -> 8.6 us
where the time goes in v4:
time: 546 us; the launch traced here: 536 us
  Pallas kernels  522 us (96%)
  local copies, waits for them, and re-layouts  12.4 us (2%)
    pallas_call x1, Pallas kernels, layer(): pl.pallas_call(kernel, in_specs=[any_] * len(parts[0][0]), out_specs=jax....  520 us

profile of v4, /device:TPU:0, one launch (start us, length us, event | category | flops | bytes accessed | tf_op | source)
XLA Modules:
  0.0 535.9 jit_solution(12766432041231966481)
XLA Ops:
  0.6 1.9 copy.21.refs_7_
  2.5 1.3 reshape.38.refs_8_
  3.8 519.8 %layer.1 = (bf16[384,2048]{1,0:T(8,128)(2,1)}, bf16[384,2048]{1,0:T(8,128)(2,1)}, bf16[384,2048]{1,0:T(8,128)(2,1)}, bf16[1536,2048]{1,0:T(8,128)(2,1)}, bf16[15...) custom-call(f32[1,2048]{1,0:T(1,128)} %bitcast.7, ...), custom_call_target="tpu_custom_call" | custom-call | tf_op jit(solution)/shard_map/layer/pallas_call | solution.py:809
  523.6 0.0 copy-start.5
  523.6 0.0 copy-start.3
  523.6 2.7 share_total.1
  526.3 0.0 copy-start
  526.3 0.0 copy-done.5
  526.3 0.6 fusion
  526.9 0.0 copy-done.3
  526.9 1.1 copy.27
  528.0 0.7 copy-done
  528.7 0.0 copy-start.4
  528.7 0.0 copy-start.2
  528.7 1.7 copy.28
  530.4 0.0 copy-done.4
  530.4 0.8 copy.29
  531.2 0.6 copy-done.2
  531.8 0.0 copy-start.1
  531.8 1.3 copy.30
  533.1 1.0 copy-done.1
  534.2 1.3 copy.31
Async XLA Ops:
  523.6 2.7 copy-start.5
  523.6 3.3 copy-start.3
  526.3 2.5 copy-start
  528.7 1.7 copy-start.4
  528.7 3.1 copy-start.2
  531.8 2.3 copy-start.1

commit v5 on v4

--- a/solution.py
+++ b/solution.py
@@ -632,15 +632,20 @@
     down, last = r.down_grad, (3, 4, 6, 7)
     down_some(0, 4, last, down.mine)
     swap = wire.go(down.mine, down.got, to_core)
+    feed_back(6, 7)
+    mid_far = send_far(r.mid, mid_terms)
     arrive(swap)
     wire.sent(swap)
     down_some(4, 4, last, down.mine, down.got)
     down_forward, down_end = start_line(down)
-    feed_back(6, 7)
-    mid_far = send_far(r.mid, mid_terms)
     swap = grad_first(r.up_grad, mlp_in, r.pre_grad)
     mid_late = send_late(r.mid, mid_terms, mid_far, r.sums_b)
-    up_forward, up_end = grad_second(r.up_grad, mlp_in, r.pre_grad, swap)
+    mlp_terms = r.mlp_terms
+
+    def down_project(*blocks):
+        product(r.hidden, mlp_terms, blocks, (r.down_weight, (units, size), lambda j: (0, j)), size, width // size)
+
+    down_project(6, 7, 2, 3)
     down_forward(0)
     arrive(*mid_early, *mid_late)
     gain_sum = r.gain_sum
@@ -659,42 +664,37 @@
     )
     near = spread(middle_all)
 
-    mlp_terms = r.mlp_terms
-
-    def down_project(*blocks):
-        product(r.hidden, mlp_terms, blocks, (r.down_weight, (units, size), lambda j: (0, j)), size, width // size)
-
-    context_back(0, 1)
-    down_project(6, 7, 2, 3)
+    up_forward, up_end = grad_second(r.up_grad, mlp_in, r.pre_grad, swap)
     arrive(near[2], near[5])
     far = relay(middle_all)
+    mlp_far = send_far(r.attn, mlp_terms)
+    down_forward(1)
+    context_back(0, 1)
     down_project(4, 5, 0, 1)
-    mlp_far = send_far(r.attn, mlp_terms)
     arrive(near[3], near[4])
     context_back(2, 3, 4, 5)
-    down_forward(1)
     attend_back(0)
-    up_forward(0)
     arrive(far[6], far[7])
     context_back(6, 7)
-    swap = grad_first(r.out_grad, middle_all, r.context)
+    up_forward(0)
     attend_back(1)
     wire.sent(*attn_far, *attn_early)
     project_back(6, 7)
     back_far = send_far(r.mid, out_terms)
-    out_forward, out_end = grad_second(r.out_grad, middle_all, r.context, swap)
     swap = grad_first(r.qkv_w_grad, attn_in, r.qkv_grad)
     project_back(2, 3, 4, 5)
     back_early = send_early(r.mid, out_terms)
-    up_forward(1)
     qkv_forward, qkv_end = grad_second(r.qkv_w_grad, attn_in, r.qkv_grad, swap)
     wire.sent(*mid_late)
     back_late = send_late(r.mid, out_terms, back_far, r.sums_b)
+    up_forward(1)
     mlp_early = send_early(r.attn, mlp_terms)
+    swap = grad_first(r.out_grad, middle_all, r.context)
     wire.sent(*attn_late)
     mlp_late = send_late(r.attn, mlp_terms, mlp_far, r.sums_a)
+    out_forward, out_end = grad_second(r.out_grad, middle_all, r.context, swap)
     project_back(0, 1)
-    out_forward(0)
+    qkv_forward(0)
     down_end(r.down_total)
     arrive(*back_early, *back_late)
 
@@ -708,13 +708,12 @@
         [r.tokens, r.middle, r.attn_gain, out_terms, r.mid.early, r.mid.late],
         [r.tokens_grad],
     )
-    qkv_forward(0)
-    out_forward(1)
-    up_end(r.up_total)
+    qkv_forward(1)
     r.gain_near_sum[...] = over_all(r.gain_near, gain_sum, m, MP, 4)
     r.gains[...] = over_all(r.gain_far, r.gain_near_sum, d, DP, 8)
-    qkv_forward(1)
-    out_end(r.out_total)
+    up_end(r.up_total)
+    out_forward(0)
+    out_forward(1)
     arrive(*mlp_early, *mlp_late)
     row_wise(
         lambda mid, *t: (mid + total(t),),
@@ -722,6 +721,7 @@
         [r.layer_output],
     )
     qkv_end()
+    out_end(r.out_total)
     wire.finish()
 
 

time: 546 us -> 528 us (0.967)
  the two profiles are of different devices: /device:TPU:0 before, /device:TPU:8 now
where the time goes in v5:
time: 528 us; the launch traced here: 517 us
  Pallas kernels  504 us (95%)
  local copies, waits for them, and re-layouts  12.4 us (2%)
    pallas_call x1, Pallas kernels, layer(): pl.pallas_call(kernel, in_specs=[any_] * len(parts[0][0]), out_specs=jax....  501 us

profile of v5, /device:TPU:8, one launch (start us, length us, event | category | flops | bytes accessed | tf_op | source)
XLA Modules:
  0.0 517.5 jit_solution(10735181865103200610)
XLA Ops:
  0.6 1.9 copy.21.refs_7_
  2.5 1.3 reshape.38.refs_8_
  3.8 501.3 %layer.1 = (bf16[384,2048]{1,0:T(8,128)(2,1)}, bf16[384,2048]{1,0:T(8,128)(2,1)}, bf16[384,2048]{1,0:T(8,128)(2,1)}, bf16[1536,2048]{1,0:T(8,128)(2,1)}, bf16[15...) custom-call(f32[1,2048]{1,0:T(1,128)} %bitcast.7, ...), custom_call_target="tpu_custom_call" | custom-call | tf_op jit(solution)/shard_map/layer/pallas_call | solution.py:809
  505.1 0.0 copy-start.5
  505.1 0.0 copy-start.3
  505.1 2.7 share_total.1
  507.8 0.0 copy-start
  507.8 0.0 copy-done.5
  507.8 0.6 fusion
  508.4 0.0 copy-done.3
  508.4 1.1 copy.27
  509.6 0.7 copy-done
  510.3 0.0 copy-start.4
  510.3 0.0 copy-start.2
  510.3 1.7 copy.28
  511.9 0.0 copy-done.4
  511.9 0.8 copy.29
  512.7 0.6 copy-done.2
  513.3 0.0 copy-start.1
  513.3 1.3 copy.30
  514.7 1.0 copy-done.1
  515.7 1.3 copy.31
Async XLA Ops:
  505.1 2.7 copy-start.5
  505.1 3.3 copy-start.3
  507.8 2.5 copy-start
  510.3 1.7 copy-start.4
  510.3 3.1 copy-start.2
  513.3 2.3 copy-start.1

commit v6 on v5

--- a/solution.py
+++ b/solution.py
@@ -91,6 +91,21 @@
     return same & (j <= i)
 
 
+class Sent:
+    def __init__(self, wire, slot, source, target, to):
+        self.wire, self.slot, self.ends, self.to = wire, slot, (source, target), to
+
+    def make(self):
+        source, target = (e() if callable(e) else e for e in self.ends)
+        return self.wire.copy(self.slot, source, target, self.to)
+
+    def wait_recv(self):
+        self.make().wait_recv()
+
+    def wait_send(self):
+        self.make().wait_send()
+
+
 class Wire:
     def __init__(self, send, recv):
         self.send, self.recv, self.count, self.ends = send, recv, 0, []
@@ -110,8 +125,8 @@
         )
 
     def go(self, source, target, to):
-        copy = self.copy(self.slot(), source, target, to)
-        copy.start()
+        copy = Sent(self, self.slot(), source, target, to)
+        copy.make().start()
         self.ends.append(copy)
         return copy
 
@@ -155,7 +170,7 @@
     pl.semaphore_wait(barrier, len(others))
 
     def at(ref, block):
-        return ref.at[pl.ds(block * half, half)]
+        return lambda: ref.at[pl.ds(block * half, half)]
 
     qkv_w = r.qkv_w
     loads = [
@@ -482,53 +497,6 @@
         grad_product(left, right, 1 - core, into.mine)
         return wire.go(into.mine, into.got, to_core)
 
-    def line(mine, got, sums, step, place):
-        pick = lambda at: jnp.clip(at if step > 0 else 3 - at, 0, 3)
-        slots = [wire.slot() for _ in range(3)]
-        to = {DP: jnp.clip(d + 2 * step, 0, 7)}
-
-        def copy(t, source):
-            return wire.copy(slots[t], source, got.at[t], to)
-
-        @pl.when(place == 0)
-        def _():
-            for t in range(3):
-                copy(t, mine.at[pick(3 - t)]).start()
-
-        def forward(t):
-            @pl.when((place >= 1) & (place <= t + 1))
-            def _():
-                copy(t, mine.at[0]).wait_recv()
-                n = mine.shape[2]
-                size = mine.shape[1] // 2
-
-                def body(a, b, out):
-                    out[...] = (a[0].astype(f32) + b[...].astype(f32)).astype(bf16)
-
-                stage(
-                    body,
-                    (2,),
-                    [
-                        (mine, (1, size, n), lambda i: (pick(place + 2 - t), i, 0)),
-                        (got.at[t], (size, n), lambda i: (i, 0)),
-                    ],
-                    [(sums.at[t], (size, n), lambda i: (i, 0))],
-                )
-                copy(t + 1, sums.at[t]).start()
-
-        def end():
-            @pl.when(place >= 1)
-            def _():
-                copy(2, mine.at[0]).wait_recv()
-
-            for t in range(3):
-
-                @pl.when((place <= t) & (place < 3))
-                def _():
-                    copy(t, mine.at[0]).wait_send()
-
-        return forward, end
-
     def grad_second(into, left, right, swap):
         swap.wait_recv()
         wire.sent(swap)
@@ -536,16 +504,69 @@
         return start_line(into)
 
     def start_line(into):
-        up = line(into.mine, into.right, into.right_sums, 1, z)
-        down = line(into.mine, into.left, into.left_sums, -1, 3 - z)
+        mine = into.mine
+        n = mine.shape[2]
+        part = share // 2
+        ways = []
+        for step, got, sums in ((1, into.right, into.right_sums), (-1, into.left, into.left_sums)):
+            slots = [wire.slot() for _ in range(3)]
+            to = {DP: jnp.clip(d + 2 * step, 0, 7)}
+            place = z if step > 0 else 3 - z
+            ways.append((step, place, got, sums, slots, to))
+
+        def of(step, place):
+            return jnp.clip(place if step > 0 else 3 - place, 0, 3)
+
+        def copy(way, t, source):
+            _, _, got, _, slots, to = way
+            return wire.copy(slots[t], source, got.at[t], to)
+
+        for way in ways:
+
+            @pl.when(way[1] == 0)
+            def _():
+                for t in range(3):
+                    copy(way, t, mine.at[of(way[0], 3 - t)]).start()
+
+        def add(t, ways):
+            for way in ways:
+                copy(way, t, mine.at[0]).wait_recv()
+
+            def body(*refs):
+                for w in range(len(ways)):
+                    a, b = refs[2 * w : 2 * w + 2]
+                    refs[2 * len(ways) + w][...] = (a[0].astype(f32) + b[...].astype(f32)).astype(bf16)
+
+            ins, outs = [], []
+            for step, place, got, sums, _, _ in ways:
+                ins.append((mine, (1, part, n), lambda i, s=step, p=place: (of(s, p + 2 - t), i, 0)))
+                ins.append((got.at[t], (part, n), lambda i: (i, 0)))
+                outs.append((sums.at[t], (part, n), lambda i: (i, 0)))
+            stage(body, (2,), ins, outs)
+            for way in ways:
+                copy(way, t + 1, way[3].at[t]).start()
 
         def forward(t):
-            up[0](t)
-            down[0](t)
+            if t == 1:
+                pl.when((z == 1) | (z == 2))(lambda: add(1, ways))
+                return
+            for way in ways:
+                pl.when(way[1] == 1)(lambda: add(0, [way]))
 
         def end(turned=None):
-            up[1]()
-            down[1]()
+            for way in ways:
+                place = way[1]
+
+                @pl.when(place >= 1)
+                def _():
+                    copy(way, 2, mine.at[0]).wait_recv()
+
+                for t in range(3):
+
+                    @pl.when((place <= t) & (place < 3))
+                    def _():
+                        copy(way, t, mine.at[0]).wait_send()
+
             if turned is not None:
                 share_total(into, turned)
 
@@ -590,10 +611,16 @@
     arrive(near[3], near[4])
     cot_near = {2: wire.go(at(cot_all, 0), at(cot_all, 2), to_x), 5: wire.go(at(cot_all, 1), at(cot_all, 5), to_y)}
     project(2, 3, 4, 5)
-    attend(0)
-    arrive(far[6], far[7])
-    project(6, 7)
-    attend(1)
+
+    @pl.loop(0, 2)
+    def _(s):
+        @pl.when(s == 1)
+        def _():
+            arrive(far[6], far[7])
+            project(6, 7)
+
+        attend(s)
+
     out_terms = r.out_terms
     out_project(6, 7)
     attn_far = send_far(r.attn, out_terms)
@@ -616,16 +643,26 @@
     )
     near = spread(mlp_in)
     arrive(cot_near[2], cot_near[5])
-    feed(0, 1)
-    arrive(near[2], near[5])
-    far = relay(mlp_in)
-    cot_far = relay(cot_all)
-    feed(2, 5)
     mid_terms = r.mid_terms
-    mid_early = send_early(r.mid, mid_terms)
-    down_some(0, 8, (0, 1, 2, 5))
-    arrive(near[3], near[4], cot_near[3], cot_near[4])
-    feed(3, 4)
+    far, cot_far, mid_early = {}, {}, []
+
+    @pl.loop(0, 3)
+    def _(g):
+        @pl.when(g == 1)
+        def _():
+            arrive(near[2], near[5])
+            far.update(relay(mlp_in))
+            cot_far.update(relay(cot_all))
+
+        @pl.when(g == 2)
+        def _():
+            mid_early.extend(send_early(r.mid, mid_terms))
+            down_some(0, 8, (0, 1, 2, 5))
+            arrive(near[3], near[4], cot_near[3], cot_near[4])
+
+        later = (g + 1) // 2
+        feed(g + later, 1 - g + 5 * later)
+
     arrive(far[6], far[7])
     feed_forward(6, 7)
     arrive(cot_far[6], cot_far[7])
@@ -671,30 +708,36 @@
     down_forward(1)
     context_back(0, 1)
     down_project(4, 5, 0, 1)
+    mlp_early = send_early(r.attn, mlp_terms)
     arrive(near[3], near[4])
     context_back(2, 3, 4, 5)
-    attend_back(0)
-    arrive(far[6], far[7])
-    context_back(6, 7)
-    up_forward(0)
-    attend_back(1)
+
+    @pl.loop(0, 2)
+    def _(s):
+        @pl.when(s == 1)
+        def _():
+            arrive(far[6], far[7])
+            context_back(6, 7)
+            up_forward(0)
+
+        attend_back(s)
+
     wire.sent(*attn_far, *attn_early)
+    swap = grad_first(r.qkv_w_grad, attn_in, r.qkv_grad)
     project_back(6, 7)
     back_far = send_far(r.mid, out_terms)
-    swap = grad_first(r.qkv_w_grad, attn_in, r.qkv_grad)
+    qkv_forward, qkv_end = grad_second(r.qkv_w_grad, attn_in, r.qkv_grad, swap)
     project_back(2, 3, 4, 5)
     back_early = send_early(r.mid, out_terms)
-    qkv_forward, qkv_end = grad_second(r.qkv_w_grad, attn_in, r.qkv_grad, swap)
     wire.sent(*mid_late)
     back_late = send_late(r.mid, out_terms, back_far, r.sums_b)
     up_forward(1)
-    mlp_early = send_early(r.attn, mlp_terms)
+    qkv_forward(0)
     swap = grad_first(r.out_grad, middle_all, r.context)
     wire.sent(*attn_late)
     mlp_late = send_late(r.attn, mlp_terms, mlp_far, r.sums_a)
     out_forward, out_end = grad_second(r.out_grad, middle_all, r.context, swap)
     project_back(0, 1)
-    qkv_forward(0)
     down_end(r.down_total)
     arrive(*back_early, *back_late)
 
@@ -709,10 +752,10 @@
         [r.tokens_grad],
     )
     qkv_forward(1)
+    out_forward(0)
     r.gain_near_sum[...] = over_all(r.gain_near, gain_sum, m, MP, 4)
     r.gains[...] = over_all(r.gain_far, r.gain_near_sum, d, DP, 8)
     up_end(r.up_total)
-    out_forward(0)
     out_forward(1)
     arrive(*mlp_early, *mlp_late)
     row_wise(

time: 528 us -> 513 us (0.972)
  the two profiles are of different devices: /device:TPU:8 before, /device:TPU:0 now
where the time goes in v6:
time: 513 us; the launch traced here: 511 us
  Pallas kernels  497 us (97%)
  local copies, waits for them, and re-layouts  12.4 us (2%)
    pallas_call x1, Pallas kernels, layer(): pl.pallas_call(kernel, in_specs=[any_] * len(parts[0][0]), out_specs=jax....  495 us

profile of v6, /device:TPU:0, one launch (start us, length us, event | category | flops | bytes accessed | tf_op | source)
XLA Modules:
  0.0 510.5 jit_solution(4649949626797604653)
XLA Ops:
  0.6 1.9 copy.21.refs_7_
  2.5 1.3 reshape.38.refs_8_
  3.8 494.8 %layer.1 = (bf16[384,2048]{1,0:T(8,128)(2,1)}, bf16[384,2048]{1,0:T(8,128)(2,1)}, bf16[384,2048]{1,0:T(8,128)(2,1)}, bf16[1536,2048]{1,0:T(8,128)(2,1)}, bf16[15...) custom-call(f32[1,2048]{1,0:T(1,128)} %bitcast.7, ...), custom_call_target="tpu_custom_call" | custom-call | tf_op jit(solution)/shard_map/layer/pallas_call | solution.py:852
  498.6 0.0 copy-start.5
  498.6 0.0 copy-start.3
  498.6 2.7 share_total.1
  501.3 0.0 copy-start
  501.3 0.0 copy-done.5
  501.3 0.6 fusion
  501.9 0.0 copy-done.3
  501.9 1.1 copy.27
  503.1 0.7 copy-done
  503.8 0.0 copy-start.4
  503.8 0.0 copy-start.2
  503.8 1.7 copy.28
  505.4 0.0 copy-done.4
  505.4 0.8 copy.29
  506.2 0.6 copy-done.2
  506.8 0.0 copy-start.1
  506.9 1.3 copy.30
  508.2 1.0 copy-done.1
  509.2 1.3 copy.31
Async XLA Ops:
  498.6 2.7 copy-start.5
  498.6 3.3 copy-start.3
  501.3 2.5 copy-start
  503.8 1.7 copy-start.4
  503.8 3.1 copy-start.2
  506.8 2.3 copy-start.1

commit v7 on v6

--- a/solution.py
+++ b/solution.py
@@ -310,43 +310,41 @@
     f0, f1, f2 = r.f0, r.f1, r.f2
 
     def head_ins(s):
-        ins = [
-            (r.seg_col, (1, length, 1), lambda h: (lax.rem(m // 2 + s, 2), 0, 0)),
-            (r.seg_row, (1, 1, length), lambda h: (lax.rem(m // 2 + s, 2), 0, 0)),
-        ]
+        ins = []
         for which in range(3):
             ins.append((r.qkv, (length, HEAD_DIM), lambda h, w=which: (s, w * heads + h)))
         return ins
 
-    def scores_of(seg_col, seg_row, q0, k0, k1):
-        s = dot(q[q0:k1, :], k[k0:k1, :], 1, 1)
-        keep = allowed_of(seg_col.at[0], seg_row.at[0], q0, k0, k1, CLIP_MOST)
-        s = jnp.where(keep, s, masked_score)
-        e = jnp.exp(s - jnp.max(s, axis=-1, keepdims=True))
+    def scores_of(s, q0, k0, k1):
+        which = lax.rem(m // 2 + s, 2)
+        scores = dot(q[q0:k1, :], k[k0:k1, :], 1, 1)
+        keep = allowed_of(r.seg_cols.at[which], r.seg_rows.at[which], q0, k0, k1, CLIP_MOST)
+        scores = jnp.where(keep, scores, masked_score)
+        e = jnp.exp(scores - jnp.max(scores, axis=-1, keepdims=True))
         return e * (1.0 / jnp.sum(e, axis=-1, keepdims=True))
 
     def attend(s):
-        def body(seg_col, seg_row, q_in, k_in, v_in, out):
+        def body(q_in, k_in, v_in, out):
             turn(q_in, q)
             turn(k_in, k)
             turn(v_in, v)
             for q0 in range(0, length, CLIP_MOST):
                 k0, k1 = max(0, q0 - CLIP_MOST), q0 + CLIP_MOST
-                p = scores_of(seg_col, seg_row, q0, k0, k1).astype(bf16)
+                p = scores_of(s, q0, k0, k1).astype(bf16)
                 f0[q0:k1, :] = dot(p, v[k0:k1, :], 1, 0)
             turn_back(f0, out)
 
         stage(body, (heads,), head_ins(s), [(r.context, (length, HEAD_DIM), lambda h: (s, h))])
 
     def attend_back(s):
-        def body(seg_col, seg_row, q_in, k_in, v_in, c_in, dq_out, dk_out, dv_out):
+        def body(q_in, k_in, v_in, c_in, dq_out, dk_out, dv_out):
             turn(q_in, q)
             turn(k_in, k)
             turn(v_in, v)
             turn(c_in, c)
             for q0 in range(0, length, CLIP_MOST):
                 k0, k1 = max(0, q0 - CLIP_MOST), q0 + CLIP_MOST
-                p = scores_of(seg_col, seg_row, q0, k0, k1)
+                p = scores_of(s, q0, k0, k1)
                 qb, cb, kb, vb = q[q0:k1, :], c[q0:k1, :], k[k0:k1, :], v[k0:k1, :]
                 dp = dot(cb, vb, 1, 1)
                 inner = jnp.sum(p * dp, axis=-1, keepdims=True)
@@ -603,6 +601,16 @@
     )
     near = spread(attn_in)
     row_wise(lambda x: (x,), [r.out_cotangent], [cot_all])
+
+    def segments(ids):
+        same = lax.broadcasted_iota(jnp.int32, (128, 128), 0) == lax.broadcasted_iota(jnp.int32, (128, 128), 1)
+        for i in range(2):
+            for at_ in range(0, length, 128):
+                row = ids[i : i + 1, at_ : at_ + 128].astype(f32)
+                r.seg_rows[i, :, at_ : at_ + 128] = row
+                r.seg_cols[i, at_ : at_ + 128, :] = jnp.sum(jnp.where(same, row, 0.0), axis=1, keepdims=True)
+
+    stage(segments, (1,), [(r.segment_ids, (2, length), lambda i: (0, 0))], [])
     for load in loads:
         load.wait()
     project(0, 1)
@@ -706,11 +714,10 @@
     far = relay(middle_all)
     mlp_far = send_far(r.attn, mlp_terms)
     down_forward(1)
-    context_back(0, 1)
     down_project(4, 5, 0, 1)
     mlp_early = send_early(r.attn, mlp_terms)
     arrive(near[3], near[4])
-    context_back(2, 3, 4, 5)
+    context_back(0, 1, 2, 3, 4, 5)
 
     @pl.loop(0, 2)
     def _(s):
@@ -834,6 +841,8 @@
         f0=head_sum,
         f1=head_sum,
         f2=head_sum,
+        seg_rows=pltpu.VMEM((2, 1, length), f32),
+        seg_cols=pltpu.VMEM((2, length, 1), f32),
         send=pltpu.SemaphoreType.DMA((96,)),
         recv=pltpu.SemaphoreType.DMA((96,)),
         load=pltpu.SemaphoreType.DMA((3,)),
@@ -1141,8 +1150,7 @@
     got = layer(
         dict(
             tokens=tokens,
-            seg_col=segment_ids.reshape(2, length, 1),
-            seg_row=segment_ids.reshape(2, 1, length),
+            segment_ids=segment_ids,
             query_weight=query_weight,
             key_weight=key_weight,
             value_weight=value_weight,

time: 513 us -> 510 us (level)
  no operation moved by 1% of the time
where the time goes in v7:
time: 510 us; the launch traced here: 508 us
  Pallas kernels  498 us (98%)
  local copies, waits for them, and re-layouts  9.22 us (2%)
    pallas_call x1, Pallas kernels, layer(): pl.pallas_call(kernel, in_specs=[any_] * len(parts[0][0]), out_specs=jax....  495 us

profile of v7, /device:TPU:0, one launch (start us, length us, event | category | flops | bytes accessed | tf_op | source)
XLA Modules:
  0.0 507.6 jit_solution(11395672295859393834)
XLA Ops:
  0.6 495.0 %layer.1 = (bf16[384,2048]{1,0:T(8,128)(2,1)}, bf16[384,2048]{1,0:T(8,128)(2,1)}, bf16[384,2048]{1,0:T(8,128)(2,1)}, bf16[1536,2048]{1,0:T(8,128)(2,1)}, bf16[15...) custom-call(f32[1,2048]{1,0:T(1,128)} %bitcast.5, ...), custom_call_target="tpu_custom_call" | custom-call | tf_op jit(solution)/shard_map/layer/pallas_call | solution.py:861
  495.6 0.0 copy-start.5
  495.7 0.0 copy-start.3
  495.7 2.7 share_total.1
  498.3 0.0 copy-start
  498.3 0.0 copy-done.5
  498.3 0.6 fusion
  498.9 0.0 copy-done.3
  499.0 1.1 copy.26
  500.1 0.7 copy-done
  500.8 0.0 copy-start.4
  500.8 0.0 copy-start.2
  500.8 1.7 copy.27
  502.5 0.0 copy-done.4
  502.5 0.8 copy.28
  503.3 0.6 copy-done.2
  503.9 0.0 copy-start.1
  503.9 1.3 copy.29
  505.2 1.0 copy-done.1
  506.2 1.3 copy.30
Async XLA Ops:
  495.6 2.7 copy-start.5
  495.7 3.3 copy-start.3
  498.3 2.5 copy-start
  500.8 1.7 copy-start.4
  500.8 3.1 copy-start.2
  503.9 2.3 copy-start.1

commit v8 on v7

--- a/solution.py
+++ b/solution.py
@@ -745,7 +745,7 @@
     mlp_late = send_late(r.attn, mlp_terms, mlp_far, r.sums_a)
     out_forward, out_end = grad_second(r.out_grad, middle_all, r.context, swap)
     project_back(0, 1)
-    down_end(r.down_total)
+    qkv_forward(1)
     arrive(*back_early, *back_late)
 
     def first_back(x, mid, g, a, b, c_):
@@ -758,12 +758,12 @@
         [r.tokens, r.middle, r.attn_gain, out_terms, r.mid.early, r.mid.late],
         [r.tokens_grad],
     )
-    qkv_forward(1)
     out_forward(0)
     r.gain_near_sum[...] = over_all(r.gain_near, gain_sum, m, MP, 4)
     r.gains[...] = over_all(r.gain_far, r.gain_near_sum, d, DP, 8)
     up_end(r.up_total)
     out_forward(1)
+    down_end(r.down_total)
     arrive(*mlp_early, *mlp_late)
     row_wise(
         lambda mid, *t: (mid + total(t),),

time: 510 us -> 510 us (level)
  no operation moved by 1% of the time
where the time goes in v8:
time: 510 us; the launch traced here: 508 us
  Pallas kernels  498 us (98%)
  local copies, waits for them, and re-layouts  9.22 us (2%)
    pallas_call x1, Pallas kernels, layer(): pl.pallas_call(kernel, in_specs=[any_] * len(parts[0][0]), out_specs=jax....  495 us

profile of v8, /device:TPU:0, one launch (start us, length us, event | category | flops | bytes accessed | tf_op | source)
XLA Modules:
  0.0 507.6 jit_solution(1650601953530061939)
XLA Ops:
  0.6 495.0 %layer.1 = (bf16[384,2048]{1,0:T(8,128)(2,1)}, bf16[384,2048]{1,0:T(8,128)(2,1)}, bf16[384,2048]{1,0:T(8,128)(2,1)}, bf16[1536,2048]{1,0:T(8,128)(2,1)}, bf16[15...) custom-call(f32[1,2048]{1,0:T(1,128)} %bitcast.5, ...), custom_call_target="tpu_custom_call" | custom-call | tf_op jit(solution)/shard_map/layer/pallas_call | solution.py:861
  495.6 0.0 copy-start.5
  495.7 0.0 copy-start.3
  495.7 2.7 share_total.1
  498.3 0.0 copy-start
  498.3 0.0 copy-done.5
  498.3 0.6 fusion
  499.0 0.0 copy-done.3
  499.0 1.1 copy.26
  500.1 0.7 copy-done
  500.8 0.0 copy-start.4
  500.8 0.0 copy-start.2
  500.8 1.7 copy.27
  502.5 0.0 copy-done.4
  502.5 0.8 copy.28
  503.3 0.6 copy-done.2
  503.9 0.0 copy-start.1
  503.9 1.3 copy.29
  505.2 1.0 copy-done.1
  506.2 1.3 copy.30
Async XLA Ops:
  495.6 2.7 copy-start.5
  495.7 3.3 copy-start.3
  498.3 2.5 copy-start
  500.8 1.7 copy-start.4
  500.8 3.1 copy-start.2
  503.9 2.3 copy-start.1
